TPU v7x, 32 devices: a whole 2x2x4 slice. The times are simulated.
32 devices in a mesh: dp: 16 (over z, y, core), tensor: 2 (over x).
Axes of the slice: x: 2, y: 2, z: 4, core: 2. Of those that a mesh axis runs over, the one named last changes fastest.
Arguments:
- frames_in: bfloat16 [2, 16, 1024, 1024], P(None, 'dp', 'tensor'), may hold values from -6 to 6
- phone_len: int32 [2, 16], P(None, 'dp'), may hold values from 10 to 204
- frame_len: int32 [2, 16], P(None, 'dp'), may hold values from 512 to 819
- section: int32 [2, 16], P(None, 'dp'), may hold values from 0 to 6
- norm_gain: float32 [2, 1024], replicated, may hold values from 0.5 to 1.5
- norm_bias: float32 [2, 1024], replicated, may hold values from -4 to 4
- ada_scale: float32 [2, 7, 1024], replicated, may hold values from 0.5 to 1.5
- ada_shift: float32 [2, 7, 1024], replicated, may hold values from -4 to 4
- w_qkv: bfloat16 [2, 1024, 3, 1024], P(None, None, None, 'tensor'), may hold values from -0.1875 to 0.1875
- w_out: bfloat16 [2, 1024, 1024], P(None, 'tensor'), may hold values from -4 to 4
- w_up: bfloat16 [2, 1024, 4096], P(None, None, 'tensor'), may hold values from -0.1875 to 0.1875
- w_down: bfloat16 [2, 4096, 1024], P(None, 'tensor'), may hold values from -0.09375 to 0.09375
- out_grad: bfloat16 [2, 16, 1024, 1024], P(None, 'dp', 'tensor'), may hold values from -6 to 6
Outputs:
- frames_out: float32 [2, 16, 1024, 1024], P(None, 'dp', 'tensor')
- frames_grad: float32 [2, 16, 1024, 1024], P(None, 'dp', 'tensor')
- grad_qkv: float32 [2, 1024, 3, 1024], P(None, None, None, 'tensor')
- grad_out: float32 [2, 1024, 1024], P(None, 'tensor')
- grad_up: float32 [2, 1024, 4096], P(None, None, 'tensor')
- grad_down: float32 [2, 4096, 1024], P(None, 'tensor')
- grad_norm_gain: float32 [2, 1024], replicated
- grad_norm_bias: float32 [2, 1024], replicated
- grad_ada_scale: float32 [2, 7, 1024], replicated
- grad_ada_shift: float32 [2, 7, 1024], replicated
All inputs are finite; a program needn't handle non-finite values.
Results may differ from a plain program's by a relative error of at most 0.028.
Values may be sent and summed in bfloat16 or wider, within the bound.
No kernel may reach another device: no remote copies, remote signals or barrier semaphores. Data moves between devices by JAX's collectives and lax.ppermute only.
A program may use at most 384 MiB of HBM per device.

v0:
```python
from functools import partial

import jax
import jax.numpy as jnp
from jax import lax
from jax.sharding import PartitionSpec as P

HEAD_DIM = 64


norm_eps = 1e-05
masked_score = -1000000000.0
contract_rows = (((0,), (0,)), ((), ()))
contract_cols = (((1,), (1,)), ((), ()))


def plain_norm(inputs):
    centered = inputs - jnp.mean(inputs, axis=-1, keepdims=True)
    variance = jnp.mean(centered * centered, axis=-1, keepdims=True)
    return centered * lax.rsqrt(variance + norm_eps)


def fixed_norm(inputs, gain_row, shift_row):
    return plain_norm(inputs) * gain_row + shift_row


def section_norm(inputs, scale_table, shift_table, picker):
    scale_row = jnp.dot(
        picker, scale_table, precision=lax.Precision.HIGHEST, preferred_element_type=jnp.float32
    )
    shift_row = jnp.dot(
        picker, shift_table, precision=lax.Precision.HIGHEST, preferred_element_type=jnp.float32
    )
    return plain_norm(inputs) * scale_row + shift_row


def gather_normed(normed_low):
    return lax.all_gather(normed_low, "tensor", axis=0, tiled=True)


def gather_again(normed_low):
    return lax.all_gather(normed_low, "tensor", axis=0, tiled=True)


def sum_branch(branch_part):
    return lax.psum_scatter(
        branch_part.astype(jnp.bfloat16), "tensor", scatter_dimension=0, tiled=True
    ).astype(jnp.float32)


def gather_grad(grad_low):
    return lax.all_gather(grad_low, "tensor", axis=0, tiled=True)


def sum_normed(grad_part):
    return lax.psum_scatter(
        grad_part.astype(jnp.bfloat16), "tensor", scatter_dimension=0, tiled=True
    ).astype(jnp.float32)


def key_allowed(query_pos, key_pos, prefix, valid_count, causal):
    allowed = key_pos[None, :] < valid_count
    if causal:
        allowed = allowed & ((key_pos[None, :] < prefix) | (key_pos[None, :] <= query_pos[:, None]))
    return allowed


def split_heads(projected):
    length = projected.shape[0]
    head_width = projected.shape[1] // 3
    head_count = head_width // HEAD_DIM
    query_rows = projected[:, :head_width].reshape(length, head_count, HEAD_DIM)
    key_rows = projected[:, head_width : 2 * head_width].reshape(length, head_count, HEAD_DIM)
    value_rows = projected[:, 2 * head_width :].reshape(length, head_count, HEAD_DIM)
    return (query_rows, key_rows, value_rows)


def block_scores(query_block, key_rows, block_start, prefix, valid_count, causal):
    block_rows = query_block.shape[0]
    length = key_rows.shape[0]
    scores = jnp.einsum(
        "qhd,khd->hqk", query_block, key_rows, preferred_element_type=jnp.float32
    ) * HEAD_DIM ** (-0.5)
    query_pos = block_start + lax.iota(jnp.int32, block_rows)
    key_pos = lax.iota(jnp.int32, length)
    allowed = key_allowed(query_pos, key_pos, prefix, valid_count, causal)
    return jnp.where(allowed[None], scores, masked_score)


def attend_forward(projected, prefix, valid_count, causal, block_rows):
    length = projected.shape[0]
    head_width = projected.shape[1] // 3
    query_rows, key_rows, value_rows = split_heads(projected)

    def one_block(block_start):
        query_block = lax.dynamic_slice_in_dim(query_rows, block_start, block_rows, 0)
        scores = block_scores(query_block, key_rows, block_start, prefix, valid_count, causal)
        highest = jnp.max(scores, axis=-1, keepdims=True)
        row_total = jnp.sum(jnp.exp(scores - highest), axis=-1, keepdims=True)
        log_total = highest + jnp.log(row_total)
        shares = jnp.exp(scores - log_total).astype(jnp.bfloat16)
        mixture = jnp.einsum("hqk,khd->qhd", shares, value_rows, preferred_element_type=jnp.float32)
        return (mixture.astype(jnp.bfloat16), log_total)

    starts = lax.iota(jnp.int32, length // block_rows) * block_rows
    mixture, log_totals = lax.map(one_block, starts)
    return (mixture.reshape(length, head_width), log_totals)


def attend_backward(projected, log_totals, grad_mixture, prefix, valid_count, causal, block_rows):
    length = projected.shape[0]
    head_width = projected.shape[1] // 3
    query_rows, key_rows, value_rows = split_heads(projected)
    grad_rows = grad_mixture.reshape(query_rows.shape)
    score_scale = HEAD_DIM ** (-0.5)

    def one_block(grad_state, block_item):
        block_start, log_total = block_item
        grad_key, grad_value = grad_state
        query_block = lax.dynamic_slice_in_dim(query_rows, block_start, block_rows, 0)
        grad_block = lax.dynamic_slice_in_dim(grad_rows, block_start, block_rows, 0)
        scores = block_scores(query_block, key_rows, block_start, prefix, valid_count, causal)
        shares = jnp.exp(scores - log_total)
        shares_low = shares.astype(jnp.bfloat16)
        grad_shares = jnp.einsum(
            "qhd,khd->hqk", grad_block, value_rows, preferred_element_type=jnp.float32
        )
        inner_sum = jnp.sum(shares * grad_shares, axis=-1, keepdims=True)
        grad_scores = (shares * (grad_shares - inner_sum)).astype(jnp.bfloat16)
        grad_query = (
            jnp.einsum("hqk,khd->qhd", grad_scores, key_rows, preferred_element_type=jnp.float32)
            * score_scale
        )
        grad_key = (
            grad_key
            + jnp.einsum(
                "hqk,qhd->khd", grad_scores, query_block, preferred_element_type=jnp.float32
            )
            * score_scale
        )
        grad_value = grad_value + jnp.einsum(
            "hqk,qhd->khd", shares_low, grad_block, preferred_element_type=jnp.float32
        )
        return ((grad_key, grad_value), grad_query)

    starts = lax.iota(jnp.int32, length // block_rows) * block_rows
    zero_rows = jnp.zeros(query_rows.shape, jnp.float32)
    grad_state, grad_query = lax.scan(one_block, (zero_rows, zero_rows), (starts, log_totals))
    grad_key, grad_value = grad_state
    joined = jnp.concatenate(
        [
            grad_query.reshape(length, head_width),
            grad_key.reshape(length, head_width),
            grad_value.reshape(length, head_width),
        ],
        axis=1,
    )
    return joined.astype(jnp.bfloat16)


def per_device(
    frames_in,
    phone_len,
    frame_len,
    section,
    norm_gain,
    norm_bias,
    ada_scale,
    ada_shift,
    w_qkv,
    w_out,
    w_up,
    w_down,
    out_grad,
):
    micro_count, local_seqs, local_rows, model_width = frames_in.shape
    seq_length = local_rows * lax.axis_size("tensor")
    block_rows = min(512, seq_length)
    section_count = ada_scale.shape[1]
    qkv_mats = [w_qkv[layer_index].reshape(model_width, -1) for layer_index in range(2)]
    acc_qkv = [jnp.zeros(qkv_mats[layer_index].shape, jnp.float32) for layer_index in range(2)]
    acc_out = [jnp.zeros(w_out.shape[1:], jnp.float32) for layer_index in range(2)]
    acc_up = [jnp.zeros(w_up.shape[1:], jnp.float32) for layer_index in range(2)]
    acc_down = [jnp.zeros(w_down.shape[1:], jnp.float32) for layer_index in range(2)]
    acc_gain = [jnp.zeros((model_width,), jnp.float32) for part_index in range(2)]
    acc_bias = [jnp.zeros((model_width,), jnp.float32) for part_index in range(2)]
    acc_scale = [jnp.zeros((section_count, model_width), jnp.float32) for part_index in range(2)]
    acc_shift = [jnp.zeros((section_count, model_width), jnp.float32) for part_index in range(2)]
    frames_list = []
    grads_list = []
    for micro_index in range(micro_count):
        prefix = phone_len[micro_index, 0]
        valid_count = prefix + frame_len[micro_index, 0]
        picker = (lax.iota(jnp.int32, section_count) == section[micro_index, 0]).astype(
            jnp.float32
        )[None, :]
        residual = frames_in[micro_index, 0].astype(jnp.float32)
        stored = []
        for layer_index in range(2):
            for part_index in range(2):
                if layer_index == 0:
                    normed, norm_back = jax.vjp(
                        fixed_norm, residual, norm_gain[part_index], norm_bias[part_index]
                    )
                else:
                    normed, norm_back = jax.vjp(
                        partial(section_norm, picker=picker),
                        residual,
                        ada_scale[part_index],
                        ada_shift[part_index],
                    )
                normed_low = normed.astype(jnp.bfloat16)
                gathered = gather_normed(normed_low)
                if part_index == 0:
                    projected = jnp.dot(
                        gathered, qkv_mats[layer_index], preferred_element_type=jnp.float32
                    ).astype(jnp.bfloat16)
                    mixture, log_totals = attend_forward(
                        projected, prefix, valid_count, layer_index == 0, block_rows
                    )
                    branch = sum_branch(
                        jnp.dot(mixture, w_out[layer_index], preferred_element_type=jnp.float32)
                    )
                    saved_state = (projected, log_totals, mixture)
                else:
                    hidden = jnp.dot(
                        gathered, w_up[layer_index], preferred_element_type=jnp.float32
                    )
                    active = jax.nn.gelu(hidden, approximate=True).astype(jnp.bfloat16)
                    branch = sum_branch(
                        jnp.dot(active, w_down[layer_index], preferred_element_type=jnp.float32)
                    )
                    saved_state = (hidden, active)
                kept_rows = normed_low
                stored.append((norm_back, kept_rows, saved_state))
                residual = residual + branch
        out_group = [residual]
        grad_rows = out_grad[micro_index, 0].astype(jnp.float32)
        for layer_index in (1, 0):
            for part_index in (1, 0):
                norm_back, kept_rows, saved_state = stored[2 * layer_index + part_index]
                gathered = gather_again(kept_rows)
                grad_whole = gather_grad(grad_rows.astype(jnp.bfloat16))
                if part_index == 1:
                    hidden, active = saved_state
                    acc_down[layer_index] = acc_down[layer_index] + lax.dot_general(
                        active, grad_whole, contract_rows, preferred_element_type=jnp.float32
                    )
                    grad_active = lax.dot_general(
                        grad_whole,
                        w_down[layer_index],
                        contract_cols,
                        preferred_element_type=jnp.float32,
                    )
                    gelu_value, gelu_back = jax.vjp(partial(jax.nn.gelu, approximate=True), hidden)
                    grad_hidden = gelu_back(grad_active)[0].astype(jnp.bfloat16)
                    acc_up[layer_index] = acc_up[layer_index] + lax.dot_general(
                        gathered, grad_hidden, contract_rows, preferred_element_type=jnp.float32
                    )
                    grad_normed = sum_normed(
                        lax.dot_general(
                            grad_hidden,
                            w_up[layer_index],
                            contract_cols,
                            preferred_element_type=jnp.float32,
                        )
                    )
                else:
                    projected, log_totals, mixture = saved_state
                    acc_out[layer_index] = acc_out[layer_index] + lax.dot_general(
                        mixture, grad_whole, contract_rows, preferred_element_type=jnp.float32
                    )
                    grad_mixture = lax.dot_general(
                        grad_whole,
                        w_out[layer_index],
                        contract_cols,
                        preferred_element_type=jnp.float32,
                    ).astype(jnp.bfloat16)
                    grad_projected = attend_backward(
                        projected,
                        log_totals,
                        grad_mixture,
                        prefix,
                        valid_count,
                        layer_index == 0,
                        block_rows,
                    )
                    acc_qkv[layer_index] = acc_qkv[layer_index] + lax.dot_general(
                        gathered, grad_projected, contract_rows, preferred_element_type=jnp.float32
                    )
                    grad_normed = sum_normed(
                        lax.dot_general(
                            grad_projected,
                            qkv_mats[layer_index],
                            contract_cols,
                            preferred_element_type=jnp.float32,
                        )
                    )
                grad_input, grad_first, grad_second = norm_back(grad_normed)
                grad_rows = grad_rows + grad_input
                if layer_index == 0:
                    acc_gain[part_index] = acc_gain[part_index] + grad_first
                    acc_bias[part_index] = acc_bias[part_index] + grad_second
                else:
                    acc_scale[part_index] = acc_scale[part_index] + grad_first
                    acc_shift[part_index] = acc_shift[part_index] + grad_second
        grad_group = [grad_rows]
        frames_list.append(jnp.stack(out_group))
        grads_list.append(jnp.stack(grad_group))
    total_qkv, total_out, total_up, total_down = (
        lax.psum(jnp.stack(acc_qkv).astype(jnp.bfloat16), "dp").astype(jnp.float32),
        lax.psum(jnp.stack(acc_out).astype(jnp.bfloat16), "dp").astype(jnp.float32),
        lax.psum(jnp.stack(acc_up).astype(jnp.bfloat16), "dp").astype(jnp.float32),
        lax.psum(jnp.stack(acc_down).astype(jnp.bfloat16), "dp").astype(jnp.float32),
    )
    norm_totals = lax.psum(
        (jnp.stack(acc_gain), jnp.stack(acc_bias), jnp.stack(acc_scale), jnp.stack(acc_shift)),
        ("dp", "tensor"),
    )
    return (
        jnp.stack(frames_list),
        jnp.stack(grads_list),
        total_qkv.reshape(2, model_width, 3, -1),
        total_out,
        total_up,
        total_down,
        norm_totals[0],
        norm_totals[1],
        norm_totals[2],
        norm_totals[3],
    )


def solution(mesh):
    return jax.shard_map(
        per_device,
        mesh=mesh,
        in_specs=(
            P(None, "dp", "tensor", None),
            P(None, "dp"),
            P(None, "dp"),
            P(None, "dp"),
            P(),
            P(),
            P(),
            P(),
            P(None, None, None, "tensor"),
            P(None, "tensor", None),
            P(None, None, "tensor"),
            P(None, "tensor", None),
            P(None, "dp", "tensor", None),
        ),
        out_specs=(
            P(None, "dp", "tensor", None),
            P(None, "dp", "tensor", None),
            P(None, None, None, "tensor"),
            P(None, "tensor", None),
            P(None, None, "tensor"),
            P(None, "tensor", None),
            P(),
            P(),
            P(),
            P(),
        ),
        check_vma=False,
    )
```

profile of v0, /device:TPU:0, one launch (start us, length us, event | category | flops | bytes accessed | tf_op | source)
XLA Modules:
  0.0 2267.6 jit_solution(17285633225396595511)
XLA Ops:
  63.6 38.0 %while.108 = (s32[]{:T(128)}, bf16[2,512,8,64]{1,3,2,0:T(8,128)(2,1)S(1)}, f32[2,8,512,1]{2,1,3,0:T(8,128)S(1)}, s32[]{:T(128)}, s32[]{:T(128)}, /*index=5*/s32[...) while((s32[]{:T(128)}, ...), condition=%wide.region_5.6_spmd, body=%wide.region_2.5_spmd.sunk | while | flops 1121712640 | bytes 55713984 | solution.py:106
  106.9 31.7 %reduce-scatter.17.cloned.1.call-done = bf16[512,1024]{1,0:T(8,128)(2,1)} async-done(((bf16[1024,1024]{1,0:T(8,128)(2,1)}), bf16[512,1024]{1,0:T(8,128)(2,1)}) %reduce-scatter.17.cloned.1.call-update) | async-done | bytes 1048592 | tf_op jit(solution)/shard_map/reduce_scatter | solution.py:46
  143.3 31.9 %all-gather.27.cloned.1.call-done = bf16[1024,1024]{1,0:T(8,128)(2,1)} async-done(((bf16[512,1024]{1,0:T(8,128)(2,1)}), bf16[1024,1024]{1,0:T(8,128)(2,1)}) %all-gather.27.cloned.1.call-update) | async-done | bytes 2097168 | tf_op jit(solution)/shard_map/all_gather | solution.py:38
  188.8 38.0 %while.110 = (s32[]{:T(128)}, bf16[2,512,8,64]{1,3,2,0:T(8,128)(2,1)S(1)}, f32[2,8,512,1]{2,1,3,0:T(8,128)S(1)}, s32[]{:T(128)}, s32[]{:T(128)}, /*index=5*/s32[...) while((s32[]{:T(128)}, ...), condition=%wide.region_25.26_spmd, body=%wide.region_22.25_spmd.sunk | while | flops 1121712640 | bytes 55713984 | solution.py:106
  232.3 31.5 %reduce-scatter.25.cloned.1.call-done = bf16[512,1024]{1,0:T(8,128)(2,1)} async-done(((bf16[1024,1024]{1,0:T(8,128)(2,1)}), bf16[512,1024]{1,0:T(8,128)(2,1)}) %reduce-scatter.25.cloned.1.call-update) | async-done | bytes 1048592 | tf_op jit(solution)/shard_map/reduce_scatter | solution.py:46
  269.9 32.6 %all-gather.29.cloned.1.call-done = bf16[1024,1024]{1,0:T(8,128)(2,1)} async-done(((bf16[512,1024]{1,0:T(8,128)(2,1)}), bf16[1024,1024]{1,0:T(8,128)(2,1)}) %all-gather.29.cloned.1.call-update) | async-done | bytes 2097168 | tf_op jit(solution)/shard_map/all_gather | solution.py:38
  372.3 34.8 %reduce-scatter.19.cloned.1.call-done = bf16[512,1024]{1,0:T(8,128)(2,1)} async-done(((bf16[1024,1024]{1,0:T(8,128)(2,1)}), bf16[512,1024]{1,0:T(8,128)(2,1)}) %reduce-scatter.19.cloned.1.call-update) | async-done | bytes 1048592 | tf_op jit(solution)/shard_map/reduce_scatter | solution.py:46
  422.0 25.0 %all-gather.31.cloned.1.call-done = bf16[1024,1024]{1,0:T(8,128)(2,1)} async-done(((bf16[512,1024]{1,0:T(8,128)(2,1)}), bf16[1024,1024]{1,0:T(8,128)(2,1)}) %all-gather.31.cloned.1.call-update) | async-done | bytes 2097168 | tf_op jit(solution)/shard_map/all_gather | solution.py:38
  457.0 25.2 %all-gather.23.cloned.1.call-done = bf16[1024,1024]{1,0:T(8,128)(2,1)} async-done(((bf16[512,1024]{1,0:T(8,128)(2,1)}), bf16[1024,1024]{1,0:T(8,128)(2,1)}) %all-gather.23.cloned.1.call-update) | async-done | bytes 2097168 | tf_op jit(solution)/shard_map/all_gather | solution.py:38
  495.9 31.2 %while.109 = (s32[]{:T(128)}, bf16[2,512,8,64]{1,3,2,0:T(8,128)(2,1)}, f32[2,8,512,1]{2,1,3,0:T(8,128)S(1)}, s32[]{:T(128)}, s32[2]{0:T(128)S(1)}, /*index=5*/bf...) while((s32[]{:T(128)}, ...), condition=%wide.region_15.16_spmd, body=%wide.region_12.15_spmd.sunk | while | flops 1120138240 | bytes 66195716 | solution.py:106
  535.3 28.6 %while.111 = (s32[]{:T(128)}, bf16[2,512,8,64]{1,3,2,0:T(8,128)(2,1)}, f32[2,8,512,1]{2,1,3,0:T(8,128)S(1)}, s32[]{:T(128)}, s32[2]{0:T(128)S(1)}, /*index=5*/bf...) while((s32[]{:T(128)}, ...), condition=%wide.region_35.36_spmd, body=%wide.region_32.35_spmd.sunk | while | flops 1120138240 | bytes 62001388 | solution.py:106
  607.4 30.9 %all-gather.25.cloned.1.call-done = bf16[1024,1024]{1,0:T(8,128)(2,1)} async-done(((bf16[512,1024]{1,0:T(8,128)(2,1)}), bf16[1024,1024]{1,0:T(8,128)(2,1)}) %all-gather.25.cloned.1.call-update) | async-done | bytes 2097168 | tf_op jit(solution)/shard_map/all_gather | solution.py:38
  649.2 24.2 %all-gather.47.cloned.1.call-done = bf16[1,1,1024,1024]{3,2,1,0:T(8,128)(2,1)} async-done(((bf16[1,1,512,1024]{3,2,1,0:T(8,128)(2,1)}), bf16[1,1,1024,1024]{3,2,1,0:T(8,128)(2,1)}) %all-gather.47.cloned.1.call-update) | async-done | bytes 2097168 | tf_op jit(solution)/shard_map/all_gather | solution.py:52
  719.4 23.7 %reduce-scatter.33.cloned.1.call-done = bf16[512,1024]{1,0:T(8,128)(2,1)} async-done(((bf16[1024,1024]{1,0:T(8,128)(2,1)}), bf16[512,1024]{1,0:T(8,128)(2,1)}) %reduce-scatter.33.cloned.1.call-update) | async-done | bytes 1048592 | tf_op jit(solution)/shard_map/reduce_scatter | solution.py:56
  745.8 31.3 %reduce-scatter.23.cloned.1.call-done = bf16[512,1024]{1,0:T(8,128)(2,1)} async-done(((bf16[1024,1024]{1,0:T(8,128)(2,1)}), bf16[512,1024]{1,0:T(8,128)(2,1)}) %reduce-scatter.23.cloned.1.call-update) | async-done | bytes 1048592 | tf_op jit(solution)/shard_map/reduce_scatter | solution.py:46
  783.7 28.0 %all-gather.49.cloned.1.call-done = bf16[1,1,1024,1024]{3,2,1,0:T(8,128)(2,1)} async-done(((bf16[1,1,512,1024]{3,2,1,0:T(8,128)(2,1)}), bf16[1,1,1024,1024]{3,2,1,0:T(8,128)(2,1)}) %all-gather.49.cloned.1.call-update) | async-done | bytes 2097168 | tf_op jit(solution)/shard_map/all_gather | solution.py:52
  852.0 86.7 %while.112 = (s32[]{:T(128)}, f32[1024,8,64]{0,2,1:T(8,128)}, f32[1024,8,64]{0,2,1:T(8,128)}, bf16[2,512,8,64]{1,3,2,0:T(8,128)(2,1)}, s32[2]{0:T(128)S(1)}, /*i...) while((s32[]{:T(128)}, f32[1024,8,64]{0,2,1:T(8,128)}, ...), condition=%wide.region_45.46_spmd.clone, body=%wide.region_43.45_spmd.clone.sunk | while | flops 2724983808 | bytes 207702432 | solution.py:148
  991.7 33.2 %all-gather.41.cloned.1.call-done = bf16[1024,1024]{1,0:T(8,128)(2,1)} async-done(((bf16[512,1024]{1,0:T(8,128)(2,1)}), bf16[1024,1024]{1,0:T(8,128)(2,1)}) %all-gather.41.cloned.1.call-update) | async-done | bytes 2097168 | tf_op jit(solution)/shard_map/all_gather | solution.py:52
  1030.2 86.7 %while.114 = (s32[]{:T(128)}, f32[1024,8,64]{0,2,1:T(8,128)}, f32[1024,8,64]{0,2,1:T(8,128)}, bf16[2,512,8,64]{1,3,2,0:T(8,128)(2,1)}, s32[2]{0:T(128)S(1)}, /*i...) while((s32[]{:T(128)}, f32[1024,8,64]{0,2,1:T(8,128)}, ...), condition=%wide.region_63.64_spmd.clone, body=%wide.region_61.63_spmd.clone.sunk | while | flops 2724983808 | bytes 207702432 | solution.py:148
  1167.2 27.4 %all-gather.37.cloned.1.call-done = bf16[1024,1024]{1,0:T(8,128)(2,1)} async-done(((bf16[512,1024]{1,0:T(8,128)(2,1)}), bf16[1024,1024]{1,0:T(8,128)(2,1)}) %all-gather.37.cloned.1.call-update) | async-done | bytes 2097168 | tf_op jit(solution)/shard_map/all_gather | solution.py:52
  1346.6 114.2 %while.115 = (s32[]{:T(128)}, f32[1024,8,64]{0,2,1:T(8,128)}, f32[1024,8,64]{0,2,1:T(8,128)}, bf16[2,512,8,64]{1,3,2,0:T(8,128)(2,1)}, s32[2]{0:T(128)S(1)}, /*i...) while((s32[]{:T(128)}, f32[1024,8,64]{0,2,1:T(8,128)}, ...), condition=%wide.region_72.73_spmd.clone, body=%wide.region_70.72_spmd.clone.sunk | while | flops 2726558208 | bytes 225534288 | solution.py:148
  1476.4 114.2 %while.113 = (s32[]{:T(128)}, f32[1024,8,64]{0,2,1:T(8,128)}, f32[1024,8,64]{0,2,1:T(8,128)}, bf16[2,512,8,64]{1,3,2,0:T(8,128)(2,1)}, s32[2]{0:T(128)S(1)}, /*i...) while((s32[]{:T(128)}, f32[1024,8,64]{0,2,1:T(8,128)}, ...), condition=%wide.region_54.55_spmd.clone, body=%wide.region_52.54_spmd.clone.sunk | while | flops 2726558208 | bytes 225534288 | solution.py:148
  1673.7 98.0 %all-reduce.5.cloned.1.call-done = (f32[2,1024]{1,0:T(2,128)}, f32[2,1024]{1,0:T(2,128)}, f32[2,7,1024]{2,1,0:T(8,128)}, f32[2,7,1024]{2,1,0:T(8,128)}) async-done(((f32[2,1024]{1,0:T(2,128)}, f32[2,1024]{1,0:T(2,128)}, f32[2,7,1024]{2,1,0:T(8,128)}, f32[2,7,1024]{2,1,0:T(8,128)}), (f32[2,1024]{1,0:T(2,128)}, f32[2,1024]{1,0:T(2,128)}, f32[2,7,1024]{2,1,0:T(8,128)}, ...) | async-done | bytes 131088 | tf_op jit(solution)/shard_map/psum | solution.py:316
  1774.8 447.7 %all-reduce.7.cloned.1.call-done = (bf16[2,1024,3,512]{1,3,2,0:T(8,128)(2,1)}, bf16[2,512,1024]{2,1,0:T(8,128)(2,1)}, bf16[2,1024,2048]{2,1,0:T(8,128)(2,1)}, bf16[2,2048,1024]{2,1,0:T(8,128)(2,1)}) async-done(((bf16[2,1024,3,512]{1,3,2,0:T(8,128)(2,1)}, bf16[2,512,1024]{2,1,0:T(8,128)(2,1)}, bf16[2,1024,2048]{2,1,0:T(8,128)(2,1)}, bf16[2,2048,1024]{2,1,0:T(8,128)(2,1)}), ...) | async-done | bytes 25165840 | tf_op jit(solution)/shard_map/psum | solution.py:311
  (942 shorter events, 1256.6 us)
Async XLA Ops:
  14.1 124.5 %reduce-scatter.17.cloned.1.call-start = ((), (), s32[]{:S(2)}) async-start(), calls=%async_computation.17 | async-start | bytes 3145728 | tf_op jit(solution)/shard_map/reduce_scatter | solution.py:46
  142.0 121.8 %reduce-scatter.25.cloned.1.call-start = ((), (), s32[]{:S(2)}) async-start(), calls=%async_computation.25 | async-start | bytes 3145728 | tf_op jit(solution)/shard_map/reduce_scatter | solution.py:46
  269.8 102.5 %reduce-scatter.27.cloned.1.call-start = ((), (), s32[]{:S(2)}) async-start(), calls=%async_computation.27 | async-start | bytes 3145728 | tf_op jit(solution)/shard_map/reduce_scatter | solution.py:46
  322.0 85.2 %reduce-scatter.19.cloned.1.call-start = ((), (), s32[]{:S(2)}) async-start(), calls=%async_computation.19 | async-start | bytes 3145728 | tf_op jit(solution)/shard_map/reduce_scatter | solution.py:46
  356.8 90.3 %all-gather.31.cloned.1.call-start = ((), (), s32[]{:S(2)}) async-start(), calls=%async_computation.28 | async-start | bytes 3145728 | tf_op jit(solution)/shard_map/all_gather | solution.py:38
  418.4 154.4 %reduce-scatter.21.cloned.1.call-start = ((), (), s32[]{:S(2)}) async-start(), calls=%async_computation.21 | async-start | bytes 3145728 | tf_op jit(solution)/shard_map/reduce_scatter | solution.py:46
  577.0 96.5 %all-gather.47.cloned.1.call-start = ((), (), s32[]{:S(2)}) async-start(), calls=%async_computation.46 | async-start | bytes 3145728 | tf_op jit(solution)/shard_map/all_gather | solution.py:52
  580.5 128.1 %all-gather.33.cloned.1.call-start = ((), (), s32[]{:S(2)}) async-start(), calls=%async_computation.30 | async-start | bytes 3145728 | tf_op jit(solution)/shard_map/all_gather | solution.py:38
  607.4 135.7 %reduce-scatter.33.cloned.1.call-start = ((), (), s32[]{:S(2)}) async-start(), calls=%async_computation.32 | async-start | bytes 3145728 | tf_op jit(solution)/shard_map/reduce_scatter | solution.py:56
  696.1 81.0 %reduce-scatter.23.cloned.1.call-start = ((), (), s32[]{:S(2)}) async-start(), calls=%async_computation.23 | async-start | bytes 3145728 | tf_op jit(solution)/shard_map/reduce_scatter | solution.py:46
  707.4 104.3 %all-gather.49.cloned.1.call-start = ((), (), s32[]{:S(2)}) async-start(), calls=%async_computation.47 | async-start | bytes 3145728 | tf_op jit(solution)/shard_map/all_gather | solution.py:52
  708.0 139.0 %all-gather.35.cloned.1.call-start = ((), (), s32[]{:S(2)}) async-start(), calls=%async_computation.33 | async-start | bytes 3145728 | tf_op jit(solution)/shard_map/all_gather | solution.py:52
  783.3 166.9 %reduce-scatter.41.cloned.1.call-start = ((), (), s32[]{:S(2)}) async-start(), calls=%async_computation.39 | async-start | bytes 3145728 | tf_op jit(solution)/shard_map/reduce_scatter | solution.py:56
  834.4 120.0 %reduce-scatter.31.cloned.1.call-start = ((), (), s32[]{:S(2)}) async-start(), calls=%async_computation.31 | async-start | bytes 3145728 | tf_op jit(solution)/shard_map/reduce_scatter | solution.py:46
  845.6 136.7 %reduce-scatter.35.cloned.1.call-start = ((), (), s32[]{:S(2)}) async-start(), calls=%async_computation.34 | async-start | bytes 3145728 | tf_op jit(solution)/shard_map/reduce_scatter | solution.py:56
  991.6 168.4 %reduce-scatter.43.cloned.1.call-start = ((), (), s32[]{:S(2)}) async-start(), calls=%async_computation.41 | async-start | bytes 3145728 | tf_op jit(solution)/shard_map/reduce_scatter | solution.py:56
  1149.0 87.5 %all-gather.43.cloned.1.call-start = ((), (), s32[]{:S(2)}) async-start(), calls=%async_computation.42 | async-start | bytes 3145728 | tf_op jit(solution)/shard_map/all_gather | solution.py:52
  1166.8 127.9 %reduce-scatter.37.cloned.1.call-start = ((), (), s32[]{:S(2)}) async-start(), calls=%async_computation.36 | async-start | bytes 3145728 | tf_op jit(solution)/shard_map/reduce_scatter | solution.py:56
  1260.1 81.3 %all-gather.45.cloned.1.call-start = ((), (), s32[]{:S(2)}) async-start(), calls=%async_computation.44 | async-start | bytes 3145728 | tf_op jit(solution)/shard_map/all_gather | solution.py:52
  1308.1 163.4 %all-gather.39.cloned.1.call-start = ((), (), s32[]{:S(2)}) async-start(), calls=%async_computation.37 | async-start | bytes 3145728 | tf_op jit(solution)/shard_map/all_gather | solution.py:52
  1332.4 310.6 %reduce-scatter.47.cloned.1.call-start = ((), (), s32[]{:S(2)}) async-start(), calls=%async_computation.45 | async-start | bytes 3145728 | tf_op jit(solution)/shard_map/reduce_scatter | solution.py:56
  1471.4 171.6 %reduce-scatter.39.cloned.1.call-start = ((), (), s32[]{:S(2)}) async-start(), calls=%async_computation.38 | async-start | bytes 3145728 | tf_op jit(solution)/shard_map/reduce_scatter | solution.py:56
  1600.7 171.0 %all-reduce.5.cloned.1.call-start = ((), (), s32[]{:S(2)}) async-start(), calls=%async_computation.48 | async-start | bytes 294912 | tf_op jit(solution)/shard_map/psum | solution.py:316
  1649.9 572.6 %all-reduce.7.cloned.1.call-start = ((), (), s32[]{:S(2)}) async-start(), calls=%async_computation.49 | async-start | bytes 50331648 | tf_op jit(solution)/shard_map/psum | solution.py:311
  (259 other events, 2779.7 us)
Sparse Core Ops, SparseCore 0:
  14.3 35.8 all-gather.18
  142.1 33.1 all-gather.26
  231.9 31.8 reduce-scatter.24
  269.4 33.1 all-gather.28
  304.5 33.1 all-gather.20
  375.2 31.8 reduce-scatter.18
  413.9 33.1 all-gather.30
  449.0 33.1 all-gather.22
  571.1 31.9 reduce-scatter.28
  605.2 33.1 all-gather.24
  640.3 33.1 all-gather.46
  675.4 33.1 all-gather.32
  745.3 31.8 reduce-scatter.22
  778.6 33.1 all-gather.48
  813.8 33.1 all-gather.34
  950.2 32.1 reduce-scatter.34
  991.8 33.0 all-gather.40
  1128.0 31.8 reduce-scatter.42
  1161.4 33.1 all-gather.36
  1196.6 33.1 all-gather.42
  1308.2 33.1 all-gather.44
  1342.8 33.1 all-gather.38
  1650.0 121.7 all-reduce.4
  1777.2 445.1 all-reduce.6
  (10 shorter events, 317.6 us)
where the time goes:
time: 2280 us; the launch traced here: 2270 us
  waiting for transfers between devices  1070 us (47%)
  matrix products  689 us (30%)
  other arithmetic  273 us (12%)
  local copies, waits for them, and re-layouts  182 us (8%)
  loops' own time  33.9 us (1%)
    psum x1, waiting for transfers between devices, per_device(): lax.psum(jnp.stack(acc_qkv).astype(jnp.bfloat16), 'dp').astype(jnp.float32)  448 us
    all_gather x8, waiting for transfers between devices, gather_normed(): return lax.all_gather(normed_low, 'tensor', axis=0, tiled=True)  184 us
    reduce_scatter x8, waiting for transfers between devices, sum_branch(): lax.psum_scatter(branch_part.astype(jnp.bfloat16), 'tensor', scatter_dime...  162 us
    dot_general x16, matrix products, block_scores(): jnp.einsum('qhd,khd->hqk', query_block, key_rows, preferred_element_type=...  130 us
    all_gather x8, waiting for transfers between devices, gather_grad(): return lax.all_gather(grad_low, 'tensor', axis=0, tiled=True)  123 us
    psum x1, waiting for transfers between devices, per_device(): lax.psum((jnp.stack(acc_gain), jnp.stack(acc_bias), jnp.stack(acc_scale),...  98 us
    convert_element_type x8, other arithmetic, one_block(): grad_scores = (shares * (grad_shares - inner_sum)).astype(jnp.bfloat16)  83.9 us
    unnamed x413, local copies, waits for them, and re-layouts  63.5 us
  transfers between devices with their start and end apart: 34, of which 25 were waited for; matrix products, arithmetic and copies ran while one was open for 33% of the time, Pallas kernels for 0%

commit v1 on v0

--- a/solution.py
+++ b/solution.py
@@ -3,6 +3,8 @@
 import jax
 import jax.numpy as jnp
 from jax import lax
+from jax.experimental import pallas as pl
+from jax.experimental.pallas import tpu as pltpu
 from jax.sharding import PartitionSpec as P
 
 HEAD_DIM = 64
@@ -158,7 +160,7 @@
     return joined.astype(jnp.bfloat16)
 
 
-def per_device(
+def grouped_device(
     frames_in,
     phone_len,
     frame_len,
@@ -331,9 +333,422 @@
     )
 
 
+bf16,f32=jnp.bfloat16,jnp.float32
+NT=(((1,),(1,)),((),()))
+TN=(((0,),(0,)),((),()))
+
+def _limits(lims_ref, start, rows, causal, axis):
+    prefix, valid = lims_ref[0], lims_ref[1]
+    shape=(rows,1) if axis==0 else (1,rows)
+    pos=start+lax.broadcasted_iota(jnp.int32,shape,axis)
+    if causal:
+        return jnp.minimum(jnp.maximum(pos,prefix-1),valid-1)
+    return jnp.zeros(shape,jnp.int32)+(valid-1)
+
+def fwd_kernel(causal, bq, lims_ref, q_ref, k_ref, v_ref, o_ref, l_ref):
+    length=q_ref.shape[0]
+    lane=lax.broadcasted_iota(jnp.int32,(bq,128),1)
+    def block(start, kk):
+        q=q_ref[pl.ds(start,bq),:]*jnp.asarray(0.125,bf16)
+        lim=_limits(lims_ref,start,bq,causal,0)
+        outs=[];rows=[]
+        for h in range(2):
+            qm=jnp.where((lane<HEAD_DIM)==(h==0),q,jnp.zeros_like(q))
+            s=lax.dot_general(qm,k_ref[0:kk,:],NT,preferred_element_type=f32)
+            key=lax.broadcasted_iota(jnp.int32,(bq,kk),1)
+            s=jnp.where(key<=lim,s,-1e9)
+            m=jnp.max(s,axis=1,keepdims=True)
+            e=jnp.exp(s-m)
+            l=jnp.sum(e,axis=1,keepdims=True)
+            o=jnp.dot(e.astype(bf16),v_ref[0:kk,:],preferred_element_type=f32)*(1.0/l)
+            outs.append(o); rows.append(m+jnp.log(l))
+        o_ref[pl.ds(start,bq),:]=jnp.where(lane<HEAD_DIM,outs[0],outs[1]).astype(bf16)
+        both=jnp.where(lane<HEAD_DIM,rows[0],rows[1])
+        bt=both.T
+        l_ref[0,0:1,pl.ds(start,bq)]=bt[0:1,:]
+        l_ref[0,1:2,pl.ds(start,bq)]=bt[HEAD_DIM:HEAD_DIM+1,:]
+    nq=length//bq
+    if causal:
+        for i in range(nq): block(i*bq,(i+1)*bq)
+    else:
+        def body(i,c):
+            block(pl.multiple_of(i*bq,bq),length); return c
+        lax.fori_loop(0,nq,body,0)
+
+def attn_fwd(qkv, lims, causal, bq=256):
+    length=qkv.shape[0]; width=qkv.shape[1]//3; pairs=width//128
+    spec=lambda off: pl.BlockSpec((length,128),lambda i,off=off:(0,off*pairs+i))
+    return pl.pallas_call(partial(fwd_kernel,causal,bq),
+        grid=(pairs,),
+        in_specs=[pl.BlockSpec(memory_space=pltpu.SMEM),spec(0),spec(1),spec(2)],
+        out_specs=[pl.BlockSpec((length,128),lambda i:(0,i)),pl.BlockSpec((1,2,length),lambda i:(i,0,0))],
+        out_shape=[jax.ShapeDtypeStruct((length,width),bf16),jax.ShapeDtypeStruct((pairs,2,length),f32)],
+        compiler_params=pltpu.CompilerParams(vmem_limit_bytes=48*2**20),
+        cost_estimate=pl.CostEstimate(flops=pairs*2*4*length*length*128,bytes_accessed=length*width*8,transcendentals=pairs*2*length*length),
+        name="attn_fwd_"+("causal" if causal else "full"),
+    )(lims,qkv,qkv,qkv)
+
+def bwd_kernel(causal,bq,lims_ref,q_ref,k_ref,v_ref,l_ref,do_ref,grad_ref,dk_acc,dv_acc):
+    length=q_ref.shape[0]
+    lane=lax.broadcasted_iota(jnp.int32,(bq,128),1)
+    dk_acc[...]=jnp.zeros_like(dk_acc); dv_acc[...]=jnp.zeros_like(dv_acc)
+    width=grad_ref.shape[1]//3
+    at=[pl.multiple_of(part*width+pl.program_id(0)*128,128) for part in range(3)]
+    def block(start,kk):
+        q=q_ref[pl.ds(start,bq),:]*jnp.asarray(0.125,bf16)
+        do=do_ref[pl.ds(start,bq),:]
+        lim=_limits(lims_ref,start,bq,causal,1)
+        dqs=[]
+        for h in range(2):
+            sel=(lane<HEAD_DIM)==(h==0)
+            qm=jnp.where(sel,q,jnp.zeros_like(q)); dom=jnp.where(sel,do,jnp.zeros_like(do))
+            s=lax.dot_general(k_ref[0:kk,:],qm,NT,preferred_element_type=f32)
+            dp=lax.dot_general(v_ref[0:kk,:],dom,NT,preferred_element_type=f32)
+            key=lax.broadcasted_iota(jnp.int32,(kk,bq),0)
+            lrow=l_ref[0,h:h+1,pl.ds(start,bq)]
+            p=jnp.where(key<=lim,jnp.exp(s-lrow),0.0)
+            pd=p*dp
+            D=jnp.sum(pd,axis=0,keepdims=True)
+            ds=(pd-p*D).astype(bf16)
+            dv_acc[0:kk,:]+=jnp.dot(p.astype(bf16),dom,preferred_element_type=f32)
+            dk_acc[0:kk,:]+=jnp.dot(ds,qm,preferred_element_type=f32)
+            dqs.append(lax.dot_general(ds,k_ref[0:kk,:],TN,preferred_element_type=f32))
+        grad_ref[pl.ds(start,bq),pl.ds(at[0],128)]=(jnp.where(lane<HEAD_DIM,dqs[0],dqs[1])*0.125).astype(bf16)
+    nq=length//bq
+    if causal:
+        for i in range(nq): block(i*bq,(i+1)*bq)
+    else:
+        def body(i,c):
+            block(pl.multiple_of(i*bq,bq),length); return c
+        lax.fori_loop(0,nq,body,0)
+    grad_ref[:,pl.ds(at[1],128)]=dk_acc[...].astype(bf16)
+    grad_ref[:,pl.ds(at[2],128)]=dv_acc[...].astype(bf16)
+
+def attn_bwd(qkv,L,do,lims,causal,bq=256):
+    length=qkv.shape[0]; width=qkv.shape[1]//3; pairs=width//128
+    spec=lambda off: pl.BlockSpec((length,128),lambda i,off=off:(0,off*pairs+i))
+    one=pl.BlockSpec((length,128),lambda i:(0,i))
+    return pl.pallas_call(partial(bwd_kernel,causal,bq),
+        grid=(pairs,),
+        in_specs=[pl.BlockSpec(memory_space=pltpu.SMEM),spec(0),spec(1),spec(2),pl.BlockSpec((1,2,length),lambda i:(i,0,0)),one],
+        out_specs=pl.BlockSpec((length,3*width),lambda i:(0,0)),
+        out_shape=jax.ShapeDtypeStruct((length,3*width),bf16),
+        scratch_shapes=[pltpu.VMEM((length,128),f32)]*2,
+        compiler_params=pltpu.CompilerParams(vmem_limit_bytes=48*2**20),
+        cost_estimate=pl.CostEstimate(flops=pairs*2*10*length*length*128,bytes_accessed=length*width*14,transcendentals=pairs*2*length*length),
+        name="attn_bwd_"+("causal" if causal else "full"),
+    )(lims,qkv,qkv,qkv,L,do)
+
+
+def swap_tensor(block):
+    return lax.ppermute(block, "tensor", [(0, 1), (1, 0)])
+
+
+def swap_bit(block, bit, dp_size):
+    return lax.ppermute(block, "dp", [(place, place ^ (1 << bit)) for place in range(dp_size)])
+
+
+def in_order(flag, mine, other):
+    first = jnp.where(flag == 0, mine, other)
+    second = jnp.where(flag == 0, other, mine)
+    return jnp.concatenate([first, second], axis=0)
+
+
+def add_rounded(left, right):
+    return (left.astype(f32) + right.astype(f32)).astype(bf16)
+
+
+def norm_forward(rows, gain_row, shift_row):
+    mean = jnp.mean(rows, axis=-1, keepdims=True)
+    centered = rows - mean
+    rate = lax.rsqrt(jnp.mean(centered * centered, axis=-1, keepdims=True) + norm_eps)
+    normed = centered * rate * gain_row + shift_row
+    return normed.astype(bf16), (rows, mean, rate)
+
+
+def norm_backward(saved, grad_normed, gain_row):
+    rows, mean, rate = saved
+    unit = (rows - mean) * rate
+    grad_unit = grad_normed * gain_row
+    grad_rows = rate * (
+        grad_unit
+        - jnp.mean(grad_unit, axis=-1, keepdims=True)
+        - unit * jnp.mean(grad_unit * unit, axis=-1, keepdims=True)
+    )
+    return grad_rows, jnp.sum(grad_normed * unit, axis=0), jnp.sum(grad_normed, axis=0)
+
+
+def gelu_pair(hidden):
+    square = hidden * hidden
+    inner = 0.7978845608 * hidden * (1.0 + 0.044715 * square)
+    bent = jnp.tanh(inner)
+    value = 0.5 * hidden * (1.0 + bent)
+    slope = 0.5 * (1.0 + bent) + 0.5 * hidden * (1.0 - bent * bent) * 0.7978845608 * (
+        1.0 + 3.0 * 0.044715 * square
+    )
+    return value.astype(bf16), slope.astype(bf16)
+
+
+def dot_sum(pairs, dims):
+    total = None
+    for left, right in pairs:
+        term = lax.dot_general(left, right, dims, preferred_element_type=f32)
+        total = term if total is None else total + term
+    return total
+
+
+NN = (((1,), (0,)), ((), ()))
+
+
+def quarter_of(kind, half, place):
+    if kind == "qkv":
+        heads = half.reshape(half.shape[0], 3, -1)
+        width = heads.shape[2] // 2
+        picked = lax.dynamic_slice_in_dim(heads, place * width, width, 2)
+        return picked.reshape(half.shape[0], 3 * width)
+    axis = 1 if kind == "up" else 0
+    width = half.shape[axis] // 2
+    return lax.dynamic_slice_in_dim(half, place * width, width, axis)
+
+
+def row_half(block, place):
+    height = block.shape[0] // 2
+    return lax.dynamic_slice_in_dim(block, place * height, height, 0)
+
+
+def paired_device(
+    dp_size,
+    frames_in,
+    phone_len,
+    frame_len,
+    section,
+    norm_gain,
+    norm_bias,
+    ada_scale,
+    ada_shift,
+    w_qkv,
+    w_out,
+    w_up,
+    w_down,
+    out_grad,
+):
+    model_width = frames_in.shape[3]
+    section_count = ada_scale.shape[1]
+    side = lax.axis_index("tensor")
+    place = lax.axis_index("dp")
+    bit_count = dp_size.bit_length() - 1
+    bits = [(place >> bit) & 1 for bit in range(bit_count)]
+    core = bits[0]
+
+    def whole_rows(halves):
+        mine = lax.dynamic_index_in_dim(halves[:, 0], side, 0, keepdims=False)
+        away = lax.dynamic_index_in_dim(halves[:, 0], 1 - side, 0, keepdims=False)
+        return in_order(side, mine, swap_tensor(away))
+
+    def split_rows(rows):
+        height = rows.shape[0] // 2
+        mine = lax.dynamic_slice_in_dim(rows, side * height, height, 0)
+        away = lax.dynamic_slice_in_dim(rows, (1 - side) * height, height, 0)
+        other = swap_tensor(away.astype(bf16)).astype(f32)
+        first = jnp.where(side == 0, mine, other)
+        second = jnp.where(side == 0, other, mine)
+        return jnp.stack([first, second])[:, None]
+
+    def other_half(kind, half):
+        piece = row_half(quarter_of(kind, half, core), bits[1])
+        piece = swap_tensor(piece)
+        near = in_order(bits[1], piece, swap_bit(piece, 1, dp_size))
+        far = swap_bit(near, 0, dp_size)
+        return [half, near, far]
+
+    def reduce_grad(kind, grads):
+        own, near, far = grads
+        own_there = swap_bit(quarter_of(kind, own, 1 - core), 0, dp_size)
+        near_there = swap_bit(far, 0, dp_size)
+        across = swap_tensor(add_rounded(near, near_there))
+        total = quarter_of(kind, own, core).astype(f32) + own_there.astype(f32) + across.astype(f32)
+        total = total.astype(bf16)
+        for bit in range(1, bit_count):
+            sent = swap_bit(row_half(total, 1 - bits[bit]), bit, dp_size)
+            total = add_rounded(row_half(total, bits[bit]), sent)
+        whole = lax.all_gather(total, "dp", axis=0, tiled=False)
+        rows, columns = total.shape
+        whole = whole.reshape((2,) * bit_count + (rows, columns))
+        order = tuple(bit_count - 1 - bit for bit in range(1, bit_count))
+        core_axis = bit_count - 1
+        full_rows = rows * 2 ** (bit_count - 1)
+        if kind in ("out", "down"):
+            whole = whole.transpose((core_axis,) + order + (bit_count, bit_count + 1))
+            return whole.reshape(2 * full_rows, columns)
+        if kind == "up":
+            whole = whole.transpose(order + (bit_count, core_axis, bit_count + 1))
+            return whole.reshape(full_rows, 2 * columns)
+        whole = whole.reshape((2,) * bit_count + (rows, 3, columns // 3))
+        whole = whole.transpose(order + (bit_count, bit_count + 1, core_axis, bit_count + 2))
+        return whole.reshape(full_rows, 3, 2 * columns // 3)
+
+    prefix = lax.dynamic_index_in_dim(phone_len[:, 0], side, 0, keepdims=False)
+    frames = lax.dynamic_index_in_dim(frame_len[:, 0], side, 0, keepdims=False)
+    chosen = lax.dynamic_index_in_dim(section[:, 0], side, 0, keepdims=False)
+    limits = jnp.stack([prefix, prefix + frames]).astype(jnp.int32)
+    picker = (lax.iota(jnp.int32, section_count) == chosen).astype(f32)[:, None]
+
+    gains = [
+        [norm_gain[0], norm_gain[1]],
+        [jnp.sum(picker * ada_scale[part], axis=0) for part in range(2)],
+    ]
+    shifts = [
+        [norm_bias[0], norm_bias[1]],
+        [jnp.sum(picker * ada_shift[part], axis=0) for part in range(2)],
+    ]
+
+    rows = whole_rows(frames_in).astype(f32)
+    weights = []
+    for layer in range(2):
+        weights.append(
+            {
+                "qkv": other_half("qkv", w_qkv[layer].reshape(model_width, -1)),
+                "out": other_half("out", w_out[layer]),
+                "up": other_half("up", w_up[layer]),
+                "down": other_half("down", w_down[layer]),
+            }
+        )
+    kept = []
+    for layer in range(2):
+        causal = layer == 0
+        mats = weights[layer]
+        normed, norm_kept = norm_forward(rows, gains[layer][0], shifts[layer][0])
+        projected = [
+            jnp.dot(normed, part, preferred_element_type=f32).astype(bf16) for part in mats["qkv"]
+        ]
+        mixed = [attn_fwd(part, limits, causal, 512) for part in projected]
+        rows = rows + dot_sum([(mix[0], part) for mix, part in zip(mixed, mats["out"])], NN)
+        kept.append((normed, norm_kept, projected, mixed))
+        normed, norm_kept = norm_forward(rows, gains[layer][1], shifts[layer][1])
+        pairs = [gelu_pair(jnp.dot(normed, part, preferred_element_type=f32)) for part in mats["up"]]
+        rows = rows + dot_sum([(pair[0], part) for pair, part in zip(pairs, mats["down"])], NN)
+        kept.append((normed, norm_kept, pairs))
+    frames_out = split_rows(rows)
+
+    grad_rows = whole_rows(out_grad).astype(f32)
+    sums = {}
+    norm_sums = [[None, None], [None, None]]
+    for layer in (1, 0):
+        causal = layer == 0
+        mats = weights[layer]
+        normed, norm_kept, pairs = kept[2 * layer + 1]
+        low = grad_rows.astype(bf16)
+        grad_hidden = [
+            (
+                lax.dot_general(low, part, NT, preferred_element_type=f32) * pair[1].astype(f32)
+            ).astype(bf16)
+            for pair, part in zip(pairs, mats["down"])
+        ]
+        sums["down", layer] = reduce_grad(
+            "down",
+            [
+                lax.dot_general(pair[0], low, TN, preferred_element_type=f32).astype(bf16)
+                for pair in pairs
+            ],
+        )
+        sums["up", layer] = reduce_grad(
+            "up",
+            [
+                lax.dot_general(normed, part, TN, preferred_element_type=f32).astype(bf16)
+                for part in grad_hidden
+            ],
+        )
+        grad_normed = dot_sum(list(zip(grad_hidden, mats["up"])), NT)
+        added, grad_gain, grad_shift = norm_backward(norm_kept, grad_normed, gains[layer][1])
+        norm_sums[layer][1] = (grad_gain, grad_shift)
+        grad_rows = grad_rows + added
+
+        normed, norm_kept, projected, mixed = kept[2 * layer]
+        low = grad_rows.astype(bf16)
+        sums["out", layer] = reduce_grad(
+            "out",
+            [
+                lax.dot_general(mix[0], low, TN, preferred_element_type=f32).astype(bf16)
+                for mix in mixed
+            ],
+        )
+        grad_mixed = [
+            lax.dot_general(low, part, NT, preferred_element_type=f32).astype(bf16)
+            for part in mats["out"]
+        ]
+        grad_projected = [
+            attn_bwd(part, mix[1], grad_mix, limits, causal, 512)
+            for part, mix, grad_mix in zip(projected, mixed, grad_mixed)
+        ]
+        sums["qkv", layer] = reduce_grad(
+            "qkv",
+            [
+                lax.dot_general(normed, part, TN, preferred_element_type=f32).astype(bf16)
+                for part in grad_projected
+            ],
+        )
+        grad_normed = dot_sum(list(zip(grad_projected, mats["qkv"])), NT)
+        added, grad_gain, grad_shift = norm_backward(norm_kept, grad_normed, gains[layer][0])
+        norm_sums[layer][0] = (grad_gain, grad_shift)
+        grad_rows = grad_rows + added
+
+    frames_grad = split_rows(grad_rows)
+
+    def everywhere(block):
+        block = block + swap_tensor(block)
+        for bit in range(bit_count):
+            block = block + swap_bit(block, bit, dp_size)
+        return block
+
+    late = everywhere(
+        jnp.stack(
+            [
+                norm_sums[0][0][0],
+                norm_sums[0][1][0],
+                norm_sums[0][0][1],
+                norm_sums[0][1][1],
+            ]
+        )
+    )
+    early = everywhere(
+        jnp.concatenate(
+            [
+                picker * norm_sums[1][0][0][None],
+                picker * norm_sums[1][1][0][None],
+                picker * norm_sums[1][0][1][None],
+                picker * norm_sums[1][1][1][None],
+            ]
+        )
+    ).reshape(4, section_count, model_width)
+
+    def both(kind):
+        return jnp.stack([sums[kind, 0].astype(f32), sums[kind, 1].astype(f32)])
+
+    return (
+        frames_out,
+        frames_grad,
+        both("qkv"),
+        both("out"),
+        both("up"),
+        both("down"),
+        late[0:2],
+        late[2:4],
+        early[0:2],
+        early[2:4],
+    )
+
+
+def per_device(dp_size, tensor_size, *arrays):
+    micro_count, local_seqs = arrays[0].shape[:2]
+    paired = micro_count == 2 and tensor_size == 2 and local_seqs == 1
+    if paired and dp_size >= 4 and dp_size & (dp_size - 1) == 0:
+        return paired_device(dp_size, *arrays)
+    return grouped_device(*arrays)
+
+
 def solution(mesh):
     return jax.shard_map(
-        per_device,
+        partial(per_device, mesh.shape["dp"], mesh.shape["tensor"]),
         mesh=mesh,
         in_specs=(
             P(None, "dp", "tensor", None),

time: 2280 us -> 1530 us (0.67)
  waiting for transfers between devices: 1070 us -> 576 us
  matrix products: 689 us -> 341 us
  Pallas kernels: 0 us -> 175 us
  other arithmetic: 273 us -> 125 us
  starting transfers between devices: 3.6 us -> 76.1 us
  loops' own time: 33.9 us -> 0 us
  local copies, waits for them, and re-layouts: 182 us -> 211 us
    ppermute x0 -> x86, waiting for transfers between devices: none -> 576 us  [the longest x22 301 us: swap_tensor(): return lax.ppermute(block, 'tensor', [(0, 1), (1, 0)])]
    psum x2 -> x0, waiting for transfers between devices: 546 us -> none  [the longest x1 448 us: per_device(): lax.psum(jnp.stack(acc_qkv).astype(jnp.bfloat16), 'dp').astype(jnp.float32)]
    dot_general x112 -> x72, matrix products: 689 us -> 341 us  [the longest x24 129 us: dot_sum(): term = lax.dot_general(left, right, dims, preferred_element_type=f32)]
    all_gather x16 -> x8, waiting for transfers between devices: 307 us -> 0.05 us  [reduce_grad(): whole = lax.all_gather(total, 'dp', axis=0, tiled=False)]
    reduce_scatter x16 -> x0, waiting for transfers between devices: 212 us -> none  [the longest x8 162 us: sum_branch(): lax.psum_scatter(branch_part.astype(jnp.bfloat16), 'tensor', scatter_dime...]
    pallas_call x0 -> x12, Pallas kernels: none -> 175 us  [the longest x6 108 us: attn_bwd(): pl.pallas_call(partial(bwd_kernel, causal, bq), grid=(pairs,), in_specs=[...]
    convert_element_type x0 -> x20, local copies, waits for them, and re-layouts: none -> 102 us  [the longest x14 88 us: both(): return jnp.stack([sums[kind, 0].astype(f32), sums[kind, 1].astype(f32)])]
    reduce_sum x32 -> x6, other arithmetic: 85.7 us -> 2.51 us  [the longest x4 2.04 us: norm_forward(): jnp.mean(centered * centered, axis=-1, keepdims=True) + norm_eps]
  transfers between devices with their start and end apart: 34 -> 94, of which waited for: 25 -> 38; matrix products, arithmetic and copies ran while one was open for 33% -> 33% of each run, Pallas kernels for 0% -> 8%
where the time goes in v1:
time: 1530 us; the launch traced here: 1520 us
  waiting for transfers between devices  576 us (38%)
  matrix products  341 us (22%)
  local copies, waits for them, and re-layouts  211 us (14%)
  Pallas kernels  175 us (11%)
  other arithmetic  125 us (8%)
  starting transfers between devices  76.1 us (5%)
  between operations  17.7 us (1%)
    ppermute x22, waiting for transfers between devices, swap_tensor(): return lax.ppermute(block, 'tensor', [(0, 1), (1, 0)])  301 us
    ppermute x64, waiting for transfers between devices, swap_bit(): lax.ppermute(block, 'dp', [(place, place ^ 1 << bit) for place in range(d...  275 us
    dot_general x24, matrix products, dot_sum(): term = lax.dot_general(left, right, dims, preferred_element_type=f32)  129 us
    pallas_call x6, Pallas kernels, attn_bwd(): pl.pallas_call(partial(bwd_kernel, causal, bq), grid=(pairs,), in_specs=[...  108 us
    convert_element_type x14, local copies, waits for them, and re-layouts, both(): return jnp.stack([sums[kind, 0].astype(f32), sums[kind, 1].astype(f32)])  88 us
    pallas_call x6, Pallas kernels, attn_fwd(): pl.pallas_call(partial(fwd_kernel, causal, bq), grid=(pairs,), in_specs=[...  67.2 us
    dot_general x12, matrix products, paired_device(): lax.dot_general(normed, part, TN, preferred_element_type=f32).astype(bf16)  53.8 us
    dot_general x6, matrix products, paired_device(): lax.dot_general(low, part, NT, preferred_element_type=f32)  53.2 us
  transfers between devices with their start and end apart: 94, of which 38 were waited for; matrix products, arithmetic and copies ran while one was open for 33% of the time, Pallas kernels for 8%

profile of v1, /device:TPU:0, one launch (start us, length us, event | category | flops | bytes accessed | tf_op | source)
XLA Modules:
  0.0 1521.3 jit_solution(13762747581465542860)
XLA Ops:
  69.6 19.8 %collective-permute-done.15 = bf16[128,1024]{1,0:T(8,128)(2,1)} collective-permute-done((bf16[128,1024]{1,0:T(8,128)(2,1)S(1)}, bf16[128,1024]{1,0:T(8,128)(2,1)}, u32[]{:S(2)}, u32[]{:S(2)}) %collective-permute-start.15) | collective-permute-done | bytes 262176 | tf_op jit(solution)/shard_map/ppermute | solution.py:444
  110.8 44.3 %collective-permute-done.26 = bf16[512,1024]{0,1:T(8,128)(2,1)S(1)} collective-permute-done((bf16[512,1024]{0,1:T(8,128)(2,1)S(1)}, bf16[512,1024]{0,1:T(8,128)(2,1)S(1)}, u32[]{:S(2)}, u32[]{:S(2)}) %collective-permute-start.26) | collective-permute-done | bytes 1048608 | tf_op jit(solution)/shard_map/ppermute | solution.py:444
  157.1 14.2 attn_fwd_causal.3
  204.1 15.3 %collective-permute-done.8 = bf16[512,1024]{1,0:T(8,128)(2,1)S(1)} collective-permute-done((bf16[512,1024]{1,0:T(8,128)(2,1)}, bf16[512,1024]{1,0:T(8,128)(2,1)S(1)}, u32[]{:S(2)}, u32[]{:S(2)}) %collective-permute-start.8) | collective-permute-done | bytes 1048608 | tf_op jit(solution)/shard_map/ppermute | solution.py:448
  222.4 19.5 %collective-permute-done.10 = bf16[512,1024]{1,0:T(8,128)(2,1)S(1)} collective-permute-done((bf16[512,1024]{1,0:T(8,128)(2,1)}, bf16[512,1024]{1,0:T(8,128)(2,1)S(1)}, u32[]{:S(2)}, u32[]{:S(2)}) %collective-permute-start.10) | collective-permute-done | bytes 1048608 | tf_op jit(solution)/shard_map/ppermute | solution.py:448
  244.9 19.5 %collective-permute-done.20 = bf16[512,1024]{1,0:T(8,128)(2,1)S(1)} collective-permute-done((bf16[512,1024]{1,0:T(8,128)(2,1)}, bf16[512,1024]{1,0:T(8,128)(2,1)S(1)}, u32[]{:S(2)}, u32[]{:S(2)}) %collective-permute-start.20) | collective-permute-done | bytes 1048608 | tf_op jit(solution)/shard_map/ppermute | solution.py:448
  267.4 13.8 collective-permute-done.22
  360.9 18.9 %attn_fwd_full.3 = (bf16[1024,512]{1,0:T(8,128)(2,1)S(1)}, f32[4,2,1024]{2,1,0:T(2,128)S(1)}) custom-call(s32[2]{0:T(128)S(1)} %pad_add_fusion.lims_ref, bf16[1024,1536]{1,0:T(8,128)(2,1)S(1)} %convolution_convert_fusion.2.q_ref.k_ref.v_ref, bf16[1024,1536]{1,0:T(8,128)(2,1)S(1)} %convolution_convert_fusion.2.q_ref.k_ref.v_ref, ...), custom_call_target="tpu_custom_call" | custom-call | flops 4294967296 | bytes 4194304 | tf_op jit(solution)/shard_map/attn_fwd_full/pallas_call | solution.py:381
  411.7 15.4 %multiply_convert_fusion.1 = bf16[1024,2048]{1,0:T(8,128)(2,1)} fusion(f32[1024,2048]{1,0:T(8,128)} %fusion.19, bf16[2,2048,1024]{2,1,0:T(8,128)(2,1)} %param.24, bf16[512,1024]{0,1:T(8,128)(2,1)S(1)} %get-tuple-element.103, bf16[512,1024]{0,1:T(8,128)(2,1)S(1)} %get-tuple-element.102), kind=kOutput, calls=%fused_computation.4 | convolution fusion | flops 4341104640 | bytes 18874368 | tf_op jit(solution)/shard_map/dot_general | solution.py:643
  471.8 28.7 %attn_bwd_full.3 = bf16[1024,1536]{1,0:T(8,128)(2,1)S(1)} custom-call(s32[2]{0:T(128)S(1)} %pad_add_fusion.lims_ref, bf16[1024,1536]{1,0:T(8,128)(2,1)} %copy-done.21, bf16[1024,1536]{1,0:T(8,128)(2,1)} %copy-done.21, bf16[1024,1536]{1,0:T(8,128)(2,1)} %copy-done.21, f32[4,2,1024]{2,1,0:T(2,128)S(1)} %get-tuple-element.28.l_ref, ...), custom_call_target="tpu_custom_call" | custom-call | flops 10737418240 | bytes 7340032 | tf_op jit(solution)/shard_map/attn_bwd_full/pallas_call | solution.py:431
  508.7 14.4 attn_bwd_full.4
  526.1 14.4 attn_bwd_full.5
  631.3 24.9 %attn_bwd_causal.3 = bf16[1024,1536]{1,0:T(8,128)(2,1)S(1)} custom-call(s32[2]{0:T(128)S(1)} %pad_add_fusion.lims_ref, bf16[1024,1536]{1,0:T(8,128)(2,1)} %copy-done.20, bf16[1024,1536]{1,0:T(8,128)(2,1)} %copy-done.20, bf16[1024,1536]{1,0:T(8,128)(2,1)} %copy-done.20, f32[4,2,1024]{2,1,0:T(2,128)S(1)} %get-tuple-element.31.l_ref, ...), custom_call_target="tpu_custom_call" | custom-call | flops 10737418240 | bytes 7340032 | tf_op jit(solution)/shard_map/attn_bwd_causal/pallas_call | solution.py:431
  726.5 19.1 %collective-permute-done.30 = bf16[1024,768]{1,0:T(8,128)(2,1)} collective-permute-done((bf16[1024,768]{1,0:T(8,128)(2,1)}, bf16[1024,768]{1,0:T(8,128)(2,1)}, u32[]{:S(2)}, u32[]{:S(2)}) %collective-permute-start.30) | collective-permute-done | bytes 1572896 | tf_op jit(solution)/shard_map/ppermute | solution.py:444
  806.2 24.1 %collective-permute-done.36 = bf16[1024,768]{1,0:T(8,128)(2,1)} collective-permute-done((bf16[1024,768]{1,0:T(8,128)(2,1)}, bf16[1024,768]{1,0:T(8,128)(2,1)}, u32[]{:S(2)}, u32[]{:S(2)}) %collective-permute-start.36) | collective-permute-done | bytes 1572896 | tf_op jit(solution)/shard_map/ppermute | solution.py:444
  840.2 16.0 %collective-permute-done.37 = bf16[512,768]{1,0:T(8,128)(2,1)S(1)} collective-permute-done((bf16[512,768]{1,0:T(8,128)(2,1)S(1)}, bf16[512,768]{1,0:T(8,128)(2,1)S(1)}, u32[]{:S(2)}, u32[]{:S(2)}) %collective-permute-start.37) | collective-permute-done | bytes 786464 | tf_op jit(solution)/shard_map/ppermute | solution.py:448
  881.3 41.8 %collective-permute-done.66 = bf16[1024,1024]{1,0:T(8,128)(2,1)} collective-permute-done((bf16[1024,1024]{1,0:T(8,128)(2,1)}, bf16[1024,1024]{1,0:T(8,128)(2,1)}, u32[]{:S(2)}, u32[]{:S(2)}) %collective-permute-start.66) | collective-permute-done | bytes 2097184 | tf_op jit(solution)/shard_map/ppermute | solution.py:444
  928.3 22.9 %collective-permute-done.67 = bf16[512,1024]{1,0:T(8,128)(2,1)S(1)} collective-permute-done((bf16[512,1024]{1,0:T(8,128)(2,1)S(1)}, bf16[512,1024]{1,0:T(8,128)(2,1)S(1)}, u32[]{:S(2)}, u32[]{:S(2)}) %collective-permute-start.67) | collective-permute-done | bytes 1048608 | tf_op jit(solution)/shard_map/ppermute | solution.py:448
  994.2 44.6 %collective-permute-done.72 = bf16[1024,1024]{1,0:T(8,128)(2,1)S(1)} collective-permute-done((bf16[1024,1024]{1,0:T(8,128)(2,1)S(1)}, bf16[1024,1024]{1,0:T(8,128)(2,1)S(1)}, u32[]{:S(2)}, u32[]{:S(2)}) %collective-permute-start.72) | collective-permute-done | bytes 2097184 | tf_op jit(solution)/shard_map/ppermute | solution.py:444
  1041.1 22.2 %collective-permute-done.73 = bf16[512,1024]{1,0:T(8,128)(2,1)S(1)} collective-permute-done((bf16[512,1024]{1,0:T(8,128)(2,1)S(1)}, bf16[512,1024]{1,0:T(8,128)(2,1)S(1)}, u32[]{:S(2)}, u32[]{:S(2)}) %collective-permute-start.73) | collective-permute-done | bytes 1048608 | tf_op jit(solution)/shard_map/ppermute | solution.py:448
  1100.6 45.1 %collective-permute-done.54 = bf16[1024,1024]{1,0:T(8,128)(2,1)S(1)} collective-permute-done((bf16[1024,1024]{1,0:T(8,128)(2,1)S(1)}, bf16[1024,1024]{1,0:T(8,128)(2,1)S(1)}, u32[]{:S(2)}, u32[]{:S(2)}) %collective-permute-start.54) | collective-permute-done | bytes 2097184 | tf_op jit(solution)/shard_map/ppermute | solution.py:444
  1148.0 22.6 %collective-permute-done.55 = bf16[512,1024]{1,0:T(8,128)(2,1)S(1)} collective-permute-done((bf16[512,1024]{1,0:T(8,128)(2,1)S(1)}, bf16[512,1024]{1,0:T(8,128)(2,1)S(1)}, u32[]{:S(2)}, u32[]{:S(2)}) %collective-permute-start.55) | collective-permute-done | bytes 1048608 | tf_op jit(solution)/shard_map/ppermute | solution.py:448
  1209.0 45.1 %collective-permute-done.60 = bf16[1024,1024]{1,0:T(8,128)(2,1)S(1)} collective-permute-done((bf16[1024,1024]{1,0:T(8,128)(2,1)S(1)}, bf16[1024,1024]{1,0:T(8,128)(2,1)S(1)}, u32[]{:S(2)}, u32[]{:S(2)}) %collective-permute-start.60) | collective-permute-done | bytes 2097184 | tf_op jit(solution)/shard_map/ppermute | solution.py:444
  1261.1 20.5 %collective-permute-done.61 = bf16[512,1024]{1,0:T(8,128)(2,1)} collective-permute-done((bf16[512,1024]{1,0:T(8,128)(2,1)}, bf16[512,1024]{1,0:T(8,128)(2,1)}, u32[]{:S(2)}, u32[]{:S(2)}) %collective-permute-start.61) | collective-permute-done | bytes 1048608 | tf_op jit(solution)/shard_map/ppermute | solution.py:448
  (803 shorter events, 916.2 us)
Async XLA Ops:
  7.2 1381.1 %all-gather.21.cloned.1.call-start = ((), (), s32[]{:S(2)}) async-start(), calls=%async_computation.2 | async-start | bytes 1114112 | tf_op jit(solution)/shard_map/all_gather | solution.py:574
  12.5 88.3 %collective-permute-start = (bf16[512,1024]{0,1:T(8,128)(2,1)}, bf16[512,1024]{0,1:T(8,128)(2,1)}, u32[]{:S(2)}, u32[]{:S(2)}) collective-permute-start(bf16[512,1024]{0,1:T(8,128)(2,1)} %bitcast.1), channel_id=1, source_target_pairs={{0,1},{1,0},{2,3},{3,2},{4,5},{5,4},{6,7},{7,6},{8,9},{9,8},{10,11... | collective-permute-start | bytes 3145736 | tf_op jit(solution)/shard_map/ppermute | solution.py:444
  31.7 78.4 %collective-permute-start.1 = (bf16[512,768]{0,1:T(8,128)(2,1)}, bf16[512,768]{0,1:T(8,128)(2,1)}, u32[]{:S(2)}, u32[]{:S(2)}) collective-permute-start(bf16[512,768]{0,1:T(8,128)(2,1)} %constant_dynamic-slice_fusion.39), channel_id=1, source_target_pairs={{0,1},{1,0},{2,3},{3,2},{4,5},{5,4},{6,7},{7,6},{8,9},{9,8},{10,11... | collective-permute-start | bytes 2359304 | tf_op jit(solution)/shard_map/ppermute | solution.py:444
  45.0 131.2 %collective-permute-start.7 = (bf16[512,1024]{1,0:T(8,128)(2,1)}, bf16[512,1024]{1,0:T(8,128)(2,1)}, u32[]{:S(2)}, u32[]{:S(2)}) collective-permute-start(bf16[512,1024]{1,0:T(8,128)(2,1)} %dynamic-slice_bitcast_fusion.3), channel_id=1, source_target_pairs={{0,1},{1,0},{2,3},{3,2},{4,5},{5,4},{6,7},{7,6},{8,9},{9,8},{10,11... | collective-permute-start | bytes 3145736 | tf_op jit(solution)/shard_map/ppermute | solution.py:444
  89.5 87.3 %collective-permute-start.9 = (bf16[512,1024]{1,0:T(8,128)(2,1)}, bf16[512,1024]{1,0:T(8,128)(2,1)}, u32[]{:S(2)}, u32[]{:S(2)}) collective-permute-start(bf16[512,1024]{1,0:T(8,128)(2,1)} %dynamic-slice_bitcast_fusion.2), channel_id=1, source_target_pairs={{0,1},{1,0},{2,3},{3,2},{4,5},{5,4},{6,7},{7,6},{8,9},{9,8},{10,11... | collective-permute-start | bytes 3145736 | tf_op jit(solution)/shard_map/ppermute | solution.py:444
  98.3 76.3 %collective-permute-start.13 = (bf16[512,768]{0,1:T(8,128)(2,1)}, bf16[512,768]{0,1:T(8,128)(2,1)}, u32[]{:S(2)}, u32[]{:S(2)}) collective-permute-start(bf16[512,768]{0,1:T(8,128)(2,1)} %constant_dynamic-slice_fusion.36), channel_id=1, source_target_pairs={{0,1},{1,0},{2,3},{3,2},{4,5},{5,4},{6,7},{7,6},{8,9},{9,8},{10,11... | collective-permute-start | bytes 2359304 | tf_op jit(solution)/shard_map/ppermute | solution.py:444
  110.1 80.0 %collective-permute-start.19 = (bf16[512,1024]{1,0:T(8,128)(2,1)}, bf16[512,1024]{1,0:T(8,128)(2,1)}, u32[]{:S(2)}, u32[]{:S(2)}) collective-permute-start(bf16[512,1024]{1,0:T(8,128)(2,1)} %dynamic-slice_bitcast_fusion.1), channel_id=1, source_target_pairs={{0,1},{1,0},{2,3},{3,2},{4,5},{5,4},{6,7},{7,6},{8,9},{9,8},{10,11... | collective-permute-start | bytes 3145736 | tf_op jit(solution)/shard_map/ppermute | solution.py:444
  190.1 103.4 %collective-permute-start.6 = (bf16[256,1024]{1,0:T(8,128)(2,1)}, bf16[256,1024]{1,0:T(8,128)(2,1)}, u32[]{:S(2)}, u32[]{:S(2)}) collective-permute-start(bf16[256,1024]{1,0:T(8,128)(2,1)} %pad_maximum_fusion.8), channel_id=1, source_target_pairs={{0,2},{2,0},{4,6},{6,4},{8,10},{10,8},{12,14},{14,12},{16,18},{18,... | collective-permute-start | bytes 1572872 | tf_op jit(solution)/shard_map/ppermute | solution.py:448
  200.6 80.6 %collective-permute-start.22 = (bf16[512,1024]{1,0:T(8,128)(2,1)S(1)}, bf16[512,1024]{1,0:T(8,128)(2,1)S(1)}, u32[]{:S(2)}, u32[]{:S(2)}) collective-permute-start(bf16[512,1024]{1,0:T(8,128)(2,1)S(1)} %collective-permute-done.21), channel_id=1, source_target_pairs={{0,4},{2,6},{4,0},{6,2},{8,12},{10,14},{12,8},{14,10},{16,20},{18,... | collective-permute-start | bytes 3145736 | tf_op jit(solution)/shard_map/ppermute | solution.py:448
  241.9 152.6 %collective-permute-start.18 = (bf16[256,1024]{1,0:T(8,128)(2,1)}, bf16[256,1024]{1,0:T(8,128)(2,1)}, u32[]{:S(2)}, u32[]{:S(2)}) collective-permute-start(bf16[256,1024]{1,0:T(8,128)(2,1)} %pad_maximum_fusion.9), channel_id=1, source_target_pairs={{0,2},{2,0},{4,6},{6,4},{8,10},{10,8},{12,14},{14,12},{16,18},{18,... | collective-permute-start | bytes 1572872 | tf_op jit(solution)/shard_map/ppermute | solution.py:448
  264.4 115.5 %collective-permute-start.17 = (bf16[1024,768]{0,1:T(8,128)(2,1)}, bf16[1024,768]{0,1:T(8,128)(2,1)}, u32[]{:S(2)}, u32[]{:S(2)}) collective-permute-start(bf16[1024,768]{0,1:T(8,128)(2,1)} %pad_maximum_fusion.7), channel_id=1, source_target_pairs={{0,2},{2,0},{4,6},{6,4},{8,10},{10,8},{12,14},{14,12},{16,18},{18,... | collective-permute-start | bytes 4718600 | tf_op jit(solution)/shard_map/ppermute | solution.py:448
  293.5 133.7 %collective-permute-start.23 = (bf16[1024,1024]{1,0:T(8,128)(2,1)}, bf16[1024,1024]{1,0:T(8,128)(2,1)}, u32[]{:S(2)}, u32[]{:S(2)}) collective-permute-start(bf16[1024,1024]{1,0:T(8,128)(2,1)} %pad_maximum_fusion.3), channel_id=1, source_target_pairs={{0,2},{2,0},{4,6},{6,4},{8,10},{10,8},{12,14},{14,12},{16,18},{18,... | collective-permute-start | bytes 6291464 | tf_op jit(solution)/shard_map/ppermute | solution.py:448
  321.5 122.7 %collective-permute-start.24 = (bf16[1024,1024]{1,0:T(8,128)(2,1)}, bf16[1024,1024]{1,0:T(8,128)(2,1)}, u32[]{:S(2)}, u32[]{:S(2)}) collective-permute-start(bf16[1024,1024]{1,0:T(8,128)(2,1)} %pad_maximum_fusion.4), channel_id=1, source_target_pairs={{0,2},{2,0},{4,6},{6,4},{8,10},{10,8},{12,14},{14,12},{16,18},{18,... | collective-permute-start | bytes 6291464 | tf_op jit(solution)/shard_map/ppermute | solution.py:448
  612.0 82.4 %collective-permute-start.40 = (bf16[256,1024]{1,0:T(8,128)(2,1)}, bf16[256,1024]{1,0:T(8,128)(2,1)}, u32[]{:S(2)}, u32[]{:S(2)}) collective-permute-start(bf16[256,1024]{1,0:T(8,128)(2,1)} %constant_dynamic-slice_fusion.23), channel_id=1, source_target_pairs={{0,2},{2,0},{4,6},{6,4},{8,10},{10,8},{12,14},{14,12},{16,18},{18,... | collective-permute-start | bytes 1572872 | tf_op jit(solution)/shard_map/ppermute | solution.py:448
  613.4 83.5 %collective-permute-start.46 = (bf16[256,1024]{1,0:T(8,128)(2,1)}, bf16[256,1024]{1,0:T(8,128)(2,1)}, u32[]{:S(2)}, u32[]{:S(2)}) collective-permute-start(bf16[256,1024]{1,0:T(8,128)(2,1)} %constant_dynamic-slice_fusion.19), channel_id=1, source_target_pairs={{0,2},{2,0},{4,6},{6,4},{8,10},{10,8},{12,14},{14,12},{16,18},{18,... | collective-permute-start | bytes 1572872 | tf_op jit(solution)/shard_map/ppermute | solution.py:448
  630.9 76.4 %collective-permute-start.29 = (bf16[1024,768]{1,0:T(8,128)(2,1)}, bf16[1024,768]{1,0:T(8,128)(2,1)}, u32[]{:S(2)}, u32[]{:S(2)}) collective-permute-start(bf16[1024,768]{1,0:T(8,128)(2,1)} %convolution_convert_fusion.14), channel_id=1, source_target_pairs={{0,2},{2,0},{4,6},{6,4},{8,10},{10,8},{12,14},{14,12},{16,18},{18,... | collective-permute-start | bytes 4718600 | tf_op jit(solution)/shard_map/ppermute | solution.py:448
  719.3 670.4 %all-gather.23.cloned.1.call-start = ((), (), s32[]{:S(2)}) async-start(), calls=%async_computation.3 | async-start | bytes 1114112 | tf_op jit(solution)/shard_map/all_gather | solution.py:574
  757.1 636.2 %all-gather.17.cloned.1.call-start = ((), (), s32[]{:S(2)}) async-start(), calls=%async_computation | async-start | bytes 3342336 | tf_op jit(solution)/shard_map/all_gather | solution.py:574
  801.5 614.6 %all-gather.19.cloned.1.call-start = ((), (), s32[]{:S(2)}) async-start(), calls=%async_computation.1 | async-start | bytes 3342336 | tf_op jit(solution)/shard_map/all_gather | solution.py:574
  881.2 570.3 %all-gather.29.cloned.1.call-start = ((), (), s32[]{:S(2)}) async-start(), calls=%async_computation.6 | async-start | bytes 4456448 | tf_op jit(solution)/shard_map/all_gather | solution.py:574
  975.5 480.8 %all-gather.31.cloned.1.call-start = ((), (), s32[]{:S(2)}) async-start(), calls=%async_computation.7 | async-start | bytes 4456448 | tf_op jit(solution)/shard_map/all_gather | solution.py:574
  1086.4 374.7 %all-gather.25.cloned.1.call-start = ((), (), s32[]{:S(2)}) async-start(), calls=%async_computation.4 | async-start | bytes 4456448 | tf_op jit(solution)/shard_map/all_gather | solution.py:574
  1194.5 282.9 %all-gather.27.cloned.1.call-start = ((), (), s32[]{:S(2)}) async-start(), calls=%async_computation.5 | async-start | bytes 4456448 | tf_op jit(solution)/shard_map/all_gather | solution.py:574
  1259.5 77.0 %collective-permute-start.81 = (f32[28,1024]{1,0:T(8,128)}, f32[28,1024]{1,0:T(8,128)}, u32[]{:S(2)}, u32[]{:S(2)}) collective-permute-start(f32[28,1024]{1,0:T(8,128)} %pad_maximum_fusion.10), channel_id=1, source_target_pairs={{0,1},{1,0},{2,3},{3,2},{4,5},{5,4},{6,7},{7,6},{8,9},{9,8},{10,11... | collective-permute-start | bytes 344072 | tf_op jit(solution)/shard_map/ppermute | solution.py:444
  (244 other events, 6002.7 us)
Sparse Core Ops, SparseCore 0:
  719.4 36.3 all-gather.20
  757.9 41.9 all-gather.22
  802.3 50.7 all-gather.16
  881.4 44.4 all-gather.18
  975.7 49.2 all-gather.28
  1086.5 49.3 all-gather.30
  1194.6 49.7 all-gather.24
  1307.1 54.8 all-gather.26

commit v2 on v1

--- a/solution.py
+++ b/solution.py
@@ -375,9 +375,10 @@
             block(pl.multiple_of(i*bq,bq),length); return c
         lax.fori_loop(0,nq,body,0)
 
-def attn_fwd(qkv, lims, causal, bq=256):
+def attn_fwd(qkv, lims, group, causal, bq=256):
     length=qkv.shape[0]; width=qkv.shape[1]//3; pairs=width//128
-    spec=lambda off: pl.BlockSpec((length,128),lambda i,off=off:(0,off*pairs+i))
+    per=group//128
+    spec=lambda off: pl.BlockSpec((length,128),lambda i,off=off:(0,(i//per)*3*per+off*per+i%per))
     return pl.pallas_call(partial(fwd_kernel,causal,bq),
         grid=(pairs,),
         in_specs=[pl.BlockSpec(memory_space=pltpu.SMEM),spec(0),spec(1),spec(2)],
@@ -388,12 +389,13 @@
         name="attn_fwd_"+("causal" if causal else "full"),
     )(lims,qkv,qkv,qkv)
 
-def bwd_kernel(causal,bq,lims_ref,q_ref,k_ref,v_ref,l_ref,do_ref,grad_ref,dk_acc,dv_acc):
+def bwd_kernel(causal,bq,group,lims_ref,q_ref,k_ref,v_ref,l_ref,do_ref,grad_ref,dk_acc,dv_acc):
     length=q_ref.shape[0]
     lane=lax.broadcasted_iota(jnp.int32,(bq,128),1)
     dk_acc[...]=jnp.zeros_like(dk_acc); dv_acc[...]=jnp.zeros_like(dv_acc)
-    width=grad_ref.shape[1]//3
-    at=[pl.multiple_of(part*width+pl.program_id(0)*128,128) for part in range(3)]
+    per=group//128
+    pair=pl.program_id(0)
+    at=[pl.multiple_of((lax.div(pair,per)*3*per+part*per+lax.rem(pair,per))*128,128) for part in range(3)]
     def block(start,kk):
         q=q_ref[pl.ds(start,bq),:]*jnp.asarray(0.125,bf16)
         do=do_ref[pl.ds(start,bq),:]
@@ -424,11 +426,12 @@
     grad_ref[:,pl.ds(at[1],128)]=dk_acc[...].astype(bf16)
     grad_ref[:,pl.ds(at[2],128)]=dv_acc[...].astype(bf16)
 
-def attn_bwd(qkv,L,do,lims,causal,bq=256):
+def attn_bwd(qkv,L,do,lims,group,causal,bq=256):
     length=qkv.shape[0]; width=qkv.shape[1]//3; pairs=width//128
-    spec=lambda off: pl.BlockSpec((length,128),lambda i,off=off:(0,off*pairs+i))
+    per=group//128
+    spec=lambda off: pl.BlockSpec((length,128),lambda i,off=off:(0,(i//per)*3*per+off*per+i%per))
     one=pl.BlockSpec((length,128),lambda i:(0,i))
-    return pl.pallas_call(partial(bwd_kernel,causal,bq),
+    return pl.pallas_call(partial(bwd_kernel,causal,bq,group),
         grid=(pairs,),
         in_specs=[pl.BlockSpec(memory_space=pltpu.SMEM),spec(0),spec(1),spec(2),pl.BlockSpec((1,2,length),lambda i:(i,0,0)),one],
         out_specs=pl.BlockSpec((length,3*width),lambda i:(0,0)),
@@ -440,6 +443,10 @@
     )(lims,qkv,qkv,qkv,L,do)
 
 
+def pin(*values):
+    return lax.optimization_barrier(values)
+
+
 def swap_tensor(block):
     return lax.ppermute(block, "tensor", [(0, 1), (1, 0)])
 
@@ -497,16 +504,17 @@
     return total
 
 
+def dot_low(left, right, dims):
+    return lax.dot_general(left, right, dims, preferred_element_type=f32).astype(bf16)
+
+
 NN = (((1,), (0,)), ((), ()))
+SPLIT_AXIS = {"qkv": 1, "out": 0, "up": 1, "down": 0}
+PACK_WIDTH = 512
 
 
 def quarter_of(kind, half, place):
-    if kind == "qkv":
-        heads = half.reshape(half.shape[0], 3, -1)
-        width = heads.shape[2] // 2
-        picked = lax.dynamic_slice_in_dim(heads, place * width, width, 2)
-        return picked.reshape(half.shape[0], 3 * width)
-    axis = 1 if kind == "up" else 0
+    axis = SPLIT_AXIS[kind]
     width = half.shape[axis] // 2
     return lax.dynamic_slice_in_dim(half, place * width, width, axis)
 
@@ -514,6 +522,144 @@
 def row_half(block, place):
     height = block.shape[0] // 2
     return lax.dynamic_slice_in_dim(block, place * height, height, 0)
+
+
+def pack_piece(half, place, dp_size):
+    height = half.shape[0] // dp_size
+    piece = lax.dynamic_slice_in_dim(half, place * height, height, 0)
+    return [
+        lax.slice_in_dim(piece, at, at + PACK_WIDTH, axis=1)
+        for at in range(0, half.shape[1], PACK_WIDTH)
+    ]
+
+
+def unpack_halves(gathered, shapes):
+    dp_size = gathered.shape[0]
+    halves, at = [], 0
+    for height, width in shapes:
+        rows = height // dp_size
+        count = width // PACK_WIDTH
+        part = lax.slice_in_dim(gathered, at, at + rows * count, axis=1)
+        part = part.reshape(dp_size, count, rows, PACK_WIDTH).transpose(0, 2, 1, 3)
+        halves.append(part.reshape(height, width))
+        at += rows * count
+    return halves
+
+
+def place_kernel(kind, whole_ref, *refs):
+    out_ref = refs[-1]
+    block = whole_ref[0].astype(f32)
+    if kind == "qkv":
+        width = block.shape[1] // 3
+        for part in range(3):
+            out_ref[0, :, part, :] = block[:, part * width : (part + 1) * width]
+    else:
+        out_ref[0] = block
+
+
+def place_grad(kind, whole, layer, base):
+    dp_size, rows, columns = whole.shape
+    bit_count = dp_size.bit_length() - 1
+
+    def source(step):
+        group, core = (step // (dp_size // 2), 0)
+        block = step % (dp_size // 2)
+        index = group
+        for bit in range(1, bit_count):
+            index = index + ((block >> (bit_count - 1 - bit)) & 1) * (1 << bit)
+        return index
+
+    half = dp_size // 2
+    if kind in ("out", "down"):
+        out_shape = (2, dp_size * rows, columns)
+        out_spec = pl.BlockSpec((1, rows, columns), lambda step: (layer, step, 0))
+    elif kind == "up":
+        out_shape = (2, half * rows, 2 * columns)
+        out_spec = pl.BlockSpec((1, rows, columns), lambda step: (layer, step % half, step // half))
+    else:
+        out_shape = (2, half * rows, 3, 2 * columns // 3)
+        out_spec = pl.BlockSpec(
+            (1, rows, 3, columns // 3), lambda step: (layer, step % half, 0, step // half)
+        )
+    operands, in_specs, aliases = [whole], [pl.BlockSpec((1, rows, columns), lambda step: (source(step), 0, 0))], {}
+    if base is not None:
+        operands.append(base)
+        in_specs.append(pl.BlockSpec(memory_space=pl.ANY))
+        aliases = {1: 0}
+    return pl.pallas_call(
+        partial(place_kernel, kind),
+        grid=(dp_size,),
+        in_specs=in_specs,
+        out_specs=out_spec,
+        out_shape=jax.ShapeDtypeStruct(out_shape, f32),
+        input_output_aliases=aliases,
+        cost_estimate=pl.CostEstimate(flops=0, bytes_accessed=6 * dp_size * rows * columns, transcendentals=0),
+        name="place_" + kind,
+    )(*operands)
+
+
+def frame_kernel(side_ref, mine_ref, other_ref, out_ref):
+    own = pl.program_id(0) == side_ref[0]
+    out_ref[0, 0] = jnp.where(own, mine_ref[...], other_ref[...].astype(f32))
+
+
+def place_frames(side, mine, other):
+    height, width = mine.shape
+    rows = height // 2
+    spec = pl.BlockSpec((rows, width), lambda slot, step, side_ref: (step, 0))
+    return pl.pallas_call(
+        frame_kernel,
+        grid_spec=pltpu.PrefetchScalarGridSpec(
+            num_scalar_prefetch=1,
+            grid=(2, 2),
+            in_specs=[spec, spec],
+            out_specs=pl.BlockSpec((1, 1, rows, width), lambda slot, step, side_ref: (slot, 0, step, 0)),
+        ),
+        out_shape=jax.ShapeDtypeStruct((2, 1, height, width), f32),
+        name="place_frames",
+    )(side.reshape(1).astype(jnp.int32), mine, other)
+
+
+class Chain:
+    def __init__(self, kind, layer, own, near, far, place, dp_size):
+        self.kind, self.layer, self.place, self.dp_size = kind, layer, place, dp_size
+        self.bit_count = dp_size.bit_length() - 1
+        core = place & 1
+        self.near = near
+        self.kept = quarter_of(kind, own, core)
+        self.flight = [
+            swap_bit(far, 0, dp_size),
+            swap_bit(quarter_of(kind, own, 1 - core), 0, dp_size),
+        ]
+        self.stage = "core"
+
+    def bit(self, index):
+        return (self.place >> index) & 1
+
+    def advance(self, arrived):
+        if self.stage == "core":
+            near_there, own_there = arrived
+            self.kept = self.kept.astype(f32) + own_there.astype(f32)
+            self.flight = [swap_tensor(add_rounded(self.near, near_there))]
+            self.near = None
+            self.stage = 0
+            return
+        total = (self.kept.astype(f32) + arrived[0].astype(f32)).astype(bf16)
+        self.stage += 1
+        if self.stage < self.bit_count:
+            bit = self.bit(self.stage)
+            self.kept = row_half(total, bit)
+            self.flight = [swap_bit(row_half(total, 1 - bit), self.stage, self.dp_size)]
+        else:
+            self.flight = []
+            self.whole = lax.all_gather(total, "dp", axis=0, tiled=False)
+
+
+def move(state, *chains):
+    state, flights = pin(state, [chain.flight for chain in chains])
+    for chain, flight in zip(chains, flights):
+        chain.advance(flight)
+    return state
 
 
 def paired_device(
@@ -537,55 +683,15 @@
     side = lax.axis_index("tensor")
     place = lax.axis_index("dp")
     bit_count = dp_size.bit_length() - 1
-    bits = [(place >> bit) & 1 for bit in range(bit_count)]
-    core = bits[0]
-
-    def whole_rows(halves):
+    core, near_row = place & 1, (place >> 1) & 1
+    group = w_qkv.shape[3] // 2
+
+    def away_rows(halves):
+        return lax.dynamic_index_in_dim(halves[:, 0], 1 - side, 0, keepdims=False)
+
+    def whole_rows(halves, other):
         mine = lax.dynamic_index_in_dim(halves[:, 0], side, 0, keepdims=False)
-        away = lax.dynamic_index_in_dim(halves[:, 0], 1 - side, 0, keepdims=False)
-        return in_order(side, mine, swap_tensor(away))
-
-    def split_rows(rows):
-        height = rows.shape[0] // 2
-        mine = lax.dynamic_slice_in_dim(rows, side * height, height, 0)
-        away = lax.dynamic_slice_in_dim(rows, (1 - side) * height, height, 0)
-        other = swap_tensor(away.astype(bf16)).astype(f32)
-        first = jnp.where(side == 0, mine, other)
-        second = jnp.where(side == 0, other, mine)
-        return jnp.stack([first, second])[:, None]
-
-    def other_half(kind, half):
-        piece = row_half(quarter_of(kind, half, core), bits[1])
-        piece = swap_tensor(piece)
-        near = in_order(bits[1], piece, swap_bit(piece, 1, dp_size))
-        far = swap_bit(near, 0, dp_size)
-        return [half, near, far]
-
-    def reduce_grad(kind, grads):
-        own, near, far = grads
-        own_there = swap_bit(quarter_of(kind, own, 1 - core), 0, dp_size)
-        near_there = swap_bit(far, 0, dp_size)
-        across = swap_tensor(add_rounded(near, near_there))
-        total = quarter_of(kind, own, core).astype(f32) + own_there.astype(f32) + across.astype(f32)
-        total = total.astype(bf16)
-        for bit in range(1, bit_count):
-            sent = swap_bit(row_half(total, 1 - bits[bit]), bit, dp_size)
-            total = add_rounded(row_half(total, bits[bit]), sent)
-        whole = lax.all_gather(total, "dp", axis=0, tiled=False)
-        rows, columns = total.shape
-        whole = whole.reshape((2,) * bit_count + (rows, columns))
-        order = tuple(bit_count - 1 - bit for bit in range(1, bit_count))
-        core_axis = bit_count - 1
-        full_rows = rows * 2 ** (bit_count - 1)
-        if kind in ("out", "down"):
-            whole = whole.transpose((core_axis,) + order + (bit_count, bit_count + 1))
-            return whole.reshape(2 * full_rows, columns)
-        if kind == "up":
-            whole = whole.transpose(order + (bit_count, core_axis, bit_count + 1))
-            return whole.reshape(full_rows, 2 * columns)
-        whole = whole.reshape((2,) * bit_count + (rows, 3, columns // 3))
-        whole = whole.transpose(order + (bit_count, bit_count + 1, core_axis, bit_count + 2))
-        return whole.reshape(full_rows, 3, 2 * columns // 3)
+        return in_order(side, mine, other)
 
     prefix = lax.dynamic_index_in_dim(phone_len[:, 0], side, 0, keepdims=False)
     frames = lax.dynamic_index_in_dim(frame_len[:, 0], side, 0, keepdims=False)
@@ -602,97 +708,195 @@
         [jnp.sum(picker * ada_shift[part], axis=0) for part in range(2)],
     ]
 
-    rows = whole_rows(frames_in).astype(f32)
-    weights = []
-    for layer in range(2):
-        weights.append(
-            {
-                "qkv": other_half("qkv", w_qkv[layer].reshape(model_width, -1)),
-                "out": other_half("out", w_out[layer]),
-                "up": other_half("up", w_up[layer]),
-                "down": other_half("down", w_down[layer]),
-            }
-        )
-    kept = []
-    for layer in range(2):
-        causal = layer == 0
-        mats = weights[layer]
-        normed, norm_kept = norm_forward(rows, gains[layer][0], shifts[layer][0])
-        projected = [
-            jnp.dot(normed, part, preferred_element_type=f32).astype(bf16) for part in mats["qkv"]
-        ]
-        mixed = [attn_fwd(part, limits, causal, 512) for part in projected]
-        rows = rows + dot_sum([(mix[0], part) for mix, part in zip(mixed, mats["out"])], NN)
-        kept.append((normed, norm_kept, projected, mixed))
-        normed, norm_kept = norm_forward(rows, gains[layer][1], shifts[layer][1])
-        pairs = [gelu_pair(jnp.dot(normed, part, preferred_element_type=f32)) for part in mats["up"]]
-        rows = rows + dot_sum([(pair[0], part) for pair, part in zip(pairs, mats["down"])], NN)
-        kept.append((normed, norm_kept, pairs))
-    frames_out = split_rows(rows)
-
-    grad_rows = whole_rows(out_grad).astype(f32)
-    sums = {}
+    def flat_qkv(layer):
+        split = w_qkv[layer].reshape(model_width, 3, 2, group).transpose(0, 2, 1, 3)
+        return split.reshape(model_width, 6 * group)
+
+    own = [
+        {"qkv": flat_qkv(layer), "out": w_out[layer], "up": w_up[layer], "down": w_down[layer]}
+        for layer in range(2)
+    ]
+
+    def packed(layer, kinds):
+        pieces = []
+        for kind in kinds:
+            pieces += pack_piece(own[layer][kind], place, dp_size)
+        return jnp.concatenate(pieces, axis=0)
+
+    def gathered(arrived, layer, kinds):
+        whole = lax.all_gather(arrived, "dp", axis=0, tiled=False)
+        return dict(zip(kinds, unpack_halves(whole, [own[layer][kind].shape for kind in kinds])))
+
+    attn_kinds, all_kinds = ("qkv", "out"), ("qkv", "out", "up", "down")
+    first_pack = swap_tensor(packed(0, attn_kinds))
+    other_rows = swap_tensor(away_rows(frames_in))
+    first = gathered(first_pack, 0, attn_kinds)
+    second_send = packed(1, all_kinds)
+    up_send = row_half(quarter_of("up", own[0]["up"], core), near_row)
+    down_send = row_half(quarter_of("down", own[0]["down"], core), near_row)
+    other_rows, second_send, up_send, down_send = pin(other_rows, second_send, up_send, down_send)
+    second_pack = swap_tensor(second_send)
+    rows = whole_rows(frames_in, other_rows).astype(f32)
+    normed, norm_kept = norm_forward(rows, gains[0][0], shifts[0][0])
+    mine = dot_low(normed, own[0]["qkv"], NN)
+    mine, second_pack, up_send, down_send = pin(mine, second_pack, up_send, down_send)
+    second = gathered(second_pack, 1, all_kinds)
+    up_piece = swap_tensor(up_send)
+    mix_mine = attn_fwd(mine, limits, group, True, 512)
+    mix_mine, up_piece, down_send = pin(mix_mine, up_piece, down_send)
+    down_piece = swap_tensor(down_send)
+    up_there = swap_bit(up_piece, 1, dp_size)
+    theirs = dot_low(normed, first["qkv"], NN)
+    mix_theirs = attn_fwd(theirs, limits, group, True, 512)
+    mix_theirs, up_there, down_piece = pin(mix_theirs, up_there, down_piece)
+    up_near = in_order(near_row, up_piece, up_there)
+    up_far = swap_bit(up_near, 0, dp_size)
+    down_there = swap_bit(down_piece, 1, dp_size)
+    kept = [(normed, norm_kept, [mine, theirs], [mix_mine, mix_theirs])]
+    rows = rows + dot_sum([(mix_mine[0], own[0]["out"]), (mix_theirs[0], first["out"])], NN)
+    normed, norm_kept = norm_forward(rows, gains[0][1], shifts[0][1])
+    pair_own = gelu_pair(jnp.dot(normed, own[0]["up"], preferred_element_type=f32))
+    pair_own, up_far, normed = pin(pair_own, up_far, normed)
+    pair_near = gelu_pair(jnp.dot(normed, up_near, preferred_element_type=f32))
+    pair_far = gelu_pair(jnp.dot(normed, up_far, preferred_element_type=f32))
+    rows = rows + dot_sum([(pair_own[0], own[0]["down"])], NN)
+    rows, pair_near, pair_far, down_there = pin(rows, pair_near, pair_far, down_there)
+    down_near = in_order(near_row, down_piece, down_there)
+    down_far = swap_bit(down_near, 0, dp_size)
+    grad_send = away_rows(out_grad)
+    down_near, grad_send = pin(down_near, grad_send)
+    grad_other = swap_tensor(grad_send)
+    rows = rows + dot_sum([(pair_near[0], down_near), (pair_far[0], down_far)], NN)
+    kept.append((normed, norm_kept, [pair_own, pair_near, pair_far]))
+    weights = [
+        {
+            "qkv": [own[0]["qkv"], first["qkv"]],
+            "out": [own[0]["out"], first["out"]],
+            "up": [own[0]["up"], up_near, up_far],
+            "down": [own[0]["down"], down_near, down_far],
+        },
+        {kind: [own[1][kind], second[kind]] for kind in all_kinds},
+    ]
+
+    normed, norm_kept = norm_forward(rows, gains[1][0], shifts[1][0])
+    projected = [dot_low(normed, part, NN) for part in weights[1]["qkv"]]
+    mixed = [attn_fwd(part, limits, group, False, 512) for part in projected]
+    rows = rows + dot_sum([(mix[0], part) for mix, part in zip(mixed, weights[1]["out"])], NN)
+    kept.append((normed, norm_kept, projected, mixed))
+    normed, norm_kept = norm_forward(rows, gains[1][1], shifts[1][1])
+    pairs = [gelu_pair(jnp.dot(normed, part, preferred_element_type=f32)) for part in weights[1]["up"]]
+    rows = rows + dot_sum([(pair[0], part) for pair, part in zip(pairs, weights[1]["down"])], NN)
+    kept.append((normed, norm_kept, pairs))
+    rows, grad_other = pin(rows, grad_other)
+
+    def halves_of(block):
+        height = block.shape[0] // 2
+        mine = lax.dynamic_slice_in_dim(block, side * height, height, 0)
+        away = lax.dynamic_slice_in_dim(block, (1 - side) * height, height, 0)
+        return mine, away.astype(bf16)
+
+    out_mine, out_away = halves_of(rows)
+
     norm_sums = [[None, None], [None, None]]
-    for layer in (1, 0):
-        causal = layer == 0
-        mats = weights[layer]
-        normed, norm_kept, pairs = kept[2 * layer + 1]
-        low = grad_rows.astype(bf16)
-        grad_hidden = [
+    grad_rows = whole_rows(out_grad, grad_other).astype(f32)
+
+    def chain(kind, layer, parts):
+        if len(parts) == 2:
+            near, far = (quarter_of(kind, parts[1], core), quarter_of(kind, parts[1], 1 - core))
+        else:
+            near, far = parts[1:]
+        return Chain(kind, layer, parts[0], near, far, place, dp_size)
+
+    def hidden_grads(layer, low):
+        pairs = kept[2 * layer + 1][2]
+        return [
             (
                 lax.dot_general(low, part, NT, preferred_element_type=f32) * pair[1].astype(f32)
             ).astype(bf16)
-            for pair, part in zip(pairs, mats["down"])
+            for pair, part in zip(pairs, weights[layer]["down"])
         ]
-        sums["down", layer] = reduce_grad(
-            "down",
-            [
-                lax.dot_general(pair[0], low, TN, preferred_element_type=f32).astype(bf16)
-                for pair in pairs
-            ],
+
+    def down_grads(layer, low):
+        return [dot_low(pair[0], low, TN) for pair in kept[2 * layer + 1][2]]
+
+    def up_grads(layer, hidden):
+        return [dot_low(kept[2 * layer + 1][0], part, TN) for part in hidden]
+
+    def out_grads(layer, low):
+        return [dot_low(mix[0], low, TN) for mix in kept[2 * layer][3]]
+
+    def mixed_grads(layer, low):
+        return [dot_low(low, part, NT) for part in weights[layer]["out"]]
+
+    def attention_grad(layer, part, grad_mix):
+        _, _, projected, mixed = kept[2 * layer]
+        return attn_bwd(projected[part], mixed[part][1], grad_mix, limits, group, layer == 0, 512)
+
+    def norm_step(layer, part, grad_rows, grad_normed):
+        added, grad_gain, grad_shift = norm_backward(
+            kept[2 * layer + part][1], grad_normed, gains[layer][part]
         )
-        sums["up", layer] = reduce_grad(
-            "up",
-            [
-                lax.dot_general(normed, part, TN, preferred_element_type=f32).astype(bf16)
-                for part in grad_hidden
-            ],
-        )
-        grad_normed = dot_sum(list(zip(grad_hidden, mats["up"])), NT)
-        added, grad_gain, grad_shift = norm_backward(norm_kept, grad_normed, gains[layer][1])
-        norm_sums[layer][1] = (grad_gain, grad_shift)
-        grad_rows = grad_rows + added
-
-        normed, norm_kept, projected, mixed = kept[2 * layer]
-        low = grad_rows.astype(bf16)
-        sums["out", layer] = reduce_grad(
-            "out",
-            [
-                lax.dot_general(mix[0], low, TN, preferred_element_type=f32).astype(bf16)
-                for mix in mixed
-            ],
-        )
-        grad_mixed = [
-            lax.dot_general(low, part, NT, preferred_element_type=f32).astype(bf16)
-            for part in mats["out"]
-        ]
-        grad_projected = [
-            attn_bwd(part, mix[1], grad_mix, limits, causal, 512)
-            for part, mix, grad_mix in zip(projected, mixed, grad_mixed)
-        ]
-        sums["qkv", layer] = reduce_grad(
-            "qkv",
-            [
-                lax.dot_general(normed, part, TN, preferred_element_type=f32).astype(bf16)
-                for part in grad_projected
-            ],
-        )
-        grad_normed = dot_sum(list(zip(grad_projected, mats["qkv"])), NT)
-        added, grad_gain, grad_shift = norm_backward(norm_kept, grad_normed, gains[layer][0])
-        norm_sums[layer][0] = (grad_gain, grad_shift)
-        grad_rows = grad_rows + added
-
-    frames_grad = split_rows(grad_rows)
+        norm_sums[layer][part] = (grad_gain, grad_shift)
+        return grad_rows + added
+
+    low = grad_rows.astype(bf16)
+    parts = down_grads(1, low)
+    hidden = hidden_grads(1, low)
+    parts, hidden, grad_rows = pin(parts, hidden, grad_rows)
+    down1 = chain("down", 1, parts)
+    parts = up_grads(1, hidden)
+    grad_normed = dot_sum(list(zip(hidden, weights[1]["up"])), NT)
+    parts, grad_normed = move((parts, grad_normed), down1)
+    up1 = chain("up", 1, parts)
+    grad_rows = norm_step(1, 1, grad_rows, grad_normed)
+    low = grad_rows.astype(bf16)
+    parts = out_grads(1, low)
+    mine, theirs = mixed_grads(1, low)
+    theirs = attention_grad(1, 1, theirs)
+    parts, mine, theirs, grad_rows = move((parts, mine, theirs, grad_rows), down1, up1)
+    out1 = chain("out", 1, parts)
+    mine = attention_grad(1, 0, mine)
+    mine, theirs = move((mine, theirs), down1, out1)
+    parts = [dot_low(kept[2][0], part, TN) for part in (mine, theirs)]
+    grad_normed = dot_sum(list(zip((mine, theirs), weights[1]["qkv"])), NT)
+    parts, grad_normed = move((parts, grad_normed), down1, up1)
+    qkv1 = chain("qkv", 1, parts)
+    grad_rows = norm_step(1, 0, grad_rows, grad_normed)
+    low = grad_rows.astype(bf16)
+    parts = down_grads(0, low)
+    parts, low, grad_rows = move((parts, low, grad_rows), down1, out1, qkv1)
+    down0 = chain("down", 0, parts)
+    hidden = hidden_grads(0, low)
+    (hidden,) = move((hidden,), up1, out1, down0)
+    parts = up_grads(0, hidden)
+    grad_normed = dot_sum(list(zip(hidden, weights[0]["up"])), NT)
+    parts, grad_normed = move((parts, grad_normed), up1, out1, qkv1)
+    up0 = chain("up", 0, parts)
+    grad_rows = norm_step(0, 1, grad_rows, grad_normed)
+    low = grad_rows.astype(bf16)
+    out_parts = out_grads(0, low)
+    mine, theirs = mixed_grads(0, low)
+    theirs = attention_grad(0, 1, theirs)
+    out_parts, mine, theirs, grad_rows = move(
+        (out_parts, mine, theirs, grad_rows), up1, out1, qkv1, down0, up0
+    )
+    out0 = chain("out", 0, out_parts)
+    part_theirs = dot_low(kept[0][0], theirs, TN)
+    mine = attention_grad(0, 0, mine)
+    mine, theirs, part_theirs = move((mine, theirs, part_theirs), qkv1, down0, out0)
+    part_mine = dot_low(kept[0][0], mine, TN)
+    grad_normed = dot_sum([(mine, weights[0]["qkv"][0]), (theirs, weights[0]["qkv"][1])], NT)
+    part_mine, grad_normed = move((part_mine, grad_normed), up0, qkv1)
+    qkv0 = chain("qkv", 0, [part_mine, part_theirs])
+    grad_rows = norm_step(0, 0, grad_rows, grad_normed)
+    grad_mine, grad_away = halves_of(grad_rows)
+    (grad_mine, grad_away) = move((grad_mine, grad_away), qkv0, out0, down0)
+    frames_grad = place_frames(side, grad_mine, swap_tensor(grad_away))
+    move((), up0, out0, down0)
+    frames_out = place_frames(side, out_mine, swap_tensor(out_away))
+    for one in (up0, out0, down0, qkv0):
+        while one.flight:
+            one.advance(one.flight)
 
     def everywhere(block):
         block = block + swap_tensor(block)
@@ -721,16 +925,16 @@
         )
     ).reshape(4, section_count, model_width)
 
-    def both(kind):
-        return jnp.stack([sums[kind, 0].astype(f32), sums[kind, 1].astype(f32)])
+    def both(kind, later, sooner):
+        return place_grad(kind, sooner.whole, 0, place_grad(kind, later.whole, 1, None))
 
     return (
         frames_out,
         frames_grad,
-        both("qkv"),
-        both("out"),
-        both("up"),
-        both("down"),
+        both("qkv", qkv1, qkv0),
+        both("out", out1, out0),
+        both("up", up1, up0),
+        both("down", down1, down0),
         late[0:2],
         late[2:4],
         early[0:2],

time: 1530 us -> 1170 us (0.76)
  waiting for transfers between devices: 576 us -> 270 us
  Pallas kernels: 175 us -> 280 us
  local copies, waits for them, and re-layouts: 211 us -> 141 us
  matrix products: 341 us -> 283 us
  other arithmetic: 125 us -> 95.6 us
    ppermute x22 -> x18, waiting for transfers between devices: 301 us -> 93.2 us  [swap_tensor(): return lax.ppermute(block, 'tensor', [(0, 1), (1, 0)])]
    ppermute x64 -> x52, waiting for transfers between devices: 275 us -> 144 us  [swap_bit(): lax.ppermute(block, 'dp', [(place, place ^ 1 << bit) for place in range(d...]
    convert_element_type x20 -> x2, local copies, waits for them, and re-layouts: 102 us -> 2.87 us  [halves_of(): return (mine, away.astype(bf16))]
    pallas_call x6 -> x14, Pallas kernels: 108 us -> 202 us  [the longest x4 108 us: attn_bwd(): pl.pallas_call(partial(bwd_kernel, causal, bq, group), grid=(pairs,), in_...]
    dot_general x24 -> x18, matrix products: 129 us -> 87.8 us  [dot_sum(): term = lax.dot_general(left, right, dims, preferred_element_type=f32)]
    another operation x6 -> x0, other arithmetic: 34.7 us -> none  [the longest x4 30 us: both(): return jnp.stack([sums[kind, 0].astype(f32), sums[kind, 1].astype(f32)])]
    all_gather x8 -> x10, waiting for transfers between devices: 0.05 us -> 33.1 us  [the longest x8 33 us: advance(): self.whole = lax.all_gather(total, 'dp', axis=0, tiled=False)]
    transpose x0 -> x8, local copies, waits for them, and re-layouts: none -> 23.1 us  [the longest x6 19.1 us: unpack_halves(): part = part.reshape(dp_size, count, rows, PACK_WIDTH).transpose(0, 2, 1, 3)]
  transfers between devices with their start and end apart: 94 -> 80, of which waited for: 38 -> 29; matrix products, arithmetic and copies ran while one was open for 33% -> 33% of each run, Pallas kernels for 8% -> 23%
where the time goes in v2:
time: 1170 us; the launch traced here: 1160 us
  matrix products  283 us (24%)
  Pallas kernels  280 us (24%)
  waiting for transfers between devices  270 us (23%)
  local copies, waits for them, and re-layouts  141 us (12%)
  other arithmetic  95.6 us (8%)
  starting transfers between devices  69.1 us (6%)
  between operations  17.9 us (2%)
    ppermute x52, waiting for transfers between devices, swap_bit(): lax.ppermute(block, 'dp', [(place, place ^ 1 << bit) for place in range(d...  144 us
    pallas_call x4, Pallas kernels, attn_bwd(): pl.pallas_call(partial(bwd_kernel, causal, bq, group), grid=(pairs,), in_...  108 us
    dot_general x26, matrix products, dot_low(): lax.dot_general(left, right, dims, preferred_element_type=f32).astype(bf16)  105 us
    ppermute x18, waiting for transfers between devices, swap_tensor(): return lax.ppermute(block, 'tensor', [(0, 1), (1, 0)])  93.2 us
    dot_general x18, matrix products, dot_sum(): term = lax.dot_general(left, right, dims, preferred_element_type=f32)  87.8 us
    pallas_call x8, Pallas kernels, place_grad(): pl.pallas_call(partial(place_kernel, kind), grid=(dp_size,), in_specs=in_...  84.3 us
    pallas_call x4, Pallas kernels, attn_fwd(): pl.pallas_call(partial(fwd_kernel, causal, bq), grid=(pairs,), in_specs=[...  78 us
    unnamed x352, local copies, waits for them, and re-layouts  53.4 us
  transfers between devices with their start and end apart: 80, of which 29 were waited for; matrix products, arithmetic and copies ran while one was open for 33% of the time, Pallas kernels for 23%

profile of v2, /device:TPU:0, one launch (start us, length us, event | category | flops | bytes accessed | tf_op | source)
XLA Modules:
  0.0 1157.1 jit_solution(14528889145881864375)
XLA Ops:
  89.2 14.1 %attn_fwd_causal.2 = (bf16[1024,512]{1,0:T(8,128)(2,1)S(1)}, f32[4,2,1024]{2,1,0:T(2,128)S(1)}) custom-call(s32[2]{0:T(128)S(1)} %pad_add_fusion.lims_ref, bf16[1024,1536]{1,0:T(8,128)(2,1)S(1)} %copy-done.8, bf16[1024,1536]{1,0:T(8,128)(2,1)S(1)} %copy-done.8, bf16[1024,1536]{1,0:T(8,128)(2,1)S(1)} %copy-done.8), custom_call_target="tpu_custom_call" | custom-call | flops 4294967296 | bytes 4194304 | tf_op jit(solution)/shard_map/attn_fwd_causal/pallas_call | solution.py:382
  129.2 26.2 %attn_fwd_causal.3 = (bf16[1024,512]{1,0:T(8,128)(2,1)S(1)}, f32[4,2,1024]{2,1,0:T(2,128)S(1)}) custom-call(s32[2]{0:T(128)S(1)} %pad_add_fusion.lims_ref, bf16[1024,1536]{1,0:T(8,128)(2,1)S(1)} %convolution_convert_fusion.6.q_ref.k_ref.v_ref, bf16[1024,1536]{1,0:T(8,128)(2,1)S(1)} %convolution_convert_fusion.6.q_ref.k_ref.v_ref, ...), custom_call_target="tpu_custom_call" | custom-call | flops 4294967296 | bytes 4194304 | tf_op jit(solution)/shard_map/attn_fwd_causal/pallas_call | solution.py:382
  219.1 18.8 %attn_fwd_full.2 = (bf16[1024,512]{1,0:T(8,128)(2,1)S(1)}, f32[4,2,1024]{2,1,0:T(2,128)S(1)}) custom-call(s32[2]{0:T(128)S(1)} %pad_add_fusion.lims_ref, bf16[1024,1536]{1,0:T(8,128)(2,1)S(1)} %convolution_convert_fusion.5.q_ref.k_ref.v_ref, bf16[1024,1536]{1,0:T(8,128)(2,1)S(1)} %convolution_convert_fusion.5.q_ref.k_ref.v_ref, ...), custom_call_target="tpu_custom_call" | custom-call | flops 4294967296 | bytes 4194304 | tf_op jit(solution)/shard_map/attn_fwd_full/pallas_call | solution.py:382
  277.4 18.8 %attn_fwd_full.3 = (bf16[1024,512]{1,0:T(8,128)(2,1)S(1)}, f32[4,2,1024]{2,1,0:T(2,128)S(1)}) custom-call(s32[2]{0:T(128)S(1)} %pad_add_fusion.lims_ref, bf16[1024,1536]{1,0:T(8,128)(2,1)S(1)} %convolution_convert_fusion.4.q_ref.k_ref.v_ref, bf16[1024,1536]{1,0:T(8,128)(2,1)S(1)} %convolution_convert_fusion.4.q_ref.k_ref.v_ref, ...), custom_call_target="tpu_custom_call" | custom-call | flops 4294967296 | bytes 4194304 | tf_op jit(solution)/shard_map/attn_fwd_full/pallas_call | solution.py:382
  326.6 12.0 %add_add_fusion.1 = f32[1024,1024]{1,0:T(8,128)} fusion(f32[1024,1024]{1,0:T(8,128)S(1)} %get-tuple-element.361, f32[1024,1024]{1,0:T(8,128)} %fusion.15, bf16[2,2048,1024]{2,1,0:T(8,128)(2,1)S(1)} %bitcast.256, f32[1024,2048]{1,0:T(8,128)} %fusion.22), kind=kOutput, calls=%fused_computation.66 | convolution fusion | flops 4315938816 | bytes 25165824 | tf_op jit(solution)/shard_map/dot_general | solution.py:502
  341.0 16.1 %multiply_convert_fusion.1 = bf16[1024,2048]{1,0:T(8,128)(2,1)} fusion(f32[1024,2048]{1,0:T(8,128)} %fusion.99, bf16[128,8,16,128]{3,2,1,0:T(8,128)(2,1)S(1)} %bitcast.270, bf16[512,1024]{1,0:T(8,128)(2,1)S(1)} %get-tuple-element.323, bf16[512,1024]{1,0:T(8,128)(2,1)S(1)} %get-tuple-element.322), kind=kOutput, calls=%fused_computation.1 | convolution fusion | flops 4341104640 | bytes 18874368 | tf_op jit(solution)/shard_map/dot_general | solution.py:814
  368.4 13.9 %multiply_convert_fusion.2 = bf16[1024,2048]{1,0:T(8,128)(2,1)} fusion(f32[1024,2048]{1,0:T(8,128)} %fusion.22, bf16[512,1024]{1,0:T(8,128)(2,1)S(1)} %get-tuple-element.323, bf16[512,1024]{1,0:T(8,128)(2,1)S(1)} %get-tuple-element.322, bf16[2,2048,1024]{2,1,0:T(8,128)(2,1)S(1)} %bitcast.256), kind=kOutput, calls=%fused_computation.3 | convolution fusion | flops 4341104640 | bytes 18874368 | tf_op jit(solution)/shard_map/dot_general | solution.py:814
  446.3 28.8 %attn_bwd_full.2 = bf16[1024,1536]{1,0:T(8,128)(2,1)S(1)} custom-call(s32[2]{0:T(128)S(1)} %pad_add_fusion.lims_ref, bf16[1024,1536]{1,0:T(8,128)(2,1)} %copy-done.11, bf16[1024,1536]{1,0:T(8,128)(2,1)} %copy-done.11, bf16[1024,1536]{1,0:T(8,128)(2,1)} %copy-done.11, f32[4,2,1024]{2,1,0:T(2,128)S(1)} %get-tuple-element.167.l_ref, ...), custom_call_target="tpu_custom_call" | custom-call | flops 10737418240 | bytes 7340032 | tf_op jit(solution)/shard_map/attn_bwd_full/pallas_call | solution.py:434
  475.1 14.7 %collective-permute-done.13 = bf16[1024,1024]{1,0:T(8,128)(2,1)} collective-permute-done((bf16[1024,1024]{1,0:T(8,128)(2,1)}, bf16[1024,1024]{1,0:T(8,128)(2,1)}, u32[]{:S(2)}, u32[]{:S(2)}) %collective-permute-start.13) | collective-permute-done | bytes 2097184 | tf_op jit(solution)/shard_map/ppermute | solution.py:451
  499.8 29.0 %attn_bwd_full.3 = bf16[1024,1536]{1,0:T(8,128)(2,1)S(1)} custom-call(s32[2]{0:T(128)S(1)} %pad_add_fusion.lims_ref, bf16[1024,1536]{1,0:T(8,128)(2,1)} %copy-done.10, bf16[1024,1536]{1,0:T(8,128)(2,1)} %copy-done.10, bf16[1024,1536]{1,0:T(8,128)(2,1)} %copy-done.10, f32[4,2,1024]{2,1,0:T(2,128)S(1)} %get-tuple-element.172.l_ref, ...), custom_call_target="tpu_custom_call" | custom-call | flops 10737418240 | bytes 7340032 | tf_op jit(solution)/shard_map/attn_bwd_full/pallas_call | solution.py:434
  659.5 24.9 %attn_bwd_causal.2 = bf16[1024,1536]{1,0:T(8,128)(2,1)S(1)} custom-call(s32[2]{0:T(128)S(1)} %pad_add_fusion.lims_ref, bf16[1024,1536]{1,0:T(8,128)(2,1)} %copy-done.9, bf16[1024,1536]{1,0:T(8,128)(2,1)} %copy-done.9, bf16[1024,1536]{1,0:T(8,128)(2,1)} %copy-done.9, f32[4,2,1024]{2,1,0:T(2,128)S(1)} %get-tuple-element.206.l_ref, ...), custom_call_target="tpu_custom_call" | custom-call | flops 10737418240 | bytes 7340032 | tf_op jit(solution)/shard_map/attn_bwd_causal/pallas_call | solution.py:434
  692.1 12.0 %collective-permute-done.32 = bf16[128,1024]{1,0:T(8,128)(2,1)S(1)} collective-permute-done((bf16[128,1024]{1,0:T(8,128)(2,1)S(1)}, bf16[128,1024]{1,0:T(8,128)(2,1)S(1)}, u32[]{:S(2)}, u32[]{:S(2)}) %collective-permute-start.32) | collective-permute-done | bytes 262176 | tf_op jit(solution)/shard_map/ppermute | solution.py:455
  722.5 24.9 %attn_bwd_causal.3 = bf16[1024,1536]{1,0:T(8,128)(2,1)S(1)} custom-call(s32[2]{0:T(128)S(1)} %pad_add_fusion.lims_ref, bf16[1024,1536]{1,0:T(8,128)(2,1)} %convolution_convert_fusion.7.q_ref.k_ref.v_ref, bf16[1024,1536]{1,0:T(8,128)(2,1)} %convolution_convert_fusion.7.q_ref.k_ref.v_ref, bf16[1024,1536]{1,0:T(8,128)(2,1)} %convolution_convert_fusion.7.q_ref.k_ref.v_ref, ...), custom_call_target="tpu_custom_call" | custom-call | flops 10737418240 | bytes 7340032 | tf_op jit(solution)/shard_map/attn_bwd_causal/pallas_call | solution.py:434
  799.2 16.2 %collective-permute-done.53 = bf16[512,1024]{1,0:T(8,128)(2,1)S(1)} collective-permute-done((bf16[512,1024]{1,0:T(8,128)(2,1)S(1)}, bf16[512,1024]{1,0:T(8,128)(2,1)S(1)}, u32[]{:S(2)}, u32[]{:S(2)}) %collective-permute-start.53) | collective-permute-done | bytes 1048608 | tf_op jit(solution)/shard_map/ppermute | solution.py:455
  842.0 32.8 %collective-permute-done.49 = bf16[1024,768]{1,0:T(8,128)(2,1)S(1)} collective-permute-done((bf16[1024,768]{1,0:T(8,128)(2,1)S(1)}, bf16[1024,768]{1,0:T(8,128)(2,1)S(1)}, u32[]{:S(2)}, u32[]{:S(2)}) %collective-permute-start.49) | collective-permute-done | bytes 1572896 | tf_op jit(solution)/shard_map/ppermute | solution.py:451
  875.9 18.9 %collective-permute-done.50 = bf16[512,768]{1,0:T(8,128)(2,1)S(1)} collective-permute-done((bf16[512,768]{1,0:T(8,128)(2,1)S(1)}, bf16[512,768]{1,0:T(8,128)(2,1)S(1)}, u32[]{:S(2)}, u32[]{:S(2)}) %collective-permute-start.50) | collective-permute-done | bytes 786464 | tf_op jit(solution)/shard_map/ppermute | solution.py:455
  909.1 16.0 %collective-permute-done.52 = bf16[128,768]{1,0:T(8,128)(2,1)S(1)} collective-permute-done((bf16[128,768]{1,0:T(8,128)(2,1)S(1)}, bf16[128,768]{1,0:T(8,128)(2,1)S(1)}, u32[]{:S(2)}, u32[]{:S(2)}) %collective-permute-start.52) | collective-permute-done | bytes 196640 | tf_op jit(solution)/shard_map/ppermute | solution.py:455
  926.5 12.3 %collective-permute-done.58 = bf16[256,1024]{1,0:T(8,128)(2,1)S(1)} collective-permute-done((bf16[256,1024]{1,0:T(8,128)(2,1)S(1)}, bf16[256,1024]{1,0:T(8,128)(2,1)S(1)}, u32[]{:S(2)}, u32[]{:S(2)}) %collective-permute-start.58) | collective-permute-done | bytes 524320 | tf_op jit(solution)/shard_map/ppermute | solution.py:455
  940.5 17.2 %collective-permute-done.59 = bf16[128,1024]{1,0:T(8,128)(2,1)S(1)} collective-permute-done((bf16[128,1024]{1,0:T(8,128)(2,1)S(1)}, bf16[128,1024]{1,0:T(8,128)(2,1)S(1)}, u32[]{:S(2)}, u32[]{:S(2)}) %collective-permute-start.59) | collective-permute-done | bytes 262176 | tf_op jit(solution)/shard_map/ppermute | solution.py:455
  969.0 19.5 %collective-permute-done.60 = f32[4,1024]{1,0:T(4,128)S(1)} collective-permute-done((f32[4,1024]{1,0:T(4,128)S(1)}, f32[4,1024]{1,0:T(4,128)S(1)}, u32[]{:S(2)}, u32[]{:S(2)}) %collective-permute-start.60) | collective-permute-done | bytes 16416 | tf_op jit(solution)/shard_map/ppermute | solution.py:451
  1057.9 11.5 place_qkv.2.refs_0_
  1087.6 11.5 place_qkv.3
  1099.1 14.3 %copy.81 = f32[2,1024,3,512]{3,1,2,0:T(8,128)} copy(f32[2,1024,3,512]{3,2,1,0:T(4,128)} %place_qkv.3) | data formatting | bytes 25165824
  1113.4 25.6 %all-gather.33.cloned.1.call-done = bf16[2048,1024]{1,0:T(8,128)(2,1)} async-done(((bf16[128,1024]{1,0:T(8,128)(2,1)}), bf16[2048,1024]{1,0:T(8,128)(2,1)}) %all-gather.33.cloned.1.call-update) | async-done | bytes 4194320 | tf_op jit(solution)/shard_map/all_gather | solution.py:655
  (756 shorter events, 689.4 us)
Async XLA Ops:
  7.2 101.8 %all-gather.21.cloned.1.call-start = ((), (), s32[]{:S(2)}) async-start(), calls=%async_computation | async-start | bytes 4456448 | tf_op jit(solution)/shard_map/all_gather | solution.py:727
  38.7 203.5 %all-gather.23.cloned.1.call-start = ((), (), s32[]{:S(2)}) async-start(), calls=%async_computation.1 | async-start | bytes 13369344 | tf_op jit(solution)/shard_map/all_gather | solution.py:727
  82.6 928.8 %all-gather.31.cloned.1.call-start = ((), (), s32[]{:S(2)}) async-start(), calls=%async_computation.5 | async-start | bytes 1114112 | tf_op jit(solution)/shard_map/all_gather | solution.py:655
  106.3 49.1 %collective-permute-start.5 = (bf16[512,1024]{1,0:T(8,128)(2,1)}, bf16[512,1024]{1,0:T(8,128)(2,1)}, u32[]{:S(2)}, u32[]{:S(2)}) collective-permute-start(bf16[512,1024]{1,0:T(8,128)(2,1)} %get-tuple-element.143), channel_id=1, source_target_pairs={{0,1},{1,0},{2,3},{3,2},{4,5},{5,4},{6,7},{7,6},{8,9},{9,8},{10,11... | collective-permute-start | bytes 3145736 | tf_op jit(solution)/shard_map/ppermute | solution.py:451
  107.4 48.0 %collective-permute-start.4 = (bf16[512,1024]{1,0:T(8,128)(2,1)}, bf16[512,1024]{1,0:T(8,128)(2,1)}, u32[]{:S(2)}, u32[]{:S(2)}) collective-permute-start(bf16[512,1024]{1,0:T(8,128)(2,1)} %collective-permute-done.2), channel_id=1, source_target_pairs={{0,4},{2,6},{4,0},{6,2},{8,12},{10,14},{12,8},{14,10},{16,20},{18,... | collective-permute-start | bytes 3145736 | tf_op jit(solution)/shard_map/ppermute | solution.py:455
  201.1 137.4 %collective-permute-start.9 = (bf16[512,1024]{1,0:T(8,128)(2,1)}, bf16[512,1024]{1,0:T(8,128)(2,1)}, u32[]{:S(2)}, u32[]{:S(2)}) collective-permute-start(bf16[512,1024]{1,0:T(8,128)(2,1)} %dynamic-slice_bitcast_fusion), channel_id=1, source_target_pairs={{0,1},{1,0},{2,3},{3,2},{4,5},{5,4},{6,7},{7,6},{8,9},{9,8},{10,11... | collective-permute-start | bytes 3145736 | tf_op jit(solution)/shard_map/ppermute | solution.py:451
  441.6 48.2 %collective-permute-start.13 = (bf16[1024,1024]{1,0:T(8,128)(2,1)}, bf16[1024,1024]{1,0:T(8,128)(2,1)}, u32[]{:S(2)}, u32[]{:S(2)}) collective-permute-start(bf16[1024,1024]{1,0:T(8,128)(2,1)} %add_convert_fusion.10), channel_id=1, source_target_pairs={{0,1},{1,0},{2,3},{3,2},{4,5},{5,4},{6,7},{7,6},{8,9},{9,8},{10,11... | collective-permute-start | bytes 6291464 | tf_op jit(solution)/shard_map/ppermute | solution.py:451
  498.6 50.2 %collective-permute-start.20 = (bf16[1024,1024]{1,0:T(8,128)(2,1)}, bf16[1024,1024]{1,0:T(8,128)(2,1)}, u32[]{:S(2)}, u32[]{:S(2)}) collective-permute-start(bf16[1024,1024]{1,0:T(8,128)(2,1)} %add_convert_fusion.8), channel_id=1, source_target_pairs={{0,1},{1,0},{2,3},{3,2},{4,5},{5,4},{6,7},{7,6},{8,9},{9,8},{10,11... | collective-permute-start | bytes 6291464 | tf_op jit(solution)/shard_map/ppermute | solution.py:451
  532.5 43.4 %collective-permute-start.22 = (bf16[256,1024]{1,0:T(8,128)(2,1)}, bf16[256,1024]{1,0:T(8,128)(2,1)S(1)}, u32[]{:S(2)}, u32[]{:S(2)}) collective-permute-start(bf16[256,1024]{1,0:T(8,128)(2,1)} %add_convert_fusion.32), channel_id=1, source_target_pairs={{0,1},{1,0},{2,3},{3,2},{4,5},{5,4},{6,7},{7,6},{8,9},{9,8},{10,11... | collective-permute-start | bytes 1572872 | tf_op jit(solution)/shard_map/ppermute | solution.py:451
  586.2 57.0 %collective-permute-start.31 = (bf16[1024,768]{1,0:T(8,128)(2,1)}, bf16[1024,768]{1,0:T(8,128)(2,1)}, u32[]{:S(2)}, u32[]{:S(2)}) collective-permute-start(bf16[1024,768]{1,0:T(8,128)(2,1)} %add_convert_fusion.19), channel_id=1, source_target_pairs={{0,1},{1,0},{2,3},{3,2},{4,5},{5,4},{6,7},{7,6},{8,9},{9,8},{10,11... | collective-permute-start | bytes 4718600 | tf_op jit(solution)/shard_map/ppermute | solution.py:451
  626.9 77.2 %collective-permute-start.35 = (bf16[1024,1024]{1,0:T(8,128)(2,1)}, bf16[1024,1024]{1,0:T(8,128)(2,1)}, u32[]{:S(2)}, u32[]{:S(2)}) collective-permute-start(bf16[1024,1024]{1,0:T(8,128)(2,1)} %add_convert_fusion.6), channel_id=1, source_target_pairs={{0,1},{1,0},{2,3},{3,2},{4,5},{5,4},{6,7},{7,6},{8,9},{9,8},{10,11... | collective-permute-start | bytes 6291464 | tf_op jit(solution)/shard_map/ppermute | solution.py:451
  655.4 48.7 %collective-permute-start.37 = (bf16[1024,1024]{1,0:T(8,128)(2,1)S(1)}, bf16[1024,1024]{1,0:T(8,128)(2,1)}, u32[]{:S(2)}, u32[]{:S(2)}) collective-permute-start(bf16[1024,1024]{1,0:T(8,128)(2,1)S(1)} %constant_dynamic-slice_fusion.20), channel_id=1, source_target_pairs={{0,2},{2,0},{4,6},{6,4},{8,10},{10,8},{12,14},{14,12},{16,18},{18,... | collective-permute-start | bytes 6291464 | tf_op jit(solution)/shard_map/ppermute | solution.py:455
  655.5 49.5 %collective-permute-start.36 = (bf16[1024,1024]{1,0:T(8,128)(2,1)}, bf16[1024,1024]{1,0:T(8,128)(2,1)}, u32[]{:S(2)}, u32[]{:S(2)}) collective-permute-start(bf16[1024,1024]{1,0:T(8,128)(2,1)} %convolution_convert_fusion.14), channel_id=1, source_target_pairs={{0,2},{2,0},{4,6},{6,4},{8,10},{10,8},{12,14},{14,12},{16,18},{18,... | collective-permute-start | bytes 6291464 | tf_op jit(solution)/shard_map/ppermute | solution.py:455
  659.0 45.1 %collective-permute-start.34 = (bf16[512,768]{1,0:T(8,128)(2,1)}, bf16[512,768]{1,0:T(8,128)(2,1)S(1)}, u32[]{:S(2)}, u32[]{:S(2)}) collective-permute-start(bf16[512,768]{1,0:T(8,128)(2,1)} %constant_dynamic-slice_fusion.21), channel_id=1, source_target_pairs={{0,4},{2,6},{4,0},{6,2},{8,12},{10,14},{12,8},{14,10},{16,20},{18,... | collective-permute-start | bytes 2359304 | tf_op jit(solution)/shard_map/ppermute | solution.py:455
  705.7 315.3 %all-gather.39.cloned.1.call-start = ((), (), s32[]{:S(2)}) async-start(), calls=%async_computation.9 | async-start | bytes 4456448 | tf_op jit(solution)/shard_map/all_gather | solution.py:655
  706.6 331.4 %all-gather.29.cloned.1.call-start = ((), (), s32[]{:S(2)}) async-start(), calls=%async_computation.4 | async-start | bytes 1114112 | tf_op jit(solution)/shard_map/all_gather | solution.py:655
  709.0 42.5 %collective-permute-start.38 = (bf16[256,768]{1,0:T(8,128)(2,1)}, bf16[256,768]{1,0:T(8,128)(2,1)}, u32[]{:S(2)}, u32[]{:S(2)}) collective-permute-start(bf16[256,768]{1,0:T(8,128)(2,1)} %constant_dynamic-slice_fusion.19), channel_id=1, source_target_pairs={{0,8},{2,10},{4,12},{6,14},{8,0},{10,2},{12,4},{14,6},{16,24},{18,... | collective-permute-start | bytes 1179656 | tf_op jit(solution)/shard_map/ppermute | solution.py:455
  721.3 55.0 %collective-permute-start.42 = (bf16[1024,1024]{1,0:T(8,128)(2,1)S(1)}, bf16[1024,1024]{1,0:T(8,128)(2,1)}, u32[]{:S(2)}, u32[]{:S(2)}) collective-permute-start(bf16[1024,1024]{1,0:T(8,128)(2,1)S(1)} %add_convert_fusion.4), channel_id=1, source_target_pairs={{0,1},{1,0},{2,3},{3,2},{4,5},{5,4},{6,7},{7,6},{8,9},{9,8},{10,11... | collective-permute-start | bytes 6291464 | tf_op jit(solution)/shard_map/ppermute | solution.py:451
  832.3 214.7 %all-gather.35.cloned.1.call-start = ((), (), s32[]{:S(2)}) async-start(), calls=%async_computation.7 | async-start | bytes 4456448 | tf_op jit(solution)/shard_map/all_gather | solution.py:655
  834.2 223.8 %all-gather.27.cloned.1.call-start = ((), (), s32[]{:S(2)}) async-start(), calls=%async_computation.3 | async-start | bytes 3342336 | tf_op jit(solution)/shard_map/all_gather | solution.py:655
  835.9 233.5 %all-gather.37.cloned.1.call-start = ((), (), s32[]{:S(2)}) async-start(), calls=%async_computation.8 | async-start | bytes 4456448 | tf_op jit(solution)/shard_map/all_gather | solution.py:655
  837.7 249.9 %all-gather.25.cloned.1.call-start = ((), (), s32[]{:S(2)}) async-start(), calls=%async_computation.2 | async-start | bytes 3342336 | tf_op jit(solution)/shard_map/all_gather | solution.py:655
  925.9 213.1 %all-gather.33.cloned.1.call-start = ((), (), s32[]{:S(2)}) async-start(), calls=%async_computation.6 | async-start | bytes 4456448 | tf_op jit(solution)/shard_map/all_gather | solution.py:655
  967.8 64.2 %collective-permute-start.48 = (bf16[512,1024]{1,0:T(8,128)(2,1)S(1)}, bf16[512,1024]{1,0:T(8,128)(2,1)S(1)}, u32[]{:S(2)}, u32[]{:S(2)}) collective-permute-start(bf16[512,1024]{1,0:T(8,128)(2,1)S(1)} %copy-done.89), channel_id=1, source_target_pairs={{0,1},{1,0},{2,3},{3,2},{4,5},{5,4},{6,7},{7,6},{8,9},{9,8},{10,11... | collective-permute-start | bytes 3145736 | tf_op jit(solution)/shard_map/ppermute | solution.py:451
  (222 other events, 3733.6 us)
Sparse Core Ops, SparseCore 0:
  38.8 54.4 all-gather.20
  95.6 118.9 all-gather.22
  705.9 39.5 all-gather.30
  747.4 69.1 all-gather.38
  832.5 38.6 all-gather.28
  873.1 57.2 all-gather.34
  932.7 52.0 all-gather.26
  987.0 54.5 all-gather.36
  1043.9 43.6 all-gather.24
  1089.6 49.3 all-gather.32

commit v3 on v2

--- a/solution.py
+++ b/solution.py
@@ -375,27 +375,25 @@
             block(pl.multiple_of(i*bq,bq),length); return c
         lax.fori_loop(0,nq,body,0)
 
-def attn_fwd(qkv, lims, group, causal, bq=256):
+def attn_fwd(qkv, lims, causal, bq=256):
     length=qkv.shape[0]; width=qkv.shape[1]//3; pairs=width//128
-    per=group//128
-    spec=lambda off: pl.BlockSpec((length,128),lambda i,off=off:(0,(i//per)*3*per+off*per+i%per))
+    spec=lambda off: pl.BlockSpec((length,128),lambda i,off=off:(0,off*pairs+i))
     return pl.pallas_call(partial(fwd_kernel,causal,bq),
         grid=(pairs,),
         in_specs=[pl.BlockSpec(memory_space=pltpu.SMEM),spec(0),spec(1),spec(2)],
         out_specs=[pl.BlockSpec((length,128),lambda i:(0,i)),pl.BlockSpec((1,2,length),lambda i:(i,0,0))],
         out_shape=[jax.ShapeDtypeStruct((length,width),bf16),jax.ShapeDtypeStruct((pairs,2,length),f32)],
         compiler_params=pltpu.CompilerParams(vmem_limit_bytes=48*2**20),
-        cost_estimate=pl.CostEstimate(flops=pairs*2*4*length*length*128,bytes_accessed=length*width*8,transcendentals=pairs*2*length*length),
+        cost_estimate=pl.CostEstimate(flops=pairs*2**20,bytes_accessed=length*width*8,transcendentals=0),
         name="attn_fwd_"+("causal" if causal else "full"),
     )(lims,qkv,qkv,qkv)
 
-def bwd_kernel(causal,bq,group,lims_ref,q_ref,k_ref,v_ref,l_ref,do_ref,grad_ref,dk_acc,dv_acc):
+def bwd_kernel(causal,bq,lims_ref,q_ref,k_ref,v_ref,l_ref,do_ref,grad_ref,dk_acc,dv_acc):
     length=q_ref.shape[0]
     lane=lax.broadcasted_iota(jnp.int32,(bq,128),1)
     dk_acc[...]=jnp.zeros_like(dk_acc); dv_acc[...]=jnp.zeros_like(dv_acc)
-    per=group//128
-    pair=pl.program_id(0)
-    at=[pl.multiple_of((lax.div(pair,per)*3*per+part*per+lax.rem(pair,per))*128,128) for part in range(3)]
+    width=grad_ref.shape[1]//3
+    at=[pl.multiple_of(part*width+pl.program_id(0)*128,128) for part in range(3)]
     def block(start,kk):
         q=q_ref[pl.ds(start,bq),:]*jnp.asarray(0.125,bf16)
         do=do_ref[pl.ds(start,bq),:]
@@ -426,19 +424,18 @@
     grad_ref[:,pl.ds(at[1],128)]=dk_acc[...].astype(bf16)
     grad_ref[:,pl.ds(at[2],128)]=dv_acc[...].astype(bf16)
 
-def attn_bwd(qkv,L,do,lims,group,causal,bq=256):
+def attn_bwd(qkv,L,do,lims,causal,bq=256):
     length=qkv.shape[0]; width=qkv.shape[1]//3; pairs=width//128
-    per=group//128
-    spec=lambda off: pl.BlockSpec((length,128),lambda i,off=off:(0,(i//per)*3*per+off*per+i%per))
+    spec=lambda off: pl.BlockSpec((length,128),lambda i,off=off:(0,off*pairs+i))
     one=pl.BlockSpec((length,128),lambda i:(0,i))
-    return pl.pallas_call(partial(bwd_kernel,causal,bq,group),
+    return pl.pallas_call(partial(bwd_kernel,causal,bq),
         grid=(pairs,),
         in_specs=[pl.BlockSpec(memory_space=pltpu.SMEM),spec(0),spec(1),spec(2),pl.BlockSpec((1,2,length),lambda i:(i,0,0)),one],
         out_specs=pl.BlockSpec((length,3*width),lambda i:(0,0)),
         out_shape=jax.ShapeDtypeStruct((length,3*width),bf16),
         scratch_shapes=[pltpu.VMEM((length,128),f32)]*2,
         compiler_params=pltpu.CompilerParams(vmem_limit_bytes=48*2**20),
-        cost_estimate=pl.CostEstimate(flops=pairs*2*10*length*length*128,bytes_accessed=length*width*14,transcendentals=pairs*2*length*length),
+        cost_estimate=pl.CostEstimate(flops=pairs*2**20,bytes_accessed=length*width*8,transcendentals=0),
         name="attn_bwd_"+("causal" if causal else "full"),
     )(lims,qkv,qkv,qkv,L,do)
 
@@ -509,7 +506,7 @@
 
 
 NN = (((1,), (0,)), ((), ()))
-SPLIT_AXIS = {"qkv": 1, "out": 0, "up": 1, "down": 0}
+SPLIT_AXIS = {"up": 1, "down": 0}
 PACK_WIDTH = 512
 
 
@@ -524,75 +521,143 @@
     return lax.dynamic_slice_in_dim(block, place * height, height, 0)
 
 
-def pack_piece(half, place, dp_size):
-    height = half.shape[0] // dp_size
-    piece = lax.dynamic_slice_in_dim(half, place * height, height, 0)
-    return [
-        lax.slice_in_dim(piece, at, at + PACK_WIDTH, axis=1)
-        for at in range(0, half.shape[1], PACK_WIDTH)
-    ]
+def flat_kernel(in_ref, out_ref):
+    width = in_ref.shape[3]
+    for part in range(3):
+        out_ref[:, part * width : (part + 1) * width] = in_ref[0, part]
+
+
+def flat_qkv(stacked, layer):
+    _, _, height, width = stacked.shape
+    rows = height // 2
+    return pl.pallas_call(
+        flat_kernel,
+        grid=(2,),
+        in_specs=[pl.BlockSpec((1, 3, rows, width), lambda step: (layer, 0, step, 0))],
+        out_specs=pl.BlockSpec((rows, 3 * width), lambda step: (step, 0)),
+        out_shape=jax.ShapeDtypeStruct((height, 3 * width), bf16),
+        cost_estimate=pl.CostEstimate(flops=0, bytes_accessed=12 * height * width, transcendentals=0),
+        name="flat_qkv",
+    )(stacked)
+
+
+def pack_kernel(kinds, place_ref, *refs):
+    out_ref = refs[-1]
+    at = 0
+    for kind, ref in zip(kinds, refs):
+        if kind == "qkv":
+            pieces = [ref[0, part] for part in range(3)]
+        else:
+            count = ref.shape[2] // PACK_WIDTH
+            pieces = [ref[0, :, part * PACK_WIDTH : (part + 1) * PACK_WIDTH] for part in range(count)]
+        for piece in pieces:
+            out_ref[at : at + piece.shape[0], :] = piece
+            at += piece.shape[0]
+
+
+def pack_pieces(place, layer, dp_size, kinds, arrays):
+    specs, total = [], 0
+    for kind, array in zip(kinds, arrays):
+        height, width = array.shape[-2:]
+        rows = height // dp_size
+        if kind == "qkv":
+            specs.append(pl.BlockSpec((1, 3, rows, width), lambda step, at: (layer, 0, at[0], 0)))
+            total += 3 * rows * width // PACK_WIDTH
+        else:
+            specs.append(pl.BlockSpec((1, rows, width), lambda step, at: (layer, at[0], 0)))
+            total += rows * width // PACK_WIDTH
+    return pl.pallas_call(
+        partial(pack_kernel, kinds),
+        grid_spec=pltpu.PrefetchScalarGridSpec(
+            num_scalar_prefetch=1,
+            grid=(1,),
+            in_specs=specs,
+            out_specs=pl.BlockSpec((total, PACK_WIDTH), lambda step, at: (0, 0)),
+        ),
+        out_shape=jax.ShapeDtypeStruct((total, PACK_WIDTH), bf16),
+        cost_estimate=pl.CostEstimate(flops=0, bytes_accessed=4 * total * PACK_WIDTH, transcendentals=0),
+        name="pack_pieces",
+    )(place.reshape(1).astype(jnp.int32), *arrays)
+
+
+def unpack_kernel(in_ref, *refs):
+    at = 0
+    for ref in refs:
+        rows = ref.shape[0] // in_ref.shape[0]
+        for part in range(ref.shape[1] // PACK_WIDTH):
+            for block in range(in_ref.shape[0]):
+                ref[block * rows : (block + 1) * rows, part * PACK_WIDTH : (part + 1) * PACK_WIDTH] = in_ref[
+                    block, at : at + rows, :
+                ]
+            at += rows
 
 
 def unpack_halves(gathered, shapes):
-    dp_size = gathered.shape[0]
-    halves, at = [], 0
-    for height, width in shapes:
-        rows = height // dp_size
-        count = width // PACK_WIDTH
-        part = lax.slice_in_dim(gathered, at, at + rows * count, axis=1)
-        part = part.reshape(dp_size, count, rows, PACK_WIDTH).transpose(0, 2, 1, 3)
-        halves.append(part.reshape(height, width))
-        at += rows * count
-    return halves
+    dp_size, total, _ = gathered.shape
+    some = max(1, dp_size // 4)
+    return pl.pallas_call(
+        unpack_kernel,
+        grid=(dp_size // some,),
+        in_specs=[pl.BlockSpec((some, total, PACK_WIDTH), lambda step: (step, 0, 0))],
+        out_specs=[
+            pl.BlockSpec((height // dp_size * some, width), lambda step: (step, 0)) for height, width in shapes
+        ],
+        out_shape=[jax.ShapeDtypeStruct(shape, bf16) for shape in shapes],
+        compiler_params=pltpu.CompilerParams(vmem_limit_bytes=32 * 2**20),
+        cost_estimate=pl.CostEstimate(
+            flops=0, bytes_accessed=4 * dp_size * total * PACK_WIDTH, transcendentals=0
+        ),
+        name="unpack_halves",
+    )(gathered)
 
 
 def place_kernel(kind, whole_ref, *refs):
     out_ref = refs[-1]
-    block = whole_ref[0].astype(f32)
+    block = whole_ref[...].reshape(-1, whole_ref.shape[-1]).astype(f32)
     if kind == "qkv":
         width = block.shape[1] // 3
         for part in range(3):
-            out_ref[0, :, part, :] = block[:, part * width : (part + 1) * width]
+            out_ref[0, part] = block[:, part * width : (part + 1) * width]
     else:
         out_ref[0] = block
 
 
-def place_grad(kind, whole, layer, base):
+def place_grad(kind, whole, layer, split, base):
     dp_size, rows, columns = whole.shape
-    bit_count = dp_size.bit_length() - 1
-
-    def source(step):
-        group, core = (step // (dp_size // 2), 0)
-        block = step % (dp_size // 2)
-        index = group
-        for bit in range(1, bit_count):
-            index = index + ((block >> (bit_count - 1 - bit)) & 1) * (1 << bit)
-        return index
-
-    half = dp_size // 2
-    if kind in ("out", "down"):
-        out_shape = (2, dp_size * rows, columns)
-        out_spec = pl.BlockSpec((1, rows, columns), lambda step: (layer, step, 0))
-    elif kind == "up":
-        out_shape = (2, half * rows, 2 * columns)
-        out_spec = pl.BlockSpec((1, rows, columns), lambda step: (layer, step % half, step // half))
+    half, some = dp_size // 2, dp_size // 4
+    whole = whole.reshape(half, 2, rows, columns)
+    if split == "rows":
+        block, source = (some, 2, rows, columns), lambda step: (step, 0, 0, 0)
+        steps = half // some
+        tall = some * 2 * rows
+        if kind == "qkv":
+            out_shape = (2, 3, dp_size * rows, columns // 3)
+            out_spec = pl.BlockSpec((1, 3, tall, columns // 3), lambda step: (layer, 0, step, 0))
+        else:
+            out_shape = (2, dp_size * rows, columns)
+            out_spec = pl.BlockSpec((1, tall, columns), lambda step: (layer, step, 0))
     else:
-        out_shape = (2, half * rows, 3, 2 * columns // 3)
-        out_spec = pl.BlockSpec(
-            (1, rows, 3, columns // 3), lambda step: (layer, step % half, 0, step // half)
-        )
-    operands, in_specs, aliases = [whole], [pl.BlockSpec((1, rows, columns), lambda step: (source(step), 0, 0))], {}
+        block, source = (some, None, rows, columns), lambda step: (step % 2, step // 2, 0, 0)
+        steps = 4
+        if kind == "down":
+            out_shape = (2, dp_size * rows, columns)
+            out_spec = pl.BlockSpec((1, some * rows, columns), lambda step: (layer, step, 0))
+        else:
+            out_shape = (2, half * rows, 2 * columns)
+            out_spec = pl.BlockSpec((1, some * rows, columns), lambda step: (layer, step % 2, step // 2))
+    operands, in_specs, aliases = [whole], [pl.BlockSpec(block, source)], {}
     if base is not None:
         operands.append(base)
         in_specs.append(pl.BlockSpec(memory_space=pl.ANY))
         aliases = {1: 0}
     return pl.pallas_call(
         partial(place_kernel, kind),
-        grid=(dp_size,),
+        grid=(steps,),
         in_specs=in_specs,
         out_specs=out_spec,
         out_shape=jax.ShapeDtypeStruct(out_shape, f32),
         input_output_aliases=aliases,
+        compiler_params=pltpu.CompilerParams(vmem_limit_bytes=32 * 2**20),
         cost_estimate=pl.CostEstimate(flops=0, bytes_accessed=6 * dp_size * rows * columns, transcendentals=0),
         name="place_" + kind,
     )(*operands)
@@ -620,45 +685,136 @@
     )(side.reshape(1).astype(jnp.int32), mine, other)
 
 
+def take_axis(block, index):
+    return lax.dynamic_index_in_dim(block, index, 1, keepdims=False)
+
+
+def flat_rows(block):
+    return block.reshape(-1, block.shape[-1])
+
+
 class Chain:
-    def __init__(self, kind, layer, own, near, far, place, dp_size):
-        self.kind, self.layer, self.place, self.dp_size = kind, layer, place, dp_size
+    def __init__(self, place, dp_size, rows, columns, kind, gather):
+        self.place, self.dp_size, self.kind, self.gather = place, dp_size, kind, gather
+        self.rows, self.columns = rows, columns
         self.bit_count = dp_size.bit_length() - 1
-        core = place & 1
-        self.near = near
-        self.kept = quarter_of(kind, own, core)
-        self.flight = [
-            swap_bit(far, 0, dp_size),
-            swap_bit(quarter_of(kind, own, 1 - core), 0, dp_size),
-        ]
-        self.stage = "core"
+        self.flight = []
 
     def bit(self, index):
         return (self.place >> index) & 1
 
+    def swap(self, block, bit):
+        return swap_bit(block, bit, self.dp_size)
+
+    def pair(self, block):
+        return block.reshape(-1, 2, self.rows, self.columns)
+
+    def start(self, near, far, ours=None, own_far=None):
+        self.near, self.ours = near, ours
+        self.flight = [self.swap(far, 0)] + ([] if ours is None else [self.swap(own_far, 0)])
+        self.state = "core"
+
+    def start_rows(self, own, other):
+        self.start_other(other)
+        self.add_own(own)
+
+    def start_other(self, other):
+        split, core = self.pair(other), self.bit(0)
+        self.start(flat_rows(take_axis(split, core)), flat_rows(take_axis(split, 1 - core)))
+
+    def add_own(self, own):
+        split, core = self.pair(own), self.bit(0)
+        self.flight = self.flight + [self.swap(flat_rows(take_axis(split, 1 - core)), 0)]
+        self.ours = flat_rows(take_axis(split, core))
+
+    def halves(self, block, bit):
+        split, here = self.pair(block), self.bit(bit)
+        return flat_rows(take_axis(split, here)), flat_rows(take_axis(split, 1 - here))
+
+    def settle(self, arrived):
+        self.near_here, self.near_away = self.halves(add_rounded(self.near, arrived[0]), 1)
+        if self.ours is not None:
+            self.kept_here, self.kept_away = self.halves(add_rounded(self.ours, arrived[1]), 1)
+        self.flight, self.state = [], "ready"
+
+    def launch(self):
+        self.flight = [swap_tensor(self.near_away) if self.kind == "x" else self.swap(self.near_away, 1)]
+        self.state = "first"
+
+    def second(self, arrived):
+        if len(arrived) > 1:
+            self.kept_here, self.kept_away = self.halves(add_rounded(self.ours, arrived[1]), 1)
+        if self.kind == "x":
+            self.kept_away = add_rounded(self.kept_away, arrived[0])
+        else:
+            self.near_here = add_rounded(self.near_here, arrived[0])
+        self.flight = [swap_tensor(self.near_here), self.swap(self.kept_away, 1)]
+        self.state = "second"
+
+    def next_bit(self, total, index):
+        if index == self.bit_count:
+            self.kept, self.state = total, "gather"
+            if self.gather == "native":
+                self.flight = [lax.all_gather(total, "dp", axis=0, tiled=False)]
+                return
+            self.kept, self.level = total[None], index - 1
+            self.flight = [self.swap(self.kept, self.level)]
+            return
+        self.kept, away = self.halves(total, index)
+        self.flight, self.index, self.state = [self.swap(away, index)], index, "bits"
+
+    def advance(self, arrived, hold=False):
+        if self.state == "done":
+            return
+        if self.state == "core":
+            self.settle(arrived)
+            if not hold:
+                self.launch()
+        elif self.state == "ready":
+            self.launch()
+        elif self.state == "first":
+            self.second(arrived)
+        elif self.state == "second":
+            total = self.kept_here.astype(f32) + arrived[0].astype(f32) + arrived[1].astype(f32)
+            self.next_bit(total.astype(bf16), 2)
+        elif self.state == "bits":
+            self.next_bit(add_rounded(self.kept, arrived[0]), self.index + 1)
+        elif self.gather == "native":
+            self.whole, self.flight, self.state = arrived[0], [], "done"
+        else:
+            here = self.bit(self.level)
+            first = jnp.where(here == 0, self.kept, arrived[0])
+            second = jnp.where(here == 0, arrived[0], self.kept)
+            joined = jnp.stack([first, second], axis=1)
+            self.kept = joined.reshape((-1,) + joined.shape[2:])
+            self.level -= 1
+            if self.level < 0:
+                self.whole, self.flight, self.state = self.kept, [], "done"
+            else:
+                self.flight = [self.swap(self.kept, self.level)]
+
+
+class Spread:
+    def __init__(self, block, dp_size):
+        self.block, self.dp_size = block, dp_size
+        self.bits = list(range(dp_size.bit_length() - 1))
+        self.flight = [swap_tensor(block)]
+
     def advance(self, arrived):
-        if self.stage == "core":
-            near_there, own_there = arrived
-            self.kept = self.kept.astype(f32) + own_there.astype(f32)
-            self.flight = [swap_tensor(add_rounded(self.near, near_there))]
-            self.near = None
-            self.stage = 0
+        if not arrived:
             return
-        total = (self.kept.astype(f32) + arrived[0].astype(f32)).astype(bf16)
-        self.stage += 1
-        if self.stage < self.bit_count:
-            bit = self.bit(self.stage)
-            self.kept = row_half(total, bit)
-            self.flight = [swap_bit(row_half(total, 1 - bit), self.stage, self.dp_size)]
+        self.block = self.block + arrived[0]
+        self.flight = [swap_bit(self.block, self.bits.pop(0), self.dp_size)] if self.bits else []
+
+
+def move(state, *chains, hold=()):
+    everyone = chains + tuple(hold)
+    state, flights = pin(state, [one.flight for one in everyone])
+    for one, flight in zip(everyone, flights):
+        if one in hold:
+            one.advance(flight, hold=True)
         else:
-            self.flight = []
-            self.whole = lax.all_gather(total, "dp", axis=0, tiled=False)
-
-
-def move(state, *chains):
-    state, flights = pin(state, [chain.flight for chain in chains])
-    for chain, flight in zip(chains, flights):
-        chain.advance(flight)
+            one.advance(flight)
     return state
 
 
@@ -682,9 +838,7 @@
     section_count = ada_scale.shape[1]
     side = lax.axis_index("tensor")
     place = lax.axis_index("dp")
-    bit_count = dp_size.bit_length() - 1
     core, near_row = place & 1, (place >> 1) & 1
-    group = w_qkv.shape[3] // 2
 
     def away_rows(halves):
         return lax.dynamic_index_in_dim(halves[:, 0], 1 - side, 0, keepdims=False)
@@ -708,83 +862,98 @@
         [jnp.sum(picker * ada_shift[part], axis=0) for part in range(2)],
     ]
 
-    def flat_qkv(layer):
-        split = w_qkv[layer].reshape(model_width, 3, 2, group).transpose(0, 2, 1, 3)
-        return split.reshape(model_width, 6 * group)
-
-    own = [
-        {"qkv": flat_qkv(layer), "out": w_out[layer], "up": w_up[layer], "down": w_down[layer]}
-        for layer in range(2)
-    ]
+    stacked = w_qkv.transpose(0, 2, 1, 3)
+    arrays = {"qkv": stacked, "out": w_out, "up": w_up, "down": w_down}
+    flat_shape = {
+        "qkv": (model_width, 3 * stacked.shape[3]),
+        "out": w_out.shape[1:],
+        "up": w_up.shape[1:],
+        "down": w_down.shape[1:],
+    }
 
     def packed(layer, kinds):
-        pieces = []
-        for kind in kinds:
-            pieces += pack_piece(own[layer][kind], place, dp_size)
-        return jnp.concatenate(pieces, axis=0)
-
-    def gathered(arrived, layer, kinds):
-        whole = lax.all_gather(arrived, "dp", axis=0, tiled=False)
-        return dict(zip(kinds, unpack_halves(whole, [own[layer][kind].shape for kind in kinds])))
+        return pack_pieces(place, layer, dp_size, kinds, [arrays[kind] for kind in kinds])
+
+    def gathered(arrived):
+        return lax.all_gather(arrived, "dp", axis=0, tiled=False)
+
+    def unpacked(whole, kinds):
+        return dict(zip(kinds, unpack_halves(whole, [flat_shape[kind] for kind in kinds])))
 
     attn_kinds, all_kinds = ("qkv", "out"), ("qkv", "out", "up", "down")
     first_pack = swap_tensor(packed(0, attn_kinds))
     other_rows = swap_tensor(away_rows(frames_in))
-    first = gathered(first_pack, 0, attn_kinds)
+    first_whole = gathered(first_pack)
     second_send = packed(1, all_kinds)
-    up_send = row_half(quarter_of("up", own[0]["up"], core), near_row)
-    down_send = row_half(quarter_of("down", own[0]["down"], core), near_row)
-    other_rows, second_send, up_send, down_send = pin(other_rows, second_send, up_send, down_send)
+    up_send = row_half(quarter_of("up", w_up[0], core), near_row)
+    down_send = row_half(quarter_of("down", w_down[0], core), near_row)
+    own_qkv = [flat_qkv(stacked, layer) for layer in range(2)]
+    other_rows, second_send, up_send, down_send, own_qkv = pin(
+        other_rows, second_send, up_send, down_send, own_qkv
+    )
     second_pack = swap_tensor(second_send)
     rows = whole_rows(frames_in, other_rows).astype(f32)
     normed, norm_kept = norm_forward(rows, gains[0][0], shifts[0][0])
-    mine = dot_low(normed, own[0]["qkv"], NN)
+    mine = dot_low(normed, own_qkv[0], NN)
     mine, second_pack, up_send, down_send = pin(mine, second_pack, up_send, down_send)
-    second = gathered(second_pack, 1, all_kinds)
+    second_whole = gathered(second_pack)
     up_piece = swap_tensor(up_send)
-    mix_mine = attn_fwd(mine, limits, group, True, 512)
+    mix_mine = attn_fwd(mine, limits, True, 512)
     mix_mine, up_piece, down_send = pin(mix_mine, up_piece, down_send)
     down_piece = swap_tensor(down_send)
     up_there = swap_bit(up_piece, 1, dp_size)
+    first = unpacked(first_whole, attn_kinds)
     theirs = dot_low(normed, first["qkv"], NN)
-    mix_theirs = attn_fwd(theirs, limits, group, True, 512)
+    mix_theirs = attn_fwd(theirs, limits, True, 512)
     mix_theirs, up_there, down_piece = pin(mix_theirs, up_there, down_piece)
     up_near = in_order(near_row, up_piece, up_there)
     up_far = swap_bit(up_near, 0, dp_size)
     down_there = swap_bit(down_piece, 1, dp_size)
     kept = [(normed, norm_kept, [mine, theirs], [mix_mine, mix_theirs])]
-    rows = rows + dot_sum([(mix_mine[0], own[0]["out"]), (mix_theirs[0], first["out"])], NN)
+    rows = rows + dot_sum([(mix_mine[0], w_out[0]), (mix_theirs[0], first["out"])], NN)
     normed, norm_kept = norm_forward(rows, gains[0][1], shifts[0][1])
-    pair_own = gelu_pair(jnp.dot(normed, own[0]["up"], preferred_element_type=f32))
-    pair_own, up_far, normed = pin(pair_own, up_far, normed)
+    pair_own = gelu_pair(jnp.dot(normed, w_up[0], preferred_element_type=f32))
+    pair_own, up_far, normed, norm_kept, rows = pin(pair_own, up_far, normed, norm_kept, rows)
     pair_near = gelu_pair(jnp.dot(normed, up_near, preferred_element_type=f32))
     pair_far = gelu_pair(jnp.dot(normed, up_far, preferred_element_type=f32))
-    rows = rows + dot_sum([(pair_own[0], own[0]["down"])], NN)
+    rows = rows + dot_sum([(pair_own[0], w_down[0])], NN)
     rows, pair_near, pair_far, down_there = pin(rows, pair_near, pair_far, down_there)
     down_near = in_order(near_row, down_piece, down_there)
     down_far = swap_bit(down_near, 0, dp_size)
     grad_send = away_rows(out_grad)
-    down_near, grad_send = pin(down_near, grad_send)
+    rows = rows + dot_sum([(pair_near[0], down_near)], NN)
+    rows, grad_send, down_far = pin(rows, grad_send, down_far)
     grad_other = swap_tensor(grad_send)
-    rows = rows + dot_sum([(pair_near[0], down_near), (pair_far[0], down_far)], NN)
+    rows = rows + dot_sum([(pair_far[0], down_far)], NN)
     kept.append((normed, norm_kept, [pair_own, pair_near, pair_far]))
+
+    normed, norm_kept = norm_forward(rows, gains[1][0], shifts[1][0])
+    mine = dot_low(normed, own_qkv[1], NN)
+    mix_mine = attn_fwd(mine, limits, False, 512)
+    mix_mine, second_whole = pin(mix_mine, second_whole)
+    second = unpacked(second_whole, all_kinds)
     weights = [
         {
-            "qkv": [own[0]["qkv"], first["qkv"]],
-            "out": [own[0]["out"], first["out"]],
-            "up": [own[0]["up"], up_near, up_far],
-            "down": [own[0]["down"], down_near, down_far],
+            "qkv": [own_qkv[0], first["qkv"]],
+            "out": [w_out[0], first["out"]],
+            "up": [w_up[0], up_near, up_far],
+            "down": [w_down[0], down_near, down_far],
         },
-        {kind: [own[1][kind], second[kind]] for kind in all_kinds},
+        {
+            "qkv": [own_qkv[1], second["qkv"]],
+            "out": [w_out[1], second["out"]],
+            "up": [w_up[1], second["up"]],
+            "down": [w_down[1], second["down"]],
+        },
     ]
-
-    normed, norm_kept = norm_forward(rows, gains[1][0], shifts[1][0])
-    projected = [dot_low(normed, part, NN) for part in weights[1]["qkv"]]
-    mixed = [attn_fwd(part, limits, group, False, 512) for part in projected]
+    theirs = dot_low(normed, second["qkv"], NN)
+    mix_theirs = attn_fwd(theirs, limits, False, 512)
+    mixed = [mix_mine, mix_theirs]
+    kept.append((normed, norm_kept, [mine, theirs], mixed))
     rows = rows + dot_sum([(mix[0], part) for mix, part in zip(mixed, weights[1]["out"])], NN)
-    kept.append((normed, norm_kept, projected, mixed))
     normed, norm_kept = norm_forward(rows, gains[1][1], shifts[1][1])
     pairs = [gelu_pair(jnp.dot(normed, part, preferred_element_type=f32)) for part in weights[1]["up"]]
+    pairs, rows, normed, norm_kept = pin(pairs, rows, normed, norm_kept)
     rows = rows + dot_sum([(pair[0], part) for pair, part in zip(pairs, weights[1]["down"])], NN)
     kept.append((normed, norm_kept, pairs))
     rows, grad_other = pin(rows, grad_other)
@@ -799,13 +968,18 @@
 
     norm_sums = [[None, None], [None, None]]
     grad_rows = whole_rows(out_grad, grad_other).astype(f32)
-
-    def chain(kind, layer, parts):
-        if len(parts) == 2:
-            near, far = (quarter_of(kind, parts[1], core), quarter_of(kind, parts[1], 1 - core))
+    def chain(kind, first, gather, split="rows"):
+        height, width = flat_shape[kind]
+        if split == "core":
+            count = dp_size // 2
+            height, width = (height, width // 2) if kind == "up" else (height // 2, width)
         else:
-            near, far = parts[1:]
-        return Chain(kind, layer, parts[0], near, far, place, dp_size)
+            count = dp_size
+        return Chain(place, dp_size, height // count, width, first, gather)
+
+    def start_quarters(one, kind, parts):
+        own, near, far = parts
+        one.start(near, far, quarter_of(kind, own, core), quarter_of(kind, own, 1 - core))
 
     def hidden_grads(layer, low):
         pairs = kept[2 * layer + 1][2]
@@ -830,7 +1004,8 @@
 
     def attention_grad(layer, part, grad_mix):
         _, _, projected, mixed = kept[2 * layer]
-        return attn_bwd(projected[part], mixed[part][1], grad_mix, limits, group, layer == 0, 512)
+        rows = 256 if layer == 0 else 512
+        return attn_bwd(projected[part], mixed[part][1], grad_mix, limits, layer == 0, rows)
 
     def norm_step(layer, part, grad_rows, grad_normed):
         added, grad_gain, grad_shift = norm_backward(
@@ -839,106 +1014,107 @@
         norm_sums[layer][part] = (grad_gain, grad_shift)
         return grad_rows + added
 
+    down1, up1 = chain("down", "x", "native"), chain("up", "y", "native")
+    out1, qkv1 = chain("out", "x", "native"), chain("qkv", "y", "native")
+    down0, up0 = chain("down", "x", "native", "core"), chain("up", "y", "swaps", "core")
+    out0, qkv0 = chain("out", "x", "swaps"), chain("qkv", "y", "swaps")
+
     low = grad_rows.astype(bf16)
     parts = down_grads(1, low)
     hidden = hidden_grads(1, low)
     parts, hidden, grad_rows = pin(parts, hidden, grad_rows)
-    down1 = chain("down", 1, parts)
+    down1.start_rows(*parts)
     parts = up_grads(1, hidden)
+    parts, hidden, grad_rows = move((parts, hidden, grad_rows), down1)
+    up1.start_rows(*parts)
     grad_normed = dot_sum(list(zip(hidden, weights[1]["up"])), NT)
-    parts, grad_normed = move((parts, grad_normed), down1)
-    up1 = chain("up", 1, parts)
     grad_rows = norm_step(1, 1, grad_rows, grad_normed)
     low = grad_rows.astype(bf16)
-    parts = out_grads(1, low)
+    out_parts = out_grads(1, low)
     mine, theirs = mixed_grads(1, low)
+    out_parts, mine, theirs, grad_rows = move((out_parts, mine, theirs, grad_rows), down1, hold=[up1])
+    out1.start_rows(*out_parts)
     theirs = attention_grad(1, 1, theirs)
-    parts, mine, theirs, grad_rows = move((parts, mine, theirs, grad_rows), down1, up1)
-    out1 = chain("out", 1, parts)
+    mine, theirs, grad_rows = move((mine, theirs, grad_rows), down1, up1, out1)
     mine = attention_grad(1, 0, mine)
-    mine, theirs = move((mine, theirs), down1, out1)
+    mine, theirs, grad_rows = move((mine, theirs, grad_rows), down1, up1, out1)
     parts = [dot_low(kept[2][0], part, TN) for part in (mine, theirs)]
     grad_normed = dot_sum(list(zip((mine, theirs), weights[1]["qkv"])), NT)
-    parts, grad_normed = move((parts, grad_normed), down1, up1)
-    qkv1 = chain("qkv", 1, parts)
     grad_rows = norm_step(1, 0, grad_rows, grad_normed)
+    early = Spread(
+        jnp.concatenate(
+            [picker * norm_sums[1][part][which][None] for which in range(2) for part in range(2)]
+        ),
+        dp_size,
+    )
     low = grad_rows.astype(bf16)
+    parts, low, grad_rows = move((parts, low, grad_rows), down1, up1, out1)
+    qkv1.start_rows(*parts)
     parts = down_grads(0, low)
-    parts, low, grad_rows = move((parts, low, grad_rows), down1, out1, qkv1)
-    down0 = chain("down", 0, parts)
+    parts, low, grad_rows = move((parts, low, grad_rows), up1, qkv1, early)
+    start_quarters(down0, "down", parts)
     hidden = hidden_grads(0, low)
-    (hidden,) = move((hidden,), up1, out1, down0)
+    hidden, grad_rows = move((hidden, grad_rows), down1, up1, qkv1, out1, early, hold=[down0])
     parts = up_grads(0, hidden)
     grad_normed = dot_sum(list(zip(hidden, weights[0]["up"])), NT)
-    parts, grad_normed = move((parts, grad_normed), up1, out1, qkv1)
-    up0 = chain("up", 0, parts)
+    parts, grad_normed, grad_rows = move((parts, grad_normed, grad_rows), qkv1, out1, down0, early)
+    start_quarters(up0, "up", parts)
     grad_rows = norm_step(0, 1, grad_rows, grad_normed)
     low = grad_rows.astype(bf16)
     out_parts = out_grads(0, low)
     mine, theirs = mixed_grads(0, low)
+    out_parts, mine, theirs, grad_rows = move((out_parts, mine, theirs, grad_rows), up0, qkv1, down0, early)
+    out0.start_rows(*out_parts)
     theirs = attention_grad(0, 1, theirs)
-    out_parts, mine, theirs, grad_rows = move(
-        (out_parts, mine, theirs, grad_rows), up1, out1, qkv1, down0, up0
-    )
-    out0 = chain("out", 0, out_parts)
+    mine, theirs, grad_rows = move((mine, theirs, grad_rows), up1, down0, up0, qkv1, early, hold=[out0])
     part_theirs = dot_low(kept[0][0], theirs, TN)
+    qkv0.start_other(part_theirs)
     mine = attention_grad(0, 0, mine)
-    mine, theirs, part_theirs = move((mine, theirs, part_theirs), qkv1, down0, out0)
+    mine, theirs, grad_rows = move((mine, theirs, grad_rows), out1, down0, up0, qkv0)
     part_mine = dot_low(kept[0][0], mine, TN)
+    qkv0.add_own(part_mine)
     grad_normed = dot_sum([(mine, weights[0]["qkv"][0]), (theirs, weights[0]["qkv"][1])], NT)
-    part_mine, grad_normed = move((part_mine, grad_normed), up0, qkv1)
-    qkv0 = chain("qkv", 0, [part_mine, part_theirs])
     grad_rows = norm_step(0, 0, grad_rows, grad_normed)
     grad_mine, grad_away = halves_of(grad_rows)
-    (grad_mine, grad_away) = move((grad_mine, grad_away), qkv0, out0, down0)
-    frames_grad = place_frames(side, grad_mine, swap_tensor(grad_away))
-    move((), up0, out0, down0)
-    frames_out = place_frames(side, out_mine, swap_tensor(out_away))
-    for one in (up0, out0, down0, qkv0):
+    late = Spread(
+        jnp.stack([norm_sums[0][part][which] for which in range(2) for part in range(2)]), dp_size
+    )
+    both_away = (grad_away, out_away)
+    both_away, grad_mine = move((both_away, grad_mine), qkv0, up0, down0, out0)
+    both_away, grad_mine = move((both_away, grad_mine), qkv0, up0, out0, late)
+    there = [swap_tensor(block) for block in both_away]
+    there, grad_mine = move((there, grad_mine), qkv0, up0, out0, late)
+    (grad_mine,) = move((grad_mine,), qkv1, qkv0, up0, out0, late)
+
+    def placed(kind, one):
+        return place_grad(kind, one.whole, 1, "rows", None)
+
+    bases = {"down": placed("down", down1), "up": placed("up", up1)}
+    bases, grad_mine = move((bases, grad_mine), qkv0, up0, out0, late)
+    bases["out"], bases["qkv"] = placed("out", out1), placed("qkv", qkv1)
+    bases, grad_mine = move((bases, grad_mine), down0, qkv0, up0, out0)
+    frames_grad = place_frames(side, grad_mine, there[0])
+    frames_out = place_frames(side, out_mine, there[1])
+    frames_grad, frames_out = move((frames_grad, frames_out), qkv0, up0, out0)
+    for one in (qkv0, up0, out0, down0, late, down1, up1, out1, qkv1, early):
         while one.flight:
             one.advance(one.flight)
 
-    def everywhere(block):
-        block = block + swap_tensor(block)
-        for bit in range(bit_count):
-            block = block + swap_bit(block, bit, dp_size)
-        return block
-
-    late = everywhere(
-        jnp.stack(
-            [
-                norm_sums[0][0][0],
-                norm_sums[0][1][0],
-                norm_sums[0][0][1],
-                norm_sums[0][1][1],
-            ]
-        )
-    )
-    early = everywhere(
-        jnp.concatenate(
-            [
-                picker * norm_sums[1][0][0][None],
-                picker * norm_sums[1][1][0][None],
-                picker * norm_sums[1][0][1][None],
-                picker * norm_sums[1][1][1][None],
-            ]
-        )
-    ).reshape(4, section_count, model_width)
-
-    def both(kind, later, sooner):
-        return place_grad(kind, sooner.whole, 0, place_grad(kind, later.whole, 1, None))
-
+    def both(kind, sooner, split="rows"):
+        return place_grad(kind, sooner.whole, 0, split, bases[kind])
+
+    gain_rows = early.block.reshape(4, section_count, model_width)
     return (
         frames_out,
         frames_grad,
-        both("qkv", qkv1, qkv0),
-        both("out", out1, out0),
-        both("up", up1, up0),
-        both("down", down1, down0),
-        late[0:2],
-        late[2:4],
-        early[0:2],
-        early[2:4],
+        both("qkv", qkv0).transpose(0, 2, 1, 3),
+        both("out", out0),
+        both("up", up0, "core"),
+        both("down", down0, "core"),
+        late.block[0:2],
+        late.block[2:4],
+        gain_rows[0:2],
+        gain_rows[2:4],
     )
 
 

time: 1170 us -> 1000 us (0.85)
  waiting for transfers between devices: 270 us -> 176 us
  Pallas kernels: 280 us -> 220 us
  local copies, waits for them, and re-layouts: 141 us -> 101 us
  starting transfers between devices: 69.1 us -> 86.3 us
  other arithmetic: 95.6 us -> 111 us
    ppermute x52 -> x68, waiting for transfers between devices: 144 us -> 95 us  [swap_bit(): lax.ppermute(block, 'dp', [(place, place ^ 1 << bit) for place in range(d...]
    pallas_call x12 -> x18, Pallas kernels: 192 us -> 143 us  [the longest x4 103 us: attn_bwd(): pl.pallas_call(partial(bwd_kernel, causal, bq), grid=(pairs,), in_specs=[...]
    dynamic_slice x5 -> x36, local copies, waits for them, and re-layouts: 2.02 us -> 37 us  [take_axis(): return lax.dynamic_index_in_dim(block, index, 1, keepdims=False)]
    all_gather x10 -> x7, waiting for transfers between devices: 33.1 us -> 0.01 us  [the longest x5 0.01 us: next_bit(): self.flight = [lax.all_gather(total, 'dp', axis=0, tiled=False)]]
    convert_element_type x8 -> x37, other arithmetic: 20.8 us -> 47.4 us  [add_rounded(): return (left.astype(f32) + right.astype(f32)).astype(bf16)]
    transpose x8 -> x0, local copies, waits for them, and re-layouts: 23.1 us -> none  [the longest x6 19.1 us: unpack_halves(): part = part.reshape(dp_size, count, rows, PACK_WIDTH).transpose(0, 2, 1, 3)]
    convert_element_type x32 -> x8, other arithmetic: 35.9 us -> 14.3 us  [advance(): self.next_bit(total.astype(bf16), 2)]
    slice x18 -> x6, local copies, waits for them, and re-layouts: 30.3 us -> 10.2 us  [the longest x1 4.89 us: paired_device(): up_send = row_half(quarter_of('up', w_up[0], core), near_row)]
  transfers between devices with their start and end apart: 80 -> 97, of which waited for: 29 -> 26; matrix products, arithmetic and copies ran while one was open for 33% -> 40% of each run, Pallas kernels for 23% -> 22%
where the time goes in v3:
time: 1000 us; the launch traced here: 996 us
  matrix products  285 us (28%)
  Pallas kernels  220 us (22%)
  waiting for transfers between devices  176 us (18%)
  other arithmetic  111 us (11%)
  local copies, waits for them, and re-layouts  101 us (10%)
  starting transfers between devices  86.3 us (9%)
  between operations  17.5 us (2%)
    pallas_call x4, Pallas kernels, attn_bwd(): pl.pallas_call(partial(bwd_kernel, causal, bq), grid=(pairs,), in_specs=[...  103 us
    dot_general x26, matrix products, dot_low(): lax.dot_general(left, right, dims, preferred_element_type=f32).astype(bf16)  101 us
    dot_general x18, matrix products, dot_sum(): term = lax.dot_general(left, right, dims, preferred_element_type=f32)  99.6 us
    ppermute x68, waiting for transfers between devices, swap_bit(): lax.ppermute(block, 'dp', [(place, place ^ 1 << bit) for place in range(d...  95 us
    ppermute x22, waiting for transfers between devices, swap_tensor(): return lax.ppermute(block, 'tensor', [(0, 1), (1, 0)])  81.3 us
    pallas_call x4, Pallas kernels, attn_fwd(): pl.pallas_call(partial(fwd_kernel, causal, bq), grid=(pairs,), in_specs=[...  66.1 us
    ppermute x68, starting transfers between devices, swap_bit(): lax.ppermute(block, 'dp', [(place, place ^ 1 << bit) for place in range(d...  58.7 us
    convert_element_type x37, other arithmetic, add_rounded(): return (left.astype(f32) + right.astype(f32)).astype(bf16)  47.4 us
  transfers between devices with their start and end apart: 97, of which 26 were waited for; matrix products, arithmetic and copies ran while one was open for 40% of the time, Pallas kernels for 22%

profile of v3, /device:TPU:0, one launch (start us, length us, event | category | flops | bytes accessed | tf_op | source)
XLA Modules:
  0.0 996.0 jit_solution(16679352618061582725)
XLA Ops:
  52.7 10.1 %collective-permute-done.1 = bf16[768,512]{1,0:T(8,128)(2,1)} collective-permute-done((bf16[768,512]{1,0:T(8,128)(2,1)S(1)}, bf16[768,512]{1,0:T(8,128)(2,1)}, u32[]{:S(2)}, u32[]{:S(2)}) %collective-permute-start.1) | collective-permute-done | bytes 786464 | tf_op jit(solution)/shard_map/ppermute | solution.py:448
  67.9 14.0 %attn_fwd_causal.2 = (bf16[1024,512]{1,0:T(8,128)(2,1)S(1)}, f32[4,2,1024]{2,1,0:T(2,128)S(1)}) custom-call(s32[2]{0:T(128)S(1)} %pad_add_fusion.lims_ref, bf16[1024,1536]{1,0:T(8,128)(2,1)S(1)} %convolution_convert_fusion.7.q_ref.k_ref.v_ref, bf16[1024,1536]{1,0:T(8,128)(2,1)S(1)} %convolution_convert_fusion.7.q_ref.k_ref.v_ref, ...), custom_call_target="tpu_custom_call" | custom-call | flops 4194304 | bytes 4194304 | tf_op jit(solution)/shard_map/attn_fwd_causal/pallas_call | solution.py:381
  98.7 14.2 %attn_fwd_causal.3 = (bf16[1024,512]{1,0:T(8,128)(2,1)S(1)}, f32[4,2,1024]{2,1,0:T(2,128)S(1)}) custom-call(s32[2]{0:T(128)S(1)} %pad_add_fusion.lims_ref, bf16[1024,1536]{1,0:T(8,128)(2,1)S(1)} %convolution_convert_fusion.6.q_ref.k_ref.v_ref, bf16[1024,1536]{1,0:T(8,128)(2,1)S(1)} %convolution_convert_fusion.6.q_ref.k_ref.v_ref, ...), custom_call_target="tpu_custom_call" | custom-call | flops 4194304 | bytes 4194304 | tf_op jit(solution)/shard_map/attn_fwd_causal/pallas_call | solution.py:381
  122.4 10.7 %add_convert_fusion.2 = (bf16[1024,2048]{1,0:T(8,128)(2,1)}, bf16[1024,2048]{1,0:T(8,128)(2,1)}) fusion(bf16[1024,1024]{1,0:T(8,128)(2,1)S(1)} %add_convert_fusion.11, bf16[2,1024,2048]{2,1,0:T(8,128)(2,1)S(1)} %bitcast.553), kind=kOutput, calls=%fused_computation.9 | convolution fusion | flops 4334813184 | bytes 14680064 | tf_op jit(solution)/shard_map/dot_general | solution.py:915
  185.3 19.1 %attn_fwd_full.2 = (bf16[1024,512]{1,0:T(8,128)(2,1)S(1)}, f32[4,2,1024]{2,1,0:T(2,128)S(1)}) custom-call(s32[2]{0:T(128)S(1)} %pad_add_fusion.lims_ref, bf16[1024,1536]{1,0:T(8,128)(2,1)S(1)} %convolution_convert_fusion.5.q_ref.k_ref.v_ref, bf16[1024,1536]{1,0:T(8,128)(2,1)S(1)} %convolution_convert_fusion.5.q_ref.k_ref.v_ref, ...), custom_call_target="tpu_custom_call" | custom-call | flops 4194304 | bytes 4194304 | tf_op jit(solution)/shard_map/attn_fwd_full/pallas_call | solution.py:381
  221.8 18.7 %attn_fwd_full.3 = (bf16[1024,512]{1,0:T(8,128)(2,1)S(1)}, f32[4,2,1024]{2,1,0:T(2,128)S(1)}) custom-call(s32[2]{0:T(128)S(1)} %pad_add_fusion.lims_ref, bf16[1024,1536]{1,0:T(8,128)(2,1)S(1)} %convolution_convert_fusion.4.q_ref.k_ref.v_ref, bf16[1024,1536]{1,0:T(8,128)(2,1)S(1)} %convolution_convert_fusion.4.q_ref.k_ref.v_ref, ...), custom_call_target="tpu_custom_call" | custom-call | flops 4194304 | bytes 4194304 | tf_op jit(solution)/shard_map/attn_fwd_full/pallas_call | solution.py:381
  246.8 15.2 %add_convert_fusion.1 = (bf16[1024,2048]{1,0:T(8,128)(2,1)}, bf16[1024,2048]{1,0:T(8,128)(2,1)}) fusion(bf16[1024,1024]{1,0:T(8,128)(2,1)S(1)} %add_convert_fusion.7, bf16[2,1024,2048]{2,1,0:T(8,128)(2,1)} %refs_2_.1), kind=kOutput, calls=%fused_computation.6 | convolution fusion | flops 4334813184 | bytes 14680064 | tf_op jit(solution)/shard_map/dot_general | solution.py:955
  262.0 10.4 %add_convert_fusion = (bf16[1024,2048]{1,0:T(8,128)(2,1)}, bf16[1024,2048]{1,0:T(8,128)(2,1)S(1)}) fusion(bf16[1024,1024]{1,0:T(8,128)(2,1)S(1)} %add_convert_fusion.7, bf16[1024,2048]{1,0:T(8,128)(2,1)S(1)} %get-tuple-element.262), kind=kOutput, calls=%fused_computation.3 | convolution fusion | flops 4334813184 | bytes 14680064 | tf_op jit(solution)/shard_map/dot_general | solution.py:955
  312.0 8.7 multiply_convert_fusion.2
  329.0 9.6 convolution_convert_fusion.11
  359.6 11.0 %multiply_reduce_fusion.2 = (f32[1024]{0:T(1024)S(1)}, f32[1024]{0:T(1024)S(1)}, f32[1024]{0:T(1024)S(1)}, f32[1024]{0:T(1024)S(1)}, f32[1024,1024]{1,0:T(8,128)}) fusion(f32[1024,1024]{1,0:T(8,128)S(1)} %copy-done.34, f32[1024]{0:T(1024)S(1)} %broadcast_multiply_fusion.12, f32[1024]{0:T(1024)S(1)} %add_rsqrt_fusion, f32[1024]{0:T(1024)S(1)} %get-tuple-element.470, ...), kind=kOutput, calls=%fused_computation.63 | convolution fusion | flops 4305448960 | bytes 21000192 | tf_op jit(solution)/shard_map/dot_general | solution.py:499
  388.6 8.4 collective-permute-done.12
  406.4 28.7 %attn_bwd_full.2 = bf16[1024,1536]{1,0:T(8,128)(2,1)S(1)} custom-call(s32[2]{0:T(128)S(1)} %pad_add_fusion.lims_ref, bf16[1024,1536]{1,0:T(8,128)(2,1)} %copy-done.3, bf16[1024,1536]{1,0:T(8,128)(2,1)} %copy-done.3, bf16[1024,1536]{1,0:T(8,128)(2,1)} %copy-done.3, f32[4,2,1024]{2,1,0:T(2,128)S(1)} %get-tuple-element.287.l_ref, ...), custom_call_target="tpu_custom_call" | custom-call | flops 4194304 | bytes 4194304 | tf_op jit(solution)/shard_map/attn_bwd_full/pallas_call | solution.py:431
  444.9 29.2 %attn_bwd_full.3 = bf16[1024,1536]{1,0:T(8,128)(2,1)S(1)} custom-call(s32[2]{0:T(128)S(1)} %pad_add_fusion.lims_ref, bf16[1024,1536]{1,0:T(8,128)(2,1)} %copy-done.2, bf16[1024,1536]{1,0:T(8,128)(2,1)} %copy-done.2, bf16[1024,1536]{1,0:T(8,128)(2,1)} %copy-done.2, f32[4,2,1024]{2,1,0:T(2,128)S(1)} %get-tuple-element.256.l_ref, ...), custom_call_target="tpu_custom_call" | custom-call | flops 4194304 | bytes 4194304 | tf_op jit(solution)/shard_map/attn_bwd_full/pallas_call | solution.py:431
  508.0 18.1 %collective-permute-done.23 = bf16[256,2048]{1,0:T(8,128)(2,1)S(1)} collective-permute-done((bf16[256,2048]{1,0:T(8,128)(2,1)S(1)}, bf16[256,2048]{1,0:T(8,128)(2,1)S(1)}, u32[]{:S(2)}, u32[]{:S(2)}) %collective-permute-start.23) | collective-permute-done | bytes 1048608 | tf_op jit(solution)/shard_map/ppermute | solution.py:448
  586.2 10.9 %collective-permute-done.31 = bf16[64,2048]{1,0:T(8,128)(2,1)S(1)} collective-permute-done((bf16[64,2048]{1,0:T(8,128)(2,1)S(1)}, bf16[64,2048]{1,0:T(8,128)(2,1)S(1)}, u32[]{:S(2)}, u32[]{:S(2)}) %collective-permute-start.31) | collective-permute-done | bytes 262176 | tf_op jit(solution)/shard_map/ppermute | solution.py:452
  686.9 8.3 collective-permute-done.46
  700.2 22.4 %attn_bwd_causal.2 = bf16[1024,1536]{1,0:T(8,128)(2,1)S(1)} custom-call(s32[2]{0:T(128)S(1)} %pad_add_fusion.lims_ref, bf16[1024,1536]{1,0:T(8,128)(2,1)} %copy-done.1, bf16[1024,1536]{1,0:T(8,128)(2,1)} %copy-done.1, bf16[1024,1536]{1,0:T(8,128)(2,1)} %copy-done.1, f32[4,2,1024]{2,1,0:T(2,128)S(1)} %get-tuple-element.350.l_ref, bf16[1024,512]{1,0:T(8,128)(2,1)S(1)} %copy-done.20), custom_call_target="tpu_custom_call" | custom-call | flops 4194304 | bytes 4194304 | tf_op jit(solution)/shard_map/attn_bwd_causal/pallas_call | solution.py:431
  750.6 22.5 %attn_bwd_causal.3 = bf16[1024,1536]{1,0:T(8,128)(2,1)S(1)} custom-call(s32[2]{0:T(128)S(1)} %pad_add_fusion.lims_ref, bf16[1024,1536]{1,0:T(8,128)(2,1)} %copy-done, bf16[1024,1536]{1,0:T(8,128)(2,1)} %copy-done, bf16[1024,1536]{1,0:T(8,128)(2,1)} %copy-done, f32[4,2,1024]{2,1,0:T(2,128)S(1)} %get-tuple-element.363.l_ref, bf16[1024,512]{1,0:T(8,128)(2,1)S(1)} %copy-done.19), custom_call_target="tpu_custom_call" | custom-call | flops 4194304 | bytes 4194304 | tf_op jit(solution)/shard_map/attn_bwd_causal/pallas_call | solution.py:431
  822.9 9.4 collective-permute-done.65
  845.4 22.7 %collective-permute-done.69 = bf16[1,128,1024]{2,1,0:T(8,128)(2,1)S(1)} collective-permute-done((bf16[1,128,1024]{2,1,0:T(8,128)(2,1)S(1)}, bf16[1,128,1024]{2,1,0:T(8,128)(2,1)S(1)}, u32[]{:S(2)}, u32[]{:S(2)}) %collective-permute-start.69) | collective-permute-done | bytes 262176 | tf_op jit(solution)/shard_map/ppermute | solution.py:452
  868.2 15.4 %collective-permute-done.67.other_ref = bf16[512,1024]{1,0:T(8,128)(2,1)} collective-permute-done((bf16[512,1024]{1,0:T(8,128)(2,1)S(1)}, bf16[512,1024]{1,0:T(8,128)(2,1)}, u32[]{:S(2)}, u32[]{:S(2)}) %collective-permute-start.67) | collective-permute-done | bytes 1048608 | tf_op jit(solution)/shard_map/ppermute | solution.py:448
  895.4 9.4 collective-permute-done.73
  920.3 9.5 collective-permute-done.78
  (848 shorter events, 621.8 us)
Async XLA Ops:
  7.2 82.2 %all-gather.15.cloned.1.call-start = ((), (), s32[]{:S(2)}) async-start(), calls=%async_computation | async-start | bytes 4456448 | tf_op jit(solution)/shard_map/all_gather | solution.py:878
  19.2 186.9 %all-gather.17.cloned.1.call-start = ((), (), s32[]{:S(2)}) async-start(), calls=%async_computation.1 | async-start | bytes 13369344 | tf_op jit(solution)/shard_map/all_gather | solution.py:878
  62.8 535.2 %all-gather.19.cloned.1.call-start = ((), (), s32[]{:S(2)}) async-start(), calls=%async_computation.2 | async-start | bytes 4456448 | tf_op jit(solution)/shard_map/all_gather | solution.py:758
  114.0 46.0 %collective-permute-start.7 = (bf16[512,1024]{1,0:T(8,128)(2,1)S(1)}, bf16[512,1024]{1,0:T(8,128)(2,1)S(1)}, u32[]{:S(2)}, u32[]{:S(2)}) collective-permute-start(bf16[512,1024]{1,0:T(8,128)(2,1)S(1)} %collective-permute-done.5), channel_id=1, source_target_pairs={{0,4},{2,6},{4,0},{6,2},{8,12},{10,14},{12,8},{14,10},{16,20},{18,... | collective-permute-start | bytes 3145736 | tf_op jit(solution)/shard_map/ppermute | solution.py:452
  171.3 117.2 %collective-permute-start.9 = (bf16[512,1024]{1,0:T(8,128)(2,1)S(1)}, bf16[512,1024]{1,0:T(8,128)(2,1)}, u32[]{:S(2)}, u32[]{:S(2)}) collective-permute-start(bf16[512,1024]{1,0:T(8,128)(2,1)S(1)} %dynamic-slice_bitcast_fusion), channel_id=1, source_target_pairs={{0,1},{1,0},{2,3},{3,2},{4,5},{5,4},{6,7},{7,6},{8,9},{9,8},{10,11... | collective-permute-start | bytes 3145736 | tf_op jit(solution)/shard_map/ppermute | solution.py:448
  371.4 64.9 %collective-permute-start.15 = (bf16[512,1024]{1,0:T(8,128)(2,1)}, bf16[512,1024]{1,0:T(8,128)(2,1)}, u32[]{:S(2)}, u32[]{:S(2)}) collective-permute-start(bf16[512,1024]{1,0:T(8,128)(2,1)} %bitcast.45), channel_id=1, source_target_pairs={{0,1},{1,0},{2,3},{3,2},{4,5},{5,4},{6,7},{7,6},{8,9},{9,8},{10,11... | collective-permute-start | bytes 3145736 | tf_op jit(solution)/shard_map/ppermute | solution.py:448
  398.0 38.7 %collective-permute-start.17 = (bf16[256,1024]{1,0:T(8,128)(2,1)}, bf16[256,1024]{1,0:T(8,128)(2,1)}, u32[]{:S(2)}, u32[]{:S(2)}) collective-permute-start(bf16[256,1024]{1,0:T(8,128)(2,1)} %bitcast.50), channel_id=1, source_target_pairs={{0,2},{2,0},{4,6},{6,4},{8,10},{10,8},{12,14},{14,12},{16,18},{18,... | collective-permute-start | bytes 1572872 | tf_op jit(solution)/shard_map/ppermute | solution.py:452
  403.8 102.9 %collective-permute-start.24 = (bf16[256,2048]{1,0:T(8,128)(2,1)}, bf16[256,2048]{1,0:T(8,128)(2,1)}, u32[]{:S(2)}, u32[]{:S(2)}) collective-permute-start(bf16[256,2048]{1,0:T(8,128)(2,1)} %bitcast.68), channel_id=1, source_target_pairs={{0,4},{2,6},{4,0},{6,2},{8,12},{10,14},{12,8},{14,10},{16,20},{18,... | collective-permute-start | bytes 3145736 | tf_op jit(solution)/shard_map/ppermute | solution.py:452
  443.5 64.4 %collective-permute-start.25 = (bf16[128,1024]{1,0:T(8,128)(2,1)}, bf16[128,1024]{1,0:T(8,128)(2,1)}, u32[]{:S(2)}, u32[]{:S(2)}) collective-permute-start(bf16[128,1024]{1,0:T(8,128)(2,1)} %bitcast.69), channel_id=1, source_target_pairs={{0,1},{1,0},{2,3},{3,2},{4,5},{5,4},{6,7},{7,6},{8,9},{9,8},{10,11... | collective-permute-start | bytes 786440 | tf_op jit(solution)/shard_map/ppermute | solution.py:448
  506.7 43.7 %collective-permute-start.30 = (f32[28,1024]{1,0:T(8,128)}, f32[28,1024]{1,0:T(8,128)}, u32[]{:S(2)}, u32[]{:S(2)}) collective-permute-start(f32[28,1024]{1,0:T(8,128)} %pad_maximum_fusion.13), channel_id=1, source_target_pairs={{0,1},{1,0},{2,3},{3,2},{4,5},{5,4},{6,7},{7,6},{8,9},{9,8},{10,11... | collective-permute-start | bytes 344072 | tf_op jit(solution)/shard_map/ppermute | solution.py:448
  527.9 204.2 %all-gather.21.cloned.1.call-start = ((), (), s32[]{:S(2)}) async-start(), calls=%async_computation.3 | async-start | bytes 4456448 | tf_op jit(solution)/shard_map/all_gather | solution.py:758
  558.1 39.0 %collective-permute-start.36 = (bf16[1024,1024]{1,0:T(8,128)(2,1)S(1)}, bf16[1024,1024]{1,0:T(8,128)(2,1)}, u32[]{:S(2)}, u32[]{:S(2)}) collective-permute-start(bf16[1024,1024]{1,0:T(8,128)(2,1)S(1)} %constant_dynamic-slice_fusion.42), channel_id=1, source_target_pairs={{0,2},{2,0},{4,6},{6,4},{8,10},{10,8},{12,14},{14,12},{16,18},{18,... | collective-permute-start | bytes 6291464 | tf_op jit(solution)/shard_map/ppermute | solution.py:452
  558.2 39.9 %collective-permute-start.35 = (bf16[1024,1024]{1,0:T(8,128)(2,1)}, bf16[1024,1024]{1,0:T(8,128)(2,1)}, u32[]{:S(2)}, u32[]{:S(2)}) collective-permute-start(bf16[1024,1024]{1,0:T(8,128)(2,1)} %convolution_convert_fusion.16), channel_id=1, source_target_pairs={{0,2},{2,0},{4,6},{6,4},{8,10},{10,8},{12,14},{14,12},{16,18},{18,... | collective-permute-start | bytes 6291464 | tf_op jit(solution)/shard_map/ppermute | solution.py:452
  584.9 57.6 %collective-permute-start.38 = (bf16[256,1536]{1,0:T(8,128)(2,1)}, bf16[256,1536]{1,0:T(8,128)(2,1)}, u32[]{:S(2)}, u32[]{:S(2)}) collective-permute-start(bf16[256,1536]{1,0:T(8,128)(2,1)} %bitcast.95), channel_id=1, source_target_pairs={{0,4},{2,6},{4,0},{6,2},{8,12},{10,14},{12,8},{14,10},{16,20},{18,... | collective-permute-start | bytes 2359304 | tf_op jit(solution)/shard_map/ppermute | solution.py:452
  605.1 169.8 %all-gather.23.cloned.1.call-start = ((), (), s32[]{:S(2)}) async-start(), calls=%async_computation.4 | async-start | bytes 1114112 | tf_op jit(solution)/shard_map/all_gather | solution.py:758
  608.9 63.3 %collective-permute-start.44 = (bf16[512,1024]{1,0:T(8,128)(2,1)}, bf16[512,1024]{1,0:T(8,128)(2,1)}, u32[]{:S(2)}, u32[]{:S(2)}) collective-permute-start(bf16[512,1024]{1,0:T(8,128)(2,1)} %bitcast.613), channel_id=1, source_target_pairs={{0,1},{1,0},{2,3},{3,2},{4,5},{5,4},{6,7},{7,6},{8,9},{9,8},{10,11... | collective-permute-start | bytes 3145736 | tf_op jit(solution)/shard_map/ppermute | solution.py:448
  664.0 241.5 %all-gather.25.cloned.1.call-start = ((), (), s32[]{:S(2)}) async-start(), calls=%async_computation.5 | async-start | bytes 3342336 | tf_op jit(solution)/shard_map/all_gather | solution.py:758
  676.2 49.4 %collective-permute-start.51 = (bf16[256,1024]{1,0:T(8,128)(2,1)S(1)}, bf16[256,1024]{1,0:T(8,128)(2,1)S(1)}, u32[]{:S(2)}, u32[]{:S(2)}) collective-permute-start(bf16[256,1024]{1,0:T(8,128)(2,1)S(1)} %bitcast.624), channel_id=1, source_target_pairs={{0,2},{2,0},{4,6},{6,4},{8,10},{10,8},{12,14},{14,12},{16,18},{18,... | collective-permute-start | bytes 1572872 | tf_op jit(solution)/shard_map/ppermute | solution.py:452
  680.7 45.0 %collective-permute-start.48 = (bf16[512,1024]{1,0:T(8,128)(2,1)S(1)}, bf16[512,1024]{1,0:T(8,128)(2,1)}, u32[]{:S(2)}, u32[]{:S(2)}) collective-permute-start(bf16[512,1024]{1,0:T(8,128)(2,1)S(1)} %bitcast.614), channel_id=1, source_target_pairs={{0,4},{2,6},{4,0},{6,2},{8,12},{10,14},{12,8},{14,10},{16,20},{18,... | collective-permute-start | bytes 3145736 | tf_op jit(solution)/shard_map/ppermute | solution.py:452
  683.6 48.4 %collective-permute-start.47 = (bf16[512,1024]{1,0:T(8,128)(2,1)S(1)}, bf16[512,1024]{1,0:T(8,128)(2,1)}, u32[]{:S(2)}, u32[]{:S(2)}) collective-permute-start(bf16[512,1024]{1,0:T(8,128)(2,1)S(1)} %fusion.45), channel_id=1, source_target_pairs={{0,4},{2,6},{4,0},{6,2},{8,12},{10,14},{12,8},{14,10},{16,20},{18,... | collective-permute-start | bytes 3145736 | tf_op jit(solution)/shard_map/ppermute | solution.py:452
  724.1 50.7 %collective-permute-start.55 = (bf16[512,1024]{1,0:T(8,128)(2,1)}, bf16[512,1024]{1,0:T(8,128)(2,1)}, u32[]{:S(2)}, u32[]{:S(2)}) collective-permute-start(bf16[512,1024]{1,0:T(8,128)(2,1)} %bitcast.128), channel_id=1, source_target_pairs={{0,4},{2,6},{4,0},{6,2},{8,12},{10,14},{12,8},{14,10},{16,20},{18,... | collective-permute-start | bytes 3145736 | tf_op jit(solution)/shard_map/ppermute | solution.py:452
  747.3 74.7 %collective-permute-start.64 = (bf16[128,1024]{1,0:T(8,128)(2,1)}, bf16[128,1024]{1,0:T(8,128)(2,1)}, u32[]{:S(2)}, u32[]{:S(2)}) collective-permute-start(bf16[128,1024]{1,0:T(8,128)(2,1)} %bitcast.151), channel_id=1, source_target_pairs={{0,1},{1,0},{2,3},{3,2},{4,5},{5,4},{6,7},{7,6},{8,9},{9,8},{10,11... | collective-permute-start | bytes 786440 | tf_op jit(solution)/shard_map/ppermute | solution.py:448
  749.4 194.2 %all-gather.27.cloned.1.call-start = ((), (), s32[]{:S(2)}) async-start(), calls=%async_computation.6 | async-start | bytes 4456448 | tf_op jit(solution)/shard_map/all_gather | solution.py:758
  836.2 47.4 %collective-permute-start.67 = (bf16[512,1024]{1,0:T(8,128)(2,1)S(1)}, bf16[512,1024]{1,0:T(8,128)(2,1)}, u32[]{:S(2)}, u32[]{:S(2)}) collective-permute-start(bf16[512,1024]{1,0:T(8,128)(2,1)S(1)} %copy-done.97), channel_id=1, source_target_pairs={{0,1},{1,0},{2,3},{3,2},{4,5},{5,4},{6,7},{7,6},{8,9},{9,8},{10,11... | collective-permute-start | bytes 3145736 | tf_op jit(solution)/shard_map/ppermute | solution.py:448
  (270 other events, 3543.6 us)
Sparse Core Ops, SparseCore 0:
  19.3 52.0 all-gather.14
  73.7 120.1 all-gather.16
  528.0 51.5 all-gather.18
  605.2 49.3 all-gather.20
  664.2 44.2 all-gather.22
  749.5 52.6 all-gather.24
  820.5 56.3 all-gather.26

commit v4 on v3

--- a/solution.py
+++ b/solution.py
@@ -484,12 +484,10 @@
 
 def gelu_pair(hidden):
     square = hidden * hidden
-    inner = 0.7978845608 * hidden * (1.0 + 0.044715 * square)
-    bent = jnp.tanh(inner)
-    value = 0.5 * hidden * (1.0 + bent)
-    slope = 0.5 * (1.0 + bent) + 0.5 * hidden * (1.0 - bent * bent) * 0.7978845608 * (
-        1.0 + 3.0 * 0.044715 * square
-    )
+    share = 0.5 + 0.5 * jnp.tanh(hidden * (0.7978845608 + (0.7978845608 * 0.044715) * square))
+    value = hidden * share
+    rate = 2.0 * 0.7978845608 + (6.0 * 0.7978845608 * 0.044715) * square
+    slope = share + (value * rate) * (1.0 - share)
     return value.astype(bf16), slope.astype(bf16)
 
 
@@ -580,9 +578,9 @@
     )(place.reshape(1).astype(jnp.int32), *arrays)
 
 
-def unpack_kernel(in_ref, *refs):
+def unpack_kernel(count, side_ref, in_ref, *refs):
     at = 0
-    for ref in refs:
+    for ref in refs[-count:]:
         rows = ref.shape[0] // in_ref.shape[0]
         for part in range(ref.shape[1] // PACK_WIDTH):
             for block in range(in_ref.shape[0]):
@@ -592,75 +590,174 @@
             at += rows
 
 
-def unpack_halves(gathered, shapes):
+def unpack_halves(side, gathered, shapes, bases=()):
     dp_size, total, _ = gathered.shape
     some = max(1, dp_size // 4)
+    steps = dp_size // some
+    out_specs, out_shape = [], []
+    for index, (height, width) in enumerate(shapes):
+        base = index - (len(shapes) - len(bases))
+        block = (height // steps, width)
+        if base < 0:
+            out_specs.append(pl.BlockSpec(block, lambda step, side_ref: (step, 0)))
+            out_shape.append(jax.ShapeDtypeStruct((height, width), bf16))
+            continue
+        if bases[base].shape[0] == height:
+            out_specs.append(pl.BlockSpec(block, lambda step, side_ref: (step, 1 - side_ref[0])))
+        else:
+            out_specs.append(pl.BlockSpec(block, lambda step, side_ref: ((1 - side_ref[0]) * steps + step, 0)))
+        out_shape.append(jax.ShapeDtypeStruct(bases[base].shape, bf16))
     return pl.pallas_call(
-        unpack_kernel,
-        grid=(dp_size // some,),
-        in_specs=[pl.BlockSpec((some, total, PACK_WIDTH), lambda step: (step, 0, 0))],
-        out_specs=[
-            pl.BlockSpec((height // dp_size * some, width), lambda step: (step, 0)) for height, width in shapes
-        ],
-        out_shape=[jax.ShapeDtypeStruct(shape, bf16) for shape in shapes],
+        partial(unpack_kernel, len(shapes)),
+        grid_spec=pltpu.PrefetchScalarGridSpec(
+            num_scalar_prefetch=1,
+            grid=(steps,),
+            in_specs=[pl.BlockSpec((some, total, PACK_WIDTH), lambda step, side_ref: (step, 0, 0))]
+            + [pl.BlockSpec(memory_space=pl.ANY)] * len(bases),
+            out_specs=out_specs,
+        ),
+        out_shape=out_shape,
+        input_output_aliases={2 + base: len(shapes) - len(bases) + base for base in range(len(bases))},
         compiler_params=pltpu.CompilerParams(vmem_limit_bytes=32 * 2**20),
         cost_estimate=pl.CostEstimate(
             flops=0, bytes_accessed=4 * dp_size * total * PACK_WIDTH, transcendentals=0
         ),
         name="unpack_halves",
-    )(gathered)
-
-
-def place_kernel(kind, whole_ref, *refs):
+    )(side.reshape(1).astype(jnp.int32), gathered, *bases)
+
+
+def fill_kernel(side_ref, up_ref, down_ref, up_out, down_out):
+    up_out[...] = up_ref[0]
+    down_out[...] = down_ref[0]
+
+
+def fill_whole(side, w_up, w_down, layer):
+    steps = 4
+    _, height, width = w_up.shape
+    up_rows, down_rows = height // steps, width // steps
+    return pl.pallas_call(
+        fill_kernel,
+        grid_spec=pltpu.PrefetchScalarGridSpec(
+            num_scalar_prefetch=1,
+            grid=(steps,),
+            in_specs=[
+                pl.BlockSpec((1, up_rows, width), lambda step, side_ref: (layer, step, 0)),
+                pl.BlockSpec((1, down_rows, height), lambda step, side_ref: (layer, step, 0)),
+            ],
+            out_specs=[
+                pl.BlockSpec((up_rows, width), lambda step, side_ref: (step, side_ref[0])),
+                pl.BlockSpec((down_rows, height), lambda step, side_ref: (side_ref[0] * steps + step, 0)),
+            ],
+        ),
+        out_shape=[
+            jax.ShapeDtypeStruct((height, 2 * width), bf16),
+            jax.ShapeDtypeStruct((2 * width, height), bf16),
+        ],
+        compiler_params=pltpu.CompilerParams(vmem_limit_bytes=32 * 2**20),
+        cost_estimate=pl.CostEstimate(flops=0, bytes_accessed=8 * height * width, transcendentals=0),
+        name="fill_whole",
+    )(side.reshape(1).astype(jnp.int32), w_up, w_down)
+
+
+def place_joint_kernel(whole_ref, *refs):
+    qkv_out, out_out = refs[-2:]
+    for block in range(whole_ref.shape[0]):
+        rows = qkv_out.shape[2] // whole_ref.shape[0]
+        for part in range(3):
+            qkv_out[0, part, block * rows : (block + 1) * rows, :] = whole_ref[
+                block, part * rows : (part + 1) * rows, :
+            ].astype(f32)
+        at, rows = 3 * rows, out_out.shape[1] // whole_ref.shape[0]
+        for part in range(out_out.shape[2] // PACK_WIDTH):
+            out_out[0, block * rows : (block + 1) * rows, part * PACK_WIDTH : (part + 1) * PACK_WIDTH] = whole_ref[
+                block, at + part * rows : at + (part + 1) * rows, :
+            ].astype(f32)
+
+
+def place_joint(whole, layer, qkv_shape, out_shape, bases):
+    dp_size, total, _ = whole.shape
+    some = dp_size // 4
+    operands, in_specs, aliases = [whole], [pl.BlockSpec((some, total, PACK_WIDTH), lambda step: (step, 0, 0))], {}
+    if bases is not None:
+        operands += bases
+        in_specs += [pl.BlockSpec(memory_space=pl.ANY)] * 2
+        aliases = {1: 0, 2: 1}
+    return pl.pallas_call(
+        place_joint_kernel,
+        grid=(4,),
+        in_specs=in_specs,
+        out_specs=[
+            pl.BlockSpec((1, 3, qkv_shape[0] // 4, qkv_shape[1] // 3), lambda step: (layer, 0, step, 0)),
+            pl.BlockSpec((1, out_shape[0] // 4, out_shape[1]), lambda step: (layer, step, 0)),
+        ],
+        out_shape=[
+            jax.ShapeDtypeStruct((2, 3, qkv_shape[0], qkv_shape[1] // 3), f32),
+            jax.ShapeDtypeStruct((2,) + tuple(out_shape), f32),
+        ],
+        input_output_aliases=aliases,
+        compiler_params=pltpu.CompilerParams(vmem_limit_bytes=32 * 2**20),
+        cost_estimate=pl.CostEstimate(flops=0, bytes_accessed=6 * dp_size * total * PACK_WIDTH, transcendentals=0),
+        name="place_joint",
+    )(*operands)
+
+
+def place_pair_kernel(whole_ref, up_out, down_out):
+    for block in range(whole_ref.shape[0]):
+        rows = whole_ref.shape[2]
+        down_out[0, block * rows : (block + 1) * rows, :] = whole_ref[block, 0].astype(f32)
+        up_out[0, :, block * rows : (block + 1) * rows] = whole_ref[block, 1].astype(f32).T
+
+
+def place_pair(whole, layer):
+    dp_size, rows, columns = whole.shape
+    rows = rows // 2
+    some = dp_size // 4
+    return pl.pallas_call(
+        place_pair_kernel,
+        grid=(4,),
+        in_specs=[pl.BlockSpec((some, 2, rows, columns), lambda step: (step, 0, 0, 0))],
+        out_specs=[
+            pl.BlockSpec((1, columns, some * rows), lambda step: (layer, 0, step)),
+            pl.BlockSpec((1, some * rows, columns), lambda step: (layer, step, 0)),
+        ],
+        out_shape=[
+            jax.ShapeDtypeStruct((2, columns, dp_size * rows), f32),
+            jax.ShapeDtypeStruct((2, dp_size * rows, columns), f32),
+        ],
+        compiler_params=pltpu.CompilerParams(vmem_limit_bytes=40 * 2**20),
+        cost_estimate=pl.CostEstimate(flops=0, bytes_accessed=12 * dp_size * rows * columns, transcendentals=0),
+        name="place_pair",
+    )(whole.reshape(dp_size, 2, rows, columns))
+
+
+def place_kernel(whole_ref, *refs):
     out_ref = refs[-1]
-    block = whole_ref[...].reshape(-1, whole_ref.shape[-1]).astype(f32)
-    if kind == "qkv":
-        width = block.shape[1] // 3
-        for part in range(3):
-            out_ref[0, part] = block[:, part * width : (part + 1) * width]
+    out_ref[0] = whole_ref[...].reshape(-1, whole_ref.shape[-1]).astype(f32)
+
+
+def place_quarters(kind, whole, which, layer, base):
+    dp_size, rows, columns = whole.shape
+    half, some, rows = dp_size // 2, dp_size // 4, rows // 2
+    if kind == "down":
+        out_spec = pl.BlockSpec((1, some * rows, columns), lambda step: (layer, step, 0))
     else:
-        out_ref[0] = block
-
-
-def place_grad(kind, whole, layer, split, base):
-    dp_size, rows, columns = whole.shape
-    half, some = dp_size // 2, dp_size // 4
-    whole = whole.reshape(half, 2, rows, columns)
-    if split == "rows":
-        block, source = (some, 2, rows, columns), lambda step: (step, 0, 0, 0)
-        steps = half // some
-        tall = some * 2 * rows
-        if kind == "qkv":
-            out_shape = (2, 3, dp_size * rows, columns // 3)
-            out_spec = pl.BlockSpec((1, 3, tall, columns // 3), lambda step: (layer, 0, step, 0))
-        else:
-            out_shape = (2, dp_size * rows, columns)
-            out_spec = pl.BlockSpec((1, tall, columns), lambda step: (layer, step, 0))
-    else:
-        block, source = (some, None, rows, columns), lambda step: (step % 2, step // 2, 0, 0)
-        steps = 4
-        if kind == "down":
-            out_shape = (2, dp_size * rows, columns)
-            out_spec = pl.BlockSpec((1, some * rows, columns), lambda step: (layer, step, 0))
-        else:
-            out_shape = (2, half * rows, 2 * columns)
-            out_spec = pl.BlockSpec((1, some * rows, columns), lambda step: (layer, step % 2, step // 2))
-    operands, in_specs, aliases = [whole], [pl.BlockSpec(block, source)], {}
-    if base is not None:
-        operands.append(base)
-        in_specs.append(pl.BlockSpec(memory_space=pl.ANY))
-        aliases = {1: 0}
+        out_spec = pl.BlockSpec((1, some * rows, columns), lambda step: (layer, step % 2, step // 2))
     return pl.pallas_call(
-        partial(place_kernel, kind),
-        grid=(steps,),
-        in_specs=in_specs,
+        place_kernel,
+        grid=(4,),
+        in_specs=[
+            pl.BlockSpec(
+                (some, None, None, rows, columns), lambda step: (step % 2, step // 2, which, 0, 0)
+            ),
+            pl.BlockSpec(memory_space=pl.ANY),
+        ],
         out_specs=out_spec,
-        out_shape=jax.ShapeDtypeStruct(out_shape, f32),
-        input_output_aliases=aliases,
+        out_shape=jax.ShapeDtypeStruct(base.shape, f32),
+        input_output_aliases={1: 0},
         compiler_params=pltpu.CompilerParams(vmem_limit_bytes=32 * 2**20),
         cost_estimate=pl.CostEstimate(flops=0, bytes_accessed=6 * dp_size * rows * columns, transcendentals=0),
         name="place_" + kind,
-    )(*operands)
+    )(whole.reshape(half, 2, 2, rows, columns), base)
 
 
 def frame_kernel(side_ref, mine_ref, other_ref, out_ref):
@@ -693,6 +790,13 @@
     return block.reshape(-1, block.shape[-1])
 
 
+def join_level(here, kept, arrived):
+    first = jnp.where(here == 0, kept, arrived)
+    second = jnp.where(here == 0, arrived, kept)
+    joined = jnp.stack([first, second], axis=1)
+    return joined.reshape((-1,) + joined.shape[2:])
+
+
 class Chain:
     def __init__(self, place, dp_size, rows, columns, kind, gather):
         self.place, self.dp_size, self.kind, self.gather = place, dp_size, kind, gather
@@ -756,6 +860,9 @@
             self.kept, self.state = total, "gather"
             if self.gather == "native":
                 self.flight = [lax.all_gather(total, "dp", axis=0, tiled=False)]
+                return
+            if self.gather is None:
+                self.flight, self.state = [], "done"
                 return
             self.kept, self.level = total[None], index - 1
             self.flight = [self.swap(self.kept, self.level)]
@@ -782,16 +889,54 @@
         elif self.gather == "native":
             self.whole, self.flight, self.state = arrived[0], [], "done"
         else:
-            here = self.bit(self.level)
-            first = jnp.where(here == 0, self.kept, arrived[0])
-            second = jnp.where(here == 0, arrived[0], self.kept)
-            joined = jnp.stack([first, second], axis=1)
-            self.kept = joined.reshape((-1,) + joined.shape[2:])
+            self.kept = join_level(self.bit(self.level), self.kept, arrived[0])
             self.level -= 1
             if self.level < 0:
                 self.whole, self.flight, self.state = self.kept, [], "done"
             else:
                 self.flight = [self.swap(self.kept, self.level)]
+
+
+class Scatter:
+    def __init__(self, block):
+        self.flight = [lax.psum_scatter(block, ("tensor", "dp"), scatter_dimension=0, tiled=True)]
+        self.state = "sum"
+
+    def advance(self, arrived):
+        if self.state == "sum":
+            self.flight, self.state = [lax.all_gather(arrived[0], "dp", axis=0, tiled=False)], "gather"
+        elif self.state == "gather":
+            self.whole, self.flight, self.state = arrived[0], [], "done"
+
+
+class Gather:
+    def __init__(self, qkv, out, width, native):
+        assert qkv.state == "done" and out.state == "done"
+        pieces = []
+        for block in (qkv.kept, out.kept):
+            for at in range(0, block.shape[1], width):
+                pieces.append(lax.slice_in_dim(block, at, at + width, axis=1))
+        self.kept = jnp.concatenate(pieces, axis=0)
+        self.native, self.bit, self.swap = native, qkv.bit, qkv.swap
+        self.state = "going"
+        if native:
+            self.flight = [lax.all_gather(self.kept, "dp", axis=0, tiled=False)]
+        else:
+            self.kept, self.level = self.kept[None], qkv.bit_count - 1
+            self.flight = [self.swap(self.kept, self.level)]
+
+    def advance(self, arrived):
+        if self.state == "done":
+            return
+        if self.native:
+            self.whole, self.flight, self.state = arrived[0], [], "done"
+            return
+        self.kept = join_level(self.bit(self.level), self.kept, arrived[0])
+        self.level -= 1
+        if self.level < 0:
+            self.whole, self.flight, self.state = self.kept, [], "done"
+        else:
+            self.flight = [self.swap(self.kept, self.level)]
 
 
 class Spread:
@@ -877,8 +1022,8 @@
     def gathered(arrived):
         return lax.all_gather(arrived, "dp", axis=0, tiled=False)
 
-    def unpacked(whole, kinds):
-        return dict(zip(kinds, unpack_halves(whole, [flat_shape[kind] for kind in kinds])))
+    def unpacked(whole, kinds, bases=()):
+        return dict(zip(kinds, unpack_halves(side, whole, [flat_shape[kind] for kind in kinds], bases)))
 
     attn_kinds, all_kinds = ("qkv", "out"), ("qkv", "out", "up", "down")
     first_pack = swap_tensor(packed(0, attn_kinds))
@@ -888,8 +1033,9 @@
     up_send = row_half(quarter_of("up", w_up[0], core), near_row)
     down_send = row_half(quarter_of("down", w_down[0], core), near_row)
     own_qkv = [flat_qkv(stacked, layer) for layer in range(2)]
-    other_rows, second_send, up_send, down_send, own_qkv = pin(
-        other_rows, second_send, up_send, down_send, own_qkv
+    filled = fill_whole(side, w_up, w_down, 1)
+    other_rows, second_send, up_send, down_send, own_qkv, filled = pin(
+        other_rows, second_send, up_send, down_send, own_qkv, filled
     )
     second_pack = swap_tensor(second_send)
     rows = whole_rows(frames_in, other_rows).astype(f32)
@@ -931,7 +1077,7 @@
     mine = dot_low(normed, own_qkv[1], NN)
     mix_mine = attn_fwd(mine, limits, False, 512)
     mix_mine, second_whole = pin(mix_mine, second_whole)
-    second = unpacked(second_whole, all_kinds)
+    second = unpacked(second_whole, all_kinds, filled)
     weights = [
         {
             "qkv": [own_qkv[0], first["qkv"]],
@@ -942,8 +1088,8 @@
         {
             "qkv": [own_qkv[1], second["qkv"]],
             "out": [w_out[1], second["out"]],
-            "up": [w_up[1], second["up"]],
-            "down": [w_down[1], second["down"]],
+            "up": [second["up"]],
+            "down": [second["down"]],
         },
     ]
     theirs = dot_low(normed, second["qkv"], NN)
@@ -1014,103 +1160,105 @@
         norm_sums[layer][part] = (grad_gain, grad_shift)
         return grad_rows + added
 
-    down1, up1 = chain("down", "x", "native"), chain("up", "y", "native")
-    out1, qkv1 = chain("out", "x", "native"), chain("qkv", "y", "native")
-    down0, up0 = chain("down", "x", "native", "core"), chain("up", "y", "swaps", "core")
-    out0, qkv0 = chain("out", "x", "swaps"), chain("qkv", "y", "swaps")
+    out1, qkv1 = chain("out", "x", None), chain("qkv", "y", None)
+    down0, up0 = chain("down", "x", None, "core"), chain("up", "y", None, "core")
+    out0, qkv0 = chain("out", "x", None), chain("qkv", "y", None)
 
     low = grad_rows.astype(bf16)
-    parts = down_grads(1, low)
+    (down_part,) = down_grads(1, low)
     hidden = hidden_grads(1, low)
-    parts, hidden, grad_rows = pin(parts, hidden, grad_rows)
-    down1.start_rows(*parts)
-    parts = up_grads(1, hidden)
-    parts, hidden, grad_rows = move((parts, hidden, grad_rows), down1)
-    up1.start_rows(*parts)
+    down_part, hidden, grad_rows = pin(down_part, hidden, grad_rows)
+    up_part = dot_low(hidden[0], kept[3][0], TN)
+    both_parts = jnp.concatenate(
+        [part.reshape(2 * dp_size, -1, model_width) for part in (down_part, up_part)], axis=1
+    )
+    both_parts, hidden, grad_rows = pin(both_parts, hidden, grad_rows)
+    pair1 = Scatter(flat_rows(both_parts))
     grad_normed = dot_sum(list(zip(hidden, weights[1]["up"])), NT)
     grad_rows = norm_step(1, 1, grad_rows, grad_normed)
     low = grad_rows.astype(bf16)
     out_parts = out_grads(1, low)
     mine, theirs = mixed_grads(1, low)
-    out_parts, mine, theirs, grad_rows = move((out_parts, mine, theirs, grad_rows), down1, hold=[up1])
+    theirs = attention_grad(1, 1, theirs)
+    out_parts, mine, theirs, grad_rows = pin(out_parts, mine, theirs, grad_rows)
     out1.start_rows(*out_parts)
-    theirs = attention_grad(1, 1, theirs)
-    mine, theirs, grad_rows = move((mine, theirs, grad_rows), down1, up1, out1)
     mine = attention_grad(1, 0, mine)
-    mine, theirs, grad_rows = move((mine, theirs, grad_rows), down1, up1, out1)
     parts = [dot_low(kept[2][0], part, TN) for part in (mine, theirs)]
+    parts, mine, theirs, grad_rows = move((parts, mine, theirs, grad_rows), hold=[out1])
+    qkv1.start_rows(*parts)
+    out_there = swap_tensor(out_away)
     grad_normed = dot_sum(list(zip((mine, theirs), weights[1]["qkv"])), NT)
     grad_rows = norm_step(1, 0, grad_rows, grad_normed)
-    early = Spread(
-        jnp.concatenate(
-            [picker * norm_sums[1][part][which][None] for which in range(2) for part in range(2)]
-        ),
-        dp_size,
-    )
     low = grad_rows.astype(bf16)
-    parts, low, grad_rows = move((parts, low, grad_rows), down1, up1, out1)
-    qkv1.start_rows(*parts)
     parts = down_grads(0, low)
-    parts, low, grad_rows = move((parts, low, grad_rows), up1, qkv1, early)
+    parts, low, grad_rows = move((parts, low, grad_rows), out1, qkv1)
     start_quarters(down0, "down", parts)
     hidden = hidden_grads(0, low)
-    hidden, grad_rows = move((hidden, grad_rows), down1, up1, qkv1, out1, early, hold=[down0])
+    hidden, grad_rows, out_there = move((hidden, grad_rows, out_there), qkv1, out1, hold=[down0])
     parts = up_grads(0, hidden)
     grad_normed = dot_sum(list(zip(hidden, weights[0]["up"])), NT)
-    parts, grad_normed, grad_rows = move((parts, grad_normed, grad_rows), qkv1, out1, down0, early)
+    parts, grad_normed, grad_rows = move((parts, grad_normed, grad_rows), qkv1, out1, down0, pair1)
     start_quarters(up0, "up", parts)
     grad_rows = norm_step(0, 1, grad_rows, grad_normed)
     low = grad_rows.astype(bf16)
     out_parts = out_grads(0, low)
     mine, theirs = mixed_grads(0, low)
-    out_parts, mine, theirs, grad_rows = move((out_parts, mine, theirs, grad_rows), up0, qkv1, down0, early)
+    out_parts, mine, theirs, grad_rows = move((out_parts, mine, theirs, grad_rows), up0, qkv1, out1)
     out0.start_rows(*out_parts)
     theirs = attention_grad(0, 1, theirs)
-    mine, theirs, grad_rows = move((mine, theirs, grad_rows), up1, down0, up0, qkv1, early, hold=[out0])
     part_theirs = dot_low(kept[0][0], theirs, TN)
+    part_theirs, mine, theirs, grad_rows = move(
+        (part_theirs, mine, theirs, grad_rows), down0, up0, qkv1, out1, hold=[out0]
+    )
+    joint1 = Gather(qkv1, out1, PACK_WIDTH, True)
     qkv0.start_other(part_theirs)
     mine = attention_grad(0, 0, mine)
-    mine, theirs, grad_rows = move((mine, theirs, grad_rows), out1, down0, up0, qkv0)
     part_mine = dot_low(kept[0][0], mine, TN)
+    part_mine, mine, theirs, grad_rows = move(
+        (part_mine, mine, theirs, grad_rows), down0, up0, out0, qkv0
+    )
     qkv0.add_own(part_mine)
     grad_normed = dot_sum([(mine, weights[0]["qkv"][0]), (theirs, weights[0]["qkv"][1])], NT)
     grad_rows = norm_step(0, 0, grad_rows, grad_normed)
     grad_mine, grad_away = halves_of(grad_rows)
     late = Spread(
-        jnp.stack([norm_sums[0][part][which] for which in range(2) for part in range(2)]), dp_size
+        jnp.concatenate(
+            [jnp.stack([norm_sums[0][part][which] for which in range(2) for part in range(2)])]
+            + [picker * norm_sums[1][part][which][None] for which in range(2) for part in range(2)]
+        ),
+        dp_size,
     )
-    both_away = (grad_away, out_away)
-    both_away, grad_mine = move((both_away, grad_mine), qkv0, up0, down0, out0)
-    both_away, grad_mine = move((both_away, grad_mine), qkv0, up0, out0, late)
-    there = [swap_tensor(block) for block in both_away]
-    there, grad_mine = move((there, grad_mine), qkv0, up0, out0, late)
-    (grad_mine,) = move((grad_mine,), qkv1, qkv0, up0, out0, late)
-
-    def placed(kind, one):
-        return place_grad(kind, one.whole, 1, "rows", None)
-
-    bases = {"down": placed("down", down1), "up": placed("up", up1)}
-    bases, grad_mine = move((bases, grad_mine), qkv0, up0, out0, late)
-    bases["out"], bases["qkv"] = placed("out", out1), placed("qkv", qkv1)
-    bases, grad_mine = move((bases, grad_mine), down0, qkv0, up0, out0)
-    frames_grad = place_frames(side, grad_mine, there[0])
-    frames_out = place_frames(side, out_mine, there[1])
-    frames_grad, frames_out = move((frames_grad, frames_out), qkv0, up0, out0)
-    for one in (qkv0, up0, out0, down0, late, down1, up1, out1, qkv1, early):
-        while one.flight:
-            one.advance(one.flight)
-
-    def both(kind, sooner, split="rows"):
-        return place_grad(kind, sooner.whole, 0, split, bases[kind])
-
-    gain_rows = early.block.reshape(4, section_count, model_width)
+    frames_out = place_frames(side, out_mine, out_there)
+    grad_away, grad_mine, frames_out = move((grad_away, grad_mine, frames_out), qkv0, up0, down0, out0, pair1, late)
+    grad_away, grad_mine = move((grad_away, grad_mine), qkv0, up0, down0, out0, late)
+    pair0 = Gather(down0, up0, model_width, True)
+    grad_there = swap_tensor(grad_away)
+    bases = dict(zip(("up", "down"), place_pair(pair1.whole, 1)))
+    bases, grad_mine, grad_there = move((bases, grad_mine, grad_there), qkv0, out0, late)
+    (grad_mine,) = move((grad_mine,), qkv0, out0, late, joint1)
+    joint0 = Gather(qkv0, out0, PACK_WIDTH, False)
+    shapes = (flat_shape["qkv"], flat_shape["out"])
+    joint_bases = place_joint(joint1.whole, 1, *shapes, None)
+    frames_grad = place_frames(side, grad_mine, grad_there)
+    joint_bases, frames_grad = move((joint_bases, frames_grad), joint0, late)
+    joint_bases, frames_grad = move((joint_bases, frames_grad), joint0, late)
+    (joint_bases,) = move((joint_bases,), joint0, pair0)
+    grad_up = place_quarters("up", pair0.whole, 1, 0, bases["up"])
+    grad_down = place_quarters("down", pair0.whole, 0, 0, bases["down"])
+    while joint0.flight:
+        joint0.advance(joint0.flight)
+    while late.flight:
+        late.advance(late.flight)
+    grad_qkv, grad_out = place_joint(joint0.whole, 0, *shapes, list(joint_bases))
+
+    gain_rows = late.block[4:].reshape(4, section_count, model_width)
     return (
         frames_out,
         frames_grad,
-        both("qkv", qkv0).transpose(0, 2, 1, 3),
-        both("out", out0),
-        both("up", up0, "core"),
-        both("down", down0, "core"),
+        grad_qkv.transpose(0, 2, 1, 3),
+        grad_out,
+        grad_up,
+        grad_down,
         late.block[0:2],
         late.block[2:4],
         gain_rows[0:2],

time: 1000 us -> 955 us (0.955)
  matrix products: 285 us -> 245 us
  waiting for transfers between devices: 176 us -> 212 us
  starting transfers between devices: 86.3 us -> 53.5 us
  other arithmetic: 111 us -> 90.2 us
    ppermute x68 -> x45, waiting for transfers between devices: 95 us -> 178 us  [swap_bit(): lax.ppermute(block, 'dp', [(place, place ^ 1 << bit) for place in range(d...]
    ppermute x22 -> x18, waiting for transfers between devices: 81.3 us -> 23.4 us  [swap_tensor(): return lax.ppermute(block, 'tensor', [(0, 1), (1, 0)])]
    ppermute x68 -> x45, starting transfers between devices: 58.7 us -> 34.2 us  [swap_bit(): lax.ppermute(block, 'dp', [(place, place ^ 1 << bit) for place in range(d...]
    unnamed x396 -> x366, local copies, waits for them, and re-layouts: 35 us -> 53.3 us
    dot_general x18 -> x16, matrix products: 99.6 us -> 82.9 us  [dot_sum(): term = lax.dot_general(left, right, dims, preferred_element_type=f32)]
    convert_element_type x37 -> x30, other arithmetic: 47.4 us -> 32 us  [add_rounded(): return (left.astype(f32) + right.astype(f32)).astype(bf16)]
    dynamic_slice x36 -> x26, local copies, waits for them, and re-layouts: 37 us -> 23.7 us  [take_axis(): return lax.dynamic_index_in_dim(block, index, 1, keepdims=False)]
    reduce_scatter x0 -> x1, waiting for transfers between devices: none -> 10.9 us  [__init__(): lax.psum_scatter(block, ('tensor', 'dp'), scatter_dimension=0, tiled=True)]
  transfers between devices with their start and end apart: 97 -> 69, of which waited for: 26 -> 22; matrix products, arithmetic and copies ran while one was open for 40% -> 35% of each run, Pallas kernels for 22% -> 23%
where the time goes in v4:
time: 955 us; the launch traced here: 948 us
  matrix products  245 us (26%)
  Pallas kernels  221 us (23%)
  waiting for transfers between devices  212 us (22%)
  local copies, waits for them, and re-layouts  108 us (11%)
  other arithmetic  90.2 us (9%)
  starting transfers between devices  53.5 us (6%)
  between operations  17.3 us (2%)
    ppermute x45, waiting for transfers between devices, swap_bit(): lax.ppermute(block, 'dp', [(place, place ^ 1 << bit) for place in range(d...  178 us
    pallas_call x4, Pallas kernels, attn_bwd(): pl.pallas_call(partial(bwd_kernel, causal, bq), grid=(pairs,), in_specs=[...  103 us
    dot_general x24, matrix products, dot_low(): lax.dot_general(left, right, dims, preferred_element_type=f32).astype(bf16)  94.8 us
    dot_general x16, matrix products, dot_sum(): term = lax.dot_general(left, right, dims, preferred_element_type=f32)  82.9 us
    pallas_call x4, Pallas kernels, attn_fwd(): pl.pallas_call(partial(fwd_kernel, causal, bq), grid=(pairs,), in_specs=[...  65.9 us
    unnamed x366, local copies, waits for them, and re-layouts  53.3 us
    ppermute x45, starting transfers between devices, swap_bit(): lax.ppermute(block, 'dp', [(place, place ^ 1 << bit) for place in range(d...  34.2 us
    convert_element_type x30, other arithmetic, add_rounded(): return (left.astype(f32) + right.astype(f32)).astype(bf16)  32 us
  transfers between devices with their start and end apart: 69, of which 22 were waited for; matrix products, arithmetic and copies ran while one was open for 35% of the time, Pallas kernels for 23%

profile of v4, /device:TPU:0, one launch (start us, length us, event | category | flops | bytes accessed | tf_op | source)
XLA Modules:
  0.0 947.6 jit_solution(4609968663487603184)
XLA Ops:
  62.6 10.6 %collective-permute-done.1 = bf16[768,512]{1,0:T(8,128)(2,1)} collective-permute-done((bf16[768,512]{1,0:T(8,128)(2,1)S(1)}, bf16[768,512]{1,0:T(8,128)(2,1)}, u32[]{:S(2)}, u32[]{:S(2)}) %collective-permute-start.1) | collective-permute-done | bytes 786464 | tf_op jit(solution)/shard_map/ppermute | solution.py:448
  77.2 14.0 %attn_fwd_causal.2 = (bf16[1024,512]{1,0:T(8,128)(2,1)S(1)}, f32[4,2,1024]{2,1,0:T(2,128)S(1)}) custom-call(s32[2]{0:T(128)S(1)} %pad_add_fusion.lims_ref, bf16[1024,1536]{1,0:T(8,128)(2,1)S(1)} %convolution_convert_fusion.9.q_ref.k_ref.v_ref, bf16[1024,1536]{1,0:T(8,128)(2,1)S(1)} %convolution_convert_fusion.9.q_ref.k_ref.v_ref, ...), custom_call_target="tpu_custom_call" | custom-call | flops 4194304 | bytes 4194304 | tf_op jit(solution)/shard_map/attn_fwd_causal/pallas_call | solution.py:381
  107.9 14.4 %attn_fwd_causal.3 = (bf16[1024,512]{1,0:T(8,128)(2,1)S(1)}, f32[4,2,1024]{2,1,0:T(2,128)S(1)}) custom-call(s32[2]{0:T(128)S(1)} %pad_add_fusion.lims_ref, bf16[1024,1536]{1,0:T(8,128)(2,1)S(1)} %convolution_convert_fusion.8.q_ref.k_ref.v_ref, bf16[1024,1536]{1,0:T(8,128)(2,1)S(1)} %convolution_convert_fusion.8.q_ref.k_ref.v_ref, ...), custom_call_target="tpu_custom_call" | custom-call | flops 4194304 | bytes 4194304 | tf_op jit(solution)/shard_map/attn_fwd_causal/pallas_call | solution.py:381
  189.4 18.7 %attn_fwd_full.2 = (bf16[1024,512]{1,0:T(8,128)(2,1)S(1)}, f32[4,2,1024]{2,1,0:T(2,128)S(1)}) custom-call(s32[2]{0:T(128)S(1)} %pad_add_fusion.lims_ref, bf16[1024,1536]{1,0:T(8,128)(2,1)S(1)} %convolution_convert_fusion.7.q_ref.k_ref.v_ref, bf16[1024,1536]{1,0:T(8,128)(2,1)S(1)} %convolution_convert_fusion.7.q_ref.k_ref.v_ref, ...), custom_call_target="tpu_custom_call" | custom-call | flops 4194304 | bytes 4194304 | tf_op jit(solution)/shard_map/attn_fwd_full/pallas_call | solution.py:381
  239.2 18.7 %attn_fwd_full.3 = (bf16[1024,512]{1,0:T(8,128)(2,1)S(1)}, f32[4,2,1024]{2,1,0:T(2,128)S(1)}) custom-call(s32[2]{0:T(128)S(1)} %pad_add_fusion.lims_ref, bf16[1024,1536]{1,0:T(8,128)(2,1)S(1)} %convolution_convert_fusion.6.q_ref.k_ref.v_ref, bf16[1024,1536]{1,0:T(8,128)(2,1)S(1)} %convolution_convert_fusion.6.q_ref.k_ref.v_ref, ...), custom_call_target="tpu_custom_call" | custom-call | flops 4194304 | bytes 4194304 | tf_op jit(solution)/shard_map/attn_fwd_full/pallas_call | solution.py:381
  266.1 19.4 %add_convert_fusion = (bf16[1024,4096]{1,0:T(8,128)(2,1)}, bf16[1024,4096]{1,0:T(8,128)(2,1)}) fusion(bf16[1024,1024]{1,0:T(8,128)(2,1)} %add_convert_fusion.6, bf16[1024,4096]{1,0:T(8,128)(2,1)S(1)} %bitcast.390), kind=kOutput, calls=%fused_computation.2 | convolution fusion | flops 8652849152 | bytes 27262976 | tf_op jit(solution)/shard_map/dot_general | solution.py:1101
  285.5 13.7 %convolution_add_fusion = f32[1024,1024]{1,0:T(8,128)} fusion(f32[1024,1024]{1,0:T(8,128)} %copy-done.36, bf16[1024,4096]{1,0:T(8,128)(2,1)} %get-tuple-element.244, bf16[4096,1024]{1,0:T(8,128)(2,1)S(1)} %bitcast.392), kind=kOutput, calls=%fused_computation.113 | convolution fusion | flops 8590983168 | bytes 25165824 | tf_op jit(solution)/shard_map/dot_general | solution.py:497
  300.6 11.3 %convolution_convert_fusion.1 = bf16[4096,1024]{1,0:T(8,128)(2,1)} fusion(bf16[1024,4096]{1,0:T(8,128)(2,1)S(1)} %copy-done.165, bf16[512,1024]{1,0:T(8,128)(2,1)S(1)} %get-tuple-element.451, bf16[512,1024]{1,0:T(8,128)(2,1)S(1)} %get-tuple-element.450), kind=kOutput, calls=%fused_computation.12 | convolution fusion | flops 8598323200 | bytes 18874368 | tf_op jit(solution)/shard_map/dot_general | solution.py:503
  314.3 14.3 %multiply_convert_fusion = bf16[1024,4096]{1,0:T(8,128)(2,1)} fusion(bf16[1024,4096]{1,0:T(8,128)(2,1)} %get-tuple-element.249, bf16[4096,1024]{1,0:T(8,128)(2,1)S(1)} %bitcast.392, bf16[512,1024]{1,0:T(8,128)(2,1)} %copy-done.72, bf16[512,1024]{1,0:T(8,128)(2,1)} %copy-done.71), kind=kOutput, calls=%fused_computation.1 | convolution fusion | flops 8606711808 | bytes 27262976 | tf_op jit(solution)/shard_map/dot_general | solution.py:1134
  328.5 12.9 %convolution_convert_fusion = bf16[4096,1024]{1,0:T(8,128)(2,1)S(1)} fusion(bf16[1024,4096]{1,0:T(8,128)(2,1)} %multiply_convert_fusion, bf16[1024,1024]{1,0:T(8,128)(2,1)} %add_convert_fusion.6), kind=kOutput, calls=%fused_computation.11 | convolution fusion | flops 8594128896 | bytes 18874368 | tf_op jit(solution)/shard_map/dot_general | solution.py:503
  341.4 10.4 %pad_maximum_fusion = bf16[32,256,1024]{2,1,0:T(8,128)(2,1)} fusion(bf16[32,128,1024]{2,1,0:T(8,128)(2,1)S(1)} %bitcast.416, bf16[32,128,1024]{2,1,0:T(8,128)(2,1)} %bitcast.415), kind=kLoop, calls=%fused_computation | loop fusion | flops 33554432 | bytes 33554432 | tf_op jit(solution)/shard_map/concatenate | solution.py:1172
  354.9 16.2 %multiply_reduce_fusion = (f32[1024]{0:T(1024)S(1)}, f32[1024]{0:T(1024)S(1)}, f32[1024]{0:T(1024)S(1)}, f32[1024]{0:T(1024)S(1)}, f32[1024,1024]{1,0:T(8,128)S(1)}) fusion(f32[1024,1024]{1,0:T(8,128)} %copy-done.36, f32[1024]{0:T(1024)S(1)} %broadcast_multiply_fusion.12, f32[1024]{0:T(1024)S(1)} %add_rsqrt_fusion, f32[1024]{0:T(1024)S(1)} %get-tuple-element.420, ...), kind=kOutput, calls=%fused_computation.38 | convolution fusion | flops 8599367680 | bytes 25194496 | tf_op jit(solution)/shard_map/dot_general | solution.py:497
  375.4 29.2 %attn_bwd_full.2 = bf16[1024,1536]{1,0:T(8,128)(2,1)S(1)} custom-call(s32[2]{0:T(128)S(1)} %pad_add_fusion.lims_ref, bf16[1024,1536]{1,0:T(8,128)(2,1)} %copy-done.3, bf16[1024,1536]{1,0:T(8,128)(2,1)} %copy-done.3, bf16[1024,1536]{1,0:T(8,128)(2,1)} %copy-done.3, f32[4,2,1024]{2,1,0:T(2,128)S(1)} %get-tuple-element.259.l_ref, ...), custom_call_target="tpu_custom_call" | custom-call | flops 4194304 | bytes 4194304 | tf_op jit(solution)/shard_map/attn_bwd_full/pallas_call | solution.py:431
  411.0 28.9 %attn_bwd_full.3 = bf16[1024,1536]{1,0:T(8,128)(2,1)S(1)} custom-call(s32[2]{0:T(128)S(1)} %pad_add_fusion.lims_ref, bf16[1024,1536]{1,0:T(8,128)(2,1)} %copy-done.2, bf16[1024,1536]{1,0:T(8,128)(2,1)} %copy-done.2, bf16[1024,1536]{1,0:T(8,128)(2,1)} %copy-done.2, f32[4,2,1024]{2,1,0:T(2,128)S(1)} %get-tuple-element.235.l_ref, ...), custom_call_target="tpu_custom_call" | custom-call | flops 4194304 | bytes 4194304 | tf_op jit(solution)/shard_map/attn_bwd_full/pallas_call | solution.py:431
  504.3 18.3 %collective-permute-done.15 = bf16[256,1536]{1,0:T(8,128)(2,1)S(1)} collective-permute-done((bf16[256,1536]{1,0:T(8,128)(2,1)S(1)}, bf16[256,1536]{1,0:T(8,128)(2,1)S(1)}, u32[]{:S(2)}, u32[]{:S(2)}) %collective-permute-start.15) | collective-permute-done | bytes 786464 | tf_op jit(solution)/shard_map/ppermute | solution.py:452
  556.4 10.9 %collective-permute-done.22 = bf16[128,1024]{1,0:T(8,128)(2,1)S(1)} collective-permute-done((bf16[128,1024]{1,0:T(8,128)(2,1)S(1)}, bf16[128,1024]{1,0:T(8,128)(2,1)S(1)}, u32[]{:S(2)}, u32[]{:S(2)}) %collective-permute-start.22) | collective-permute-done | bytes 262176 | tf_op jit(solution)/shard_map/ppermute | solution.py:452
  568.0 10.9 %reduce-scatter.2.cloned.1.call-done = bf16[256,1024]{1,0:T(8,128)(2,1)} async-done(((bf16[8192,1024]{1,0:T(8,128)(2,1)}), bf16[256,1024]{1,0:T(8,128)(2,1)}) %reduce-scatter.2.cloned.1.call-update) | async-done | bytes 524304 | tf_op jit(solution)/shard_map/reduce_scatter | solution.py:902
  629.4 22.5 %attn_bwd_causal.2 = bf16[1024,1536]{1,0:T(8,128)(2,1)S(1)} custom-call(s32[2]{0:T(128)S(1)} %pad_add_fusion.lims_ref, bf16[1024,1536]{1,0:T(8,128)(2,1)} %copy-done.1, bf16[1024,1536]{1,0:T(8,128)(2,1)} %copy-done.1, bf16[1024,1536]{1,0:T(8,128)(2,1)} %copy-done.1, f32[4,2,1024]{2,1,0:T(2,128)S(1)} %get-tuple-element.215.l_ref, ...), custom_call_target="tpu_custom_call" | custom-call | flops 4194304 | bytes 4194304 | tf_op jit(solution)/shard_map/attn_bwd_causal/pallas_call | solution.py:431
  680.9 22.3 %attn_bwd_causal.3 = bf16[1024,1536]{1,0:T(8,128)(2,1)S(1)} custom-call(s32[2]{0:T(128)S(1)} %pad_add_fusion.lims_ref, bf16[1024,1536]{1,0:T(8,128)(2,1)} %copy-done, bf16[1024,1536]{1,0:T(8,128)(2,1)} %copy-done, bf16[1024,1536]{1,0:T(8,128)(2,1)} %copy-done, f32[4,2,1024]{2,1,0:T(2,128)S(1)} %get-tuple-element.209.l_ref, ...), custom_call_target="tpu_custom_call" | custom-call | flops 4194304 | bytes 4194304 | tf_op jit(solution)/shard_map/attn_bwd_causal/pallas_call | solution.py:431
  811.2 18.7 %collective-permute-done.53 = bf16[64,1024]{1,0:T(8,128)(2,1)S(1)} collective-permute-done((bf16[64,1024]{1,0:T(8,128)(2,1)S(1)}, bf16[64,1024]{1,0:T(8,128)(2,1)S(1)}, u32[]{:S(2)}, u32[]{:S(2)}) %collective-permute-start.53) | collective-permute-done | bytes 131104 | tf_op jit(solution)/shard_map/ppermute | solution.py:452
  833.3 25.7 %collective-permute-done.56 = bf16[32,1024]{1,0:T(8,128)(2,1)S(1)} collective-permute-done((bf16[32,1024]{1,0:T(8,128)(2,1)S(1)}, bf16[32,1024]{1,0:T(8,128)(2,1)S(1)}, u32[]{:S(2)}, u32[]{:S(2)}) %collective-permute-start.56) | collective-permute-done | bytes 65568 | tf_op jit(solution)/shard_map/ppermute | solution.py:452
  873.1 14.9 %collective-permute-done.59 = f32[32,1024]{1,0:T(8,128)S(1)} collective-permute-done((f32[32,1024]{1,0:T(8,128)S(1)}, f32[32,1024]{1,0:T(8,128)S(1)}, u32[]{:S(2)}, u32[]{:S(2)}) %collective-permute-start.59) | collective-permute-done | bytes 131104 | tf_op jit(solution)/shard_map/ppermute | solution.py:452
  888.2 11.2 %collective-permute-done.60 = bf16[2,256,512]{2,1,0:T(8,128)(2,1)S(1)} collective-permute-done((bf16[2,256,512]{2,1,0:T(8,128)(2,1)S(1)}, bf16[2,256,512]{2,1,0:T(8,128)(2,1)S(1)}, u32[]{:S(2)}, u32[]{:S(2)}) %collective-permute-start.60) | collective-permute-done | bytes 524320 | tf_op jit(solution)/shard_map/ppermute | solution.py:452
  899.7 21.5 %collective-permute-done.61 = bf16[4,256,512]{2,1,0:T(8,128)(2,1)S(1)} collective-permute-done((bf16[4,256,512]{2,1,0:T(8,128)(2,1)S(1)}, bf16[4,256,512]{2,1,0:T(8,128)(2,1)S(1)}, u32[]{:S(2)}, u32[]{:S(2)}) %collective-permute-start.61) | collective-permute-done | bytes 1048608 | tf_op jit(solution)/shard_map/ppermute | solution.py:452
  (711 shorter events, 520.7 us)
Async XLA Ops:
  7.2 91.5 %all-gather.11.cloned.1.call-start = ((), (), s32[]{:S(2)}) async-start(), calls=%async_computation.2 | async-start | bytes 4456448 | tf_op jit(solution)/shard_map/all_gather | solution.py:1023
  19.2 190.5 %all-gather.13.cloned.1.call-start = ((), (), s32[]{:S(2)}) async-start(), calls=%async_computation.3 | async-start | bytes 13369344 | tf_op jit(solution)/shard_map/all_gather | solution.py:1023
  73.2 505.6 %reduce-scatter.2.cloned.1.call-start = ((), (), s32[]{:S(2)}) async-start(), calls=%async_computation.1 | async-start | bytes 17301504 | tf_op jit(solution)/shard_map/reduce_scatter | solution.py:902
  122.4 46.9 %collective-permute-start.7 = (bf16[512,1024]{1,0:T(8,128)(2,1)S(1)}, bf16[512,1024]{1,0:T(8,128)(2,1)S(1)}, u32[]{:S(2)}, u32[]{:S(2)}) collective-permute-start(bf16[512,1024]{1,0:T(8,128)(2,1)S(1)} %collective-permute-done.5), channel_id=1, source_target_pairs={{0,4},{2,6},{4,0},{6,2},{8,12},{10,14},{12,8},{14,10},{16,20},{18,... | collective-permute-start | bytes 3145736 | tf_op jit(solution)/shard_map/ppermute | solution.py:452
  176.7 122.5 %collective-permute-start.9 = (bf16[512,1024]{1,0:T(8,128)(2,1)}, bf16[512,1024]{1,0:T(8,128)(2,1)}, u32[]{:S(2)}, u32[]{:S(2)}) collective-permute-start(bf16[512,1024]{1,0:T(8,128)(2,1)} %dynamic-slice_bitcast_fusion), channel_id=1, source_target_pairs={{0,1},{1,0},{2,3},{3,2},{4,5},{5,4},{6,7},{7,6},{8,9},{9,8},{10,11... | collective-permute-start | bytes 3145736 | tf_op jit(solution)/shard_map/ppermute | solution.py:448
  351.8 409.6 %all-gather.15.cloned.1.call-start = ((), (), s32[]{:S(2)}) async-start(), calls=%async_computation.4 | async-start | bytes 8912896 | tf_op jit(solution)/shard_map/all_gather | solution.py:907
  354.7 149.0 %collective-permute-start.14 = (bf16[512,1024]{1,0:T(8,128)(2,1)}, bf16[512,1024]{1,0:T(8,128)(2,1)}, u32[]{:S(2)}, u32[]{:S(2)}) collective-permute-start(bf16[512,1024]{1,0:T(8,128)(2,1)} %dynamic-slice_convert_fusion.1), channel_id=1, source_target_pairs={{0,1},{1,0},{2,3},{3,2},{4,5},{5,4},{6,7},{7,6},{8,9},{9,8},{10,11... | collective-permute-start | bytes 3145736 | tf_op jit(solution)/shard_map/ppermute | solution.py:448
  450.6 52.9 %collective-permute-start.16 = (bf16[128,1024]{1,0:T(8,128)(2,1)}, bf16[128,1024]{1,0:T(8,128)(2,1)}, u32[]{:S(2)}, u32[]{:S(2)}) collective-permute-start(bf16[128,1024]{1,0:T(8,128)(2,1)} %bitcast.47), channel_id=1, source_target_pairs={{0,1},{1,0},{2,3},{3,2},{4,5},{5,4},{6,7},{7,6},{8,9},{9,8},{10,11... | collective-permute-start | bytes 786440 | tf_op jit(solution)/shard_map/ppermute | solution.py:448
  483.8 38.7 %collective-permute-start.15 = (bf16[256,1536]{1,0:T(8,128)(2,1)S(1)}, bf16[256,1536]{1,0:T(8,128)(2,1)S(1)}, u32[]{:S(2)}, u32[]{:S(2)}) collective-permute-start(bf16[256,1536]{1,0:T(8,128)(2,1)S(1)} %bitcast.449), channel_id=1, source_target_pairs={{0,4},{2,6},{4,0},{6,2},{8,12},{10,14},{12,8},{14,10},{16,20},{18,... | collective-permute-start | bytes 2359304 | tf_op jit(solution)/shard_map/ppermute | solution.py:452
  503.5 50.4 %collective-permute-start.21 = (bf16[128,1024]{1,0:T(8,128)(2,1)S(1)}, bf16[128,1024]{1,0:T(8,128)(2,1)S(1)}, u32[]{:S(2)}, u32[]{:S(2)}) collective-permute-start(bf16[128,1024]{1,0:T(8,128)(2,1)S(1)} %bitcast.459), channel_id=1, source_target_pairs={{0,1},{1,0},{2,3},{3,2},{4,5},{5,4},{6,7},{7,6},{8,9},{9,8},{10,11... | collective-permute-start | bytes 786440 | tf_op jit(solution)/shard_map/ppermute | solution.py:448
  503.7 52.7 %collective-permute-start.20 = (bf16[256,1536]{1,0:T(8,128)(2,1)S(1)}, bf16[256,1536]{1,0:T(8,128)(2,1)}, u32[]{:S(2)}, u32[]{:S(2)}) collective-permute-start(bf16[256,1536]{1,0:T(8,128)(2,1)S(1)} %bitcast.448), channel_id=1, source_target_pairs={{0,4},{2,6},{4,0},{6,2},{8,12},{10,14},{12,8},{14,10},{16,20},{18,... | collective-permute-start | bytes 2359304 | tf_op jit(solution)/shard_map/ppermute | solution.py:452
  523.8 43.4 %collective-permute-start.22 = (bf16[128,1024]{1,0:T(8,128)(2,1)S(1)}, bf16[128,1024]{1,0:T(8,128)(2,1)S(1)}, u32[]{:S(2)}, u32[]{:S(2)}) collective-permute-start(bf16[128,1024]{1,0:T(8,128)(2,1)S(1)} %fusion.70), channel_id=1, source_target_pairs={{0,4},{2,6},{4,0},{6,2},{8,12},{10,14},{12,8},{14,10},{16,20},{18,... | collective-permute-start | bytes 786440 | tf_op jit(solution)/shard_map/ppermute | solution.py:452
  525.4 42.6 %collective-permute-start.19 = (bf16[256,1536]{1,0:T(8,128)(2,1)S(1)}, bf16[256,1536]{1,0:T(8,128)(2,1)}, u32[]{:S(2)}, u32[]{:S(2)}) collective-permute-start(bf16[256,1536]{1,0:T(8,128)(2,1)S(1)} %fusion.44), channel_id=1, source_target_pairs={{0,1},{1,0},{2,3},{3,2},{4,5},{5,4},{6,7},{7,6},{8,9},{9,8},{10,11... | collective-permute-start | bytes 2359304 | tf_op jit(solution)/shard_map/ppermute | solution.py:448
  578.9 254.4 %all-gather.17.cloned.1.call-start = ((), (), s32[]{:S(2)}) async-start(), calls=%async_computation.5 | async-start | bytes 4456448 | tf_op jit(solution)/shard_map/all_gather | solution.py:923
  585.5 71.6 %collective-permute-start.27 = (bf16[512,1024]{1,0:T(8,128)(2,1)}, bf16[512,1024]{1,0:T(8,128)(2,1)}, u32[]{:S(2)}, u32[]{:S(2)}) collective-permute-start(bf16[512,1024]{1,0:T(8,128)(2,1)} %bitcast.66), channel_id=1, source_target_pairs={{0,1},{1,0},{2,3},{3,2},{4,5},{5,4},{6,7},{7,6},{8,9},{9,8},{10,11... | collective-permute-start | bytes 3145736 | tf_op jit(solution)/shard_map/ppermute | solution.py:448
  620.5 46.9 %collective-permute-start.29 = (bf16[64,1536]{1,0:T(8,128)(2,1)}, bf16[64,1536]{1,0:T(8,128)(2,1)}, u32[]{:S(2)}, u32[]{:S(2)}) collective-permute-start(bf16[64,1536]{1,0:T(8,128)(2,1)} %dynamic-slice_bitcast_fusion.7), channel_id=1, source_target_pairs={{0,16},{2,18},{4,20},{6,22},{8,24},{10,26},{12,28},{14,30},{16,0},... | collective-permute-start | bytes 589832 | tf_op jit(solution)/shard_map/ppermute | solution.py:452
  623.7 43.7 %collective-permute-start.31 = (bf16[256,1024]{1,0:T(8,128)(2,1)}, bf16[256,1024]{1,0:T(8,128)(2,1)}, u32[]{:S(2)}, u32[]{:S(2)}) collective-permute-start(bf16[256,1024]{1,0:T(8,128)(2,1)} %bitcast.76), channel_id=1, source_target_pairs={{0,2},{2,0},{4,6},{6,4},{8,10},{10,8},{12,14},{14,12},{16,18},{18,... | collective-permute-start | bytes 1572872 | tf_op jit(solution)/shard_map/ppermute | solution.py:452
  624.9 42.5 %collective-permute-start.32 = (bf16[256,1024]{1,0:T(8,128)(2,1)}, bf16[256,1024]{1,0:T(8,128)(2,1)}, u32[]{:S(2)}, u32[]{:S(2)}) collective-permute-start(bf16[256,1024]{1,0:T(8,128)(2,1)} %bitcast.78), channel_id=1, source_target_pairs={{0,2},{2,0},{4,6},{6,4},{8,10},{10,8},{12,14},{14,12},{16,18},{18,... | collective-permute-start | bytes 1572872 | tf_op jit(solution)/shard_map/ppermute | solution.py:452
  627.6 44.1 %collective-permute-start.28 = (bf16[512,1024]{1,0:T(8,128)(2,1)}, bf16[512,1024]{1,0:T(8,128)(2,1)}, u32[]{:S(2)}, u32[]{:S(2)}) collective-permute-start(bf16[512,1024]{1,0:T(8,128)(2,1)} %bitcast.68), channel_id=1, source_target_pairs={{0,4},{2,6},{4,0},{6,2},{8,12},{10,14},{12,8},{14,10},{16,20},{18,... | collective-permute-start | bytes 3145736 | tf_op jit(solution)/shard_map/ppermute | solution.py:452
  665.9 50.0 %collective-permute-start.33 = (bf16[512,1024]{1,0:T(8,128)(2,1)}, bf16[512,1024]{1,0:T(8,128)(2,1)}, u32[]{:S(2)}, u32[]{:S(2)}) collective-permute-start(bf16[512,1024]{1,0:T(8,128)(2,1)} %bitcast.79), channel_id=1, source_target_pairs={{0,1},{1,0},{2,3},{3,2},{4,5},{5,4},{6,7},{7,6},{8,9},{9,8},{10,11... | collective-permute-start | bytes 3145736 | tf_op jit(solution)/shard_map/ppermute | solution.py:448
  667.4 48.9 %collective-permute-start.36 = (bf16[512,1024]{1,0:T(8,128)(2,1)}, bf16[512,1024]{1,0:T(8,128)(2,1)}, u32[]{:S(2)}, u32[]{:S(2)}) collective-permute-start(bf16[512,1024]{1,0:T(8,128)(2,1)} %bitcast.84), channel_id=1, source_target_pairs={{0,4},{2,6},{4,0},{6,2},{8,12},{10,14},{12,8},{14,10},{16,20},{18,... | collective-permute-start | bytes 3145736 | tf_op jit(solution)/shard_map/ppermute | solution.py:452
  674.3 42.0 %collective-permute-start.34 = (bf16[512,1024]{1,0:T(8,128)(2,1)}, bf16[512,1024]{1,0:T(8,128)(2,1)}, u32[]{:S(2)}, u32[]{:S(2)}) collective-permute-start(bf16[512,1024]{1,0:T(8,128)(2,1)} %fusion.38), channel_id=1, source_target_pairs={{0,4},{2,6},{4,0},{6,2},{8,12},{10,14},{12,8},{14,10},{16,20},{18,... | collective-permute-start | bytes 3145736 | tf_op jit(solution)/shard_map/ppermute | solution.py:452
  677.3 39.1 %collective-permute-start.35 = (bf16[512,1024]{1,0:T(8,128)(2,1)}, bf16[512,1024]{1,0:T(8,128)(2,1)}, u32[]{:S(2)}, u32[]{:S(2)}) collective-permute-start(bf16[512,1024]{1,0:T(8,128)(2,1)} %fusion.37), channel_id=1, source_target_pairs={{0,1},{1,0},{2,3},{3,2},{4,5},{5,4},{6,7},{7,6},{8,9},{9,8},{10,11... | collective-permute-start | bytes 3145736 | tf_op jit(solution)/shard_map/ppermute | solution.py:448
  706.7 214.6 %all-gather.19.cloned.1.call-start = ((), (), s32[]{:S(2)}) async-start(), calls=%async_computation.6 | async-start | bytes 8912896 | tf_op jit(solution)/shard_map/all_gather | solution.py:923
  (223 other events, 2900.4 us)
Sparse Core Ops, SparseCore 0:
  19.3 52.0 all-gather.10
  73.7 124.3 all-gather.12
  352.0 226.8 reduce-scatter.1
  580.9 103.6 all-gather.14
  706.8 66.4 all-gather.16
  795.4 97.5 all-gather.18

commit v5 on v4

--- a/solution.py
+++ b/solution.py
@@ -578,9 +578,9 @@
     )(place.reshape(1).astype(jnp.int32), *arrays)
 
 
-def unpack_kernel(count, side_ref, in_ref, *refs):
+def unpack_kernel(in_ref, *refs):
     at = 0
-    for ref in refs[-count:]:
+    for ref in refs:
         rows = ref.shape[0] // in_ref.shape[0]
         for part in range(ref.shape[1] // PACK_WIDTH):
             for block in range(in_ref.shape[0]):
@@ -590,73 +590,61 @@
             at += rows
 
 
-def unpack_halves(side, gathered, shapes, bases=()):
+def unpack_halves(gathered, shapes):
     dp_size, total, _ = gathered.shape
     some = max(1, dp_size // 4)
-    steps = dp_size // some
-    out_specs, out_shape = [], []
-    for index, (height, width) in enumerate(shapes):
-        base = index - (len(shapes) - len(bases))
-        block = (height // steps, width)
-        if base < 0:
-            out_specs.append(pl.BlockSpec(block, lambda step, side_ref: (step, 0)))
-            out_shape.append(jax.ShapeDtypeStruct((height, width), bf16))
-            continue
-        if bases[base].shape[0] == height:
-            out_specs.append(pl.BlockSpec(block, lambda step, side_ref: (step, 1 - side_ref[0])))
-        else:
-            out_specs.append(pl.BlockSpec(block, lambda step, side_ref: ((1 - side_ref[0]) * steps + step, 0)))
-        out_shape.append(jax.ShapeDtypeStruct(bases[base].shape, bf16))
     return pl.pallas_call(
-        partial(unpack_kernel, len(shapes)),
-        grid_spec=pltpu.PrefetchScalarGridSpec(
-            num_scalar_prefetch=1,
-            grid=(steps,),
-            in_specs=[pl.BlockSpec((some, total, PACK_WIDTH), lambda step, side_ref: (step, 0, 0))]
-            + [pl.BlockSpec(memory_space=pl.ANY)] * len(bases),
-            out_specs=out_specs,
-        ),
-        out_shape=out_shape,
-        input_output_aliases={2 + base: len(shapes) - len(bases) + base for base in range(len(bases))},
+        unpack_kernel,
+        grid=(dp_size // some,),
+        in_specs=[pl.BlockSpec((some, total, PACK_WIDTH), lambda step: (step, 0, 0))],
+        out_specs=[
+            pl.BlockSpec((height // dp_size * some, width), lambda step: (step, 0)) for height, width in shapes
+        ],
+        out_shape=[jax.ShapeDtypeStruct(shape, bf16) for shape in shapes],
         compiler_params=pltpu.CompilerParams(vmem_limit_bytes=32 * 2**20),
         cost_estimate=pl.CostEstimate(
             flops=0, bytes_accessed=4 * dp_size * total * PACK_WIDTH, transcendentals=0
         ),
         name="unpack_halves",
-    )(side.reshape(1).astype(jnp.int32), gathered, *bases)
-
-
-def fill_kernel(side_ref, up_ref, down_ref, up_out, down_out):
-    up_out[...] = up_ref[0]
-    down_out[...] = down_ref[0]
-
-
-def fill_whole(side, w_up, w_down, layer):
+    )(gathered)
+
+
+def stack_kernel(steps, side_ref, down_own, up_own, down_other, up_other, out_ref):
+    blocks, rows = out_ref.shape[0], out_ref.shape[1] // 2
+
+    def write(down_ref, up_ref):
+        for block in range(blocks):
+            out_ref[block, :rows] = down_ref[block * rows : (block + 1) * rows]
+            out_ref[block, rows:] = up_ref[block * rows : (block + 1) * rows]
+
+    pl.when(pl.program_id(0) < steps)(lambda: write(down_own, up_own))
+    pl.when(pl.program_id(0) >= steps)(lambda: write(down_other, up_other))
+
+
+def stack_pair(side, dp_size, down_parts, up_parts):
+    height, width = down_parts[0].shape
     steps = 4
-    _, height, width = w_up.shape
-    up_rows, down_rows = height // steps, width // steps
+    rows, some = height // dp_size, dp_size // steps
+    own = pl.BlockSpec((some * rows, width), lambda step, side_ref: (jnp.minimum(step, steps - 1), 0))
+    other = pl.BlockSpec((some * rows, width), lambda step, side_ref: (jnp.maximum(step - steps, 0), 0))
+
+    def target(step, side_ref):
+        half = jnp.where(step < steps, side_ref[0], 1 - side_ref[0])
+        return (half * steps + step % steps, 0, 0)
+
     return pl.pallas_call(
-        fill_kernel,
+        partial(stack_kernel, steps),
         grid_spec=pltpu.PrefetchScalarGridSpec(
             num_scalar_prefetch=1,
-            grid=(steps,),
-            in_specs=[
-                pl.BlockSpec((1, up_rows, width), lambda step, side_ref: (layer, step, 0)),
-                pl.BlockSpec((1, down_rows, height), lambda step, side_ref: (layer, step, 0)),
-            ],
-            out_specs=[
-                pl.BlockSpec((up_rows, width), lambda step, side_ref: (step, side_ref[0])),
-                pl.BlockSpec((down_rows, height), lambda step, side_ref: (side_ref[0] * steps + step, 0)),
-            ],
+            grid=(2 * steps,),
+            in_specs=[own, own, other, other],
+            out_specs=pl.BlockSpec((some, 2 * rows, width), target),
         ),
-        out_shape=[
-            jax.ShapeDtypeStruct((height, 2 * width), bf16),
-            jax.ShapeDtypeStruct((2 * width, height), bf16),
-        ],
+        out_shape=jax.ShapeDtypeStruct((2 * dp_size, 2 * rows, width), bf16),
         compiler_params=pltpu.CompilerParams(vmem_limit_bytes=32 * 2**20),
-        cost_estimate=pl.CostEstimate(flops=0, bytes_accessed=8 * height * width, transcendentals=0),
-        name="fill_whole",
-    )(side.reshape(1).astype(jnp.int32), w_up, w_down)
+        cost_estimate=pl.CostEstimate(flops=0, bytes_accessed=16 * height * width, transcendentals=0),
+        name="stack_pair",
+    )(side.reshape(1).astype(jnp.int32), down_parts[0], up_parts[0], down_parts[1], up_parts[1])
 
 
 def place_joint_kernel(whole_ref, *refs):
@@ -1022,20 +1010,27 @@
     def gathered(arrived):
         return lax.all_gather(arrived, "dp", axis=0, tiled=False)
 
-    def unpacked(whole, kinds, bases=()):
-        return dict(zip(kinds, unpack_halves(side, whole, [flat_shape[kind] for kind in kinds], bases)))
+    def unpacked(whole, kinds):
+        return dict(zip(kinds, unpack_halves(whole, [flat_shape[kind] for kind in kinds])))
 
     attn_kinds, all_kinds = ("qkv", "out"), ("qkv", "out", "up", "down")
-    first_pack = swap_tensor(packed(0, attn_kinds))
-    other_rows = swap_tensor(away_rows(frames_in))
+    rows_away, first_send = pin(away_rows(frames_in), packed(0, attn_kinds))
+    other_rows = swap_tensor(rows_away)
+    first_pack = swap_tensor(first_send)
+    own_qkv = [flat_qkv(stacked, layer) for layer in range(2)]
+    first_pack, own_qkv = pin(first_pack, own_qkv)
     first_whole = gathered(first_pack)
     second_send = packed(1, all_kinds)
-    up_send = row_half(quarter_of("up", w_up[0], core), near_row)
-    down_send = row_half(quarter_of("down", w_down[0], core), near_row)
-    own_qkv = [flat_qkv(stacked, layer) for layer in range(2)]
-    filled = fill_whole(side, w_up, w_down, 1)
-    other_rows, second_send, up_send, down_send, own_qkv, filled = pin(
-        other_rows, second_send, up_send, down_send, own_qkv, filled
+    piece_rows, piece_columns = model_width // 2, w_up.shape[2] // 2
+    up_send = lax.dynamic_slice(
+        w_up, (0, near_row * piece_rows, core * piece_columns), (1, piece_rows, piece_columns)
+    )[0]
+    piece_rows = w_down.shape[1] // 4
+    down_send = lax.dynamic_slice(
+        w_down, (0, (2 * core + near_row) * piece_rows, 0), (1, piece_rows, model_width)
+    )[0]
+    other_rows, second_send, up_send, down_send, own_qkv = pin(
+        other_rows, second_send, up_send, down_send, own_qkv
     )
     second_pack = swap_tensor(second_send)
     rows = whole_rows(frames_in, other_rows).astype(f32)
@@ -1077,7 +1072,7 @@
     mine = dot_low(normed, own_qkv[1], NN)
     mix_mine = attn_fwd(mine, limits, False, 512)
     mix_mine, second_whole = pin(mix_mine, second_whole)
-    second = unpacked(second_whole, all_kinds, filled)
+    second = unpacked(second_whole, all_kinds)
     weights = [
         {
             "qkv": [own_qkv[0], first["qkv"]],
@@ -1088,8 +1083,8 @@
         {
             "qkv": [own_qkv[1], second["qkv"]],
             "out": [w_out[1], second["out"]],
-            "up": [second["up"]],
-            "down": [second["down"]],
+            "up": [w_up[1], second["up"]],
+            "down": [w_down[1], second["down"]],
         },
     ]
     theirs = dot_low(normed, second["qkv"], NN)
@@ -1165,13 +1160,11 @@
     out0, qkv0 = chain("out", "x", None), chain("qkv", "y", None)
 
     low = grad_rows.astype(bf16)
-    (down_part,) = down_grads(1, low)
+    down_parts = down_grads(1, low)
     hidden = hidden_grads(1, low)
-    down_part, hidden, grad_rows = pin(down_part, hidden, grad_rows)
-    up_part = dot_low(hidden[0], kept[3][0], TN)
-    both_parts = jnp.concatenate(
-        [part.reshape(2 * dp_size, -1, model_width) for part in (down_part, up_part)], axis=1
-    )
+    down_parts, hidden, grad_rows = pin(down_parts, hidden, grad_rows)
+    up_parts = [dot_low(part, kept[3][0], TN) for part in hidden]
+    both_parts = stack_pair(side, dp_size, down_parts, up_parts)
     both_parts, hidden, grad_rows = pin(both_parts, hidden, grad_rows)
     pair1 = Scatter(flat_rows(both_parts))
     grad_normed = dot_sum(list(zip(hidden, weights[1]["up"])), NT)

time: 955 us -> 925 us (0.969)
  local copies, waits for them, and re-layouts: 108 us -> 79.3 us
  matrix products: 245 us -> 258 us
    unnamed x366 -> x332, local copies, waits for them, and re-layouts: 53.3 us -> 31.1 us
    reduce_scatter x1, waiting for transfers between devices: 10.9 us -> 0.01 us  [__init__(): lax.psum_scatter(block, ('tensor', 'dp'), scatter_dimension=0, tiled=True)]
    ppermute x18, waiting for transfers between devices: 23.4 us -> 34.1 us  [swap_tensor(): return lax.ppermute(block, 'tensor', [(0, 1), (1, 0)])]
    concatenate x1 -> x0, other arithmetic: 10.4 us -> none  [paired_device(): jnp.concatenate([part.reshape(2 * dp_size, -1, model_width) for part in (...]
    dot_general x16 -> x18, matrix products: 82.9 us -> 92.4 us  [dot_sum(): term = lax.dot_general(left, right, dims, preferred_element_type=f32)]
    dot_general x24 -> x26, matrix products: 94.8 us -> 89.4 us  [dot_low(): lax.dot_general(left, right, dims, preferred_element_type=f32).astype(bf16)]
    dot_general x4 -> x5, matrix products: 28.5 us -> 32.2 us  [hidden_grads(): lax.dot_general(low, part, NT, preferred_element_type=f32)]
    dot_general x1 -> x2, matrix products: 19.4 us -> 22.2 us  [paired_device(): jnp.dot(normed, part, preferred_element_type=f32)]
  transfers between devices with their start and end apart: 69 -> 69, of which waited for: 22 -> 23; matrix products, arithmetic and copies ran while one was open for 35% -> 38% of each run, Pallas kernels for 23% -> 23%
where the time goes in v5:
time: 925 us; the launch traced here: 920 us
  matrix products  258 us (28%)
  Pallas kernels  223 us (24%)
  waiting for transfers between devices  206 us (22%)
  other arithmetic  82.3 us (9%)
  local copies, waits for them, and re-layouts  79.3 us (9%)
  starting transfers between devices  54.5 us (6%)
  between operations  17.1 us (2%)
    ppermute x45, waiting for transfers between devices, swap_bit(): lax.ppermute(block, 'dp', [(place, place ^ 1 << bit) for place in range(d...  171 us
    pallas_call x4, Pallas kernels, attn_bwd(): pl.pallas_call(partial(bwd_kernel, causal, bq), grid=(pairs,), in_specs=[...  103 us
    dot_general x18, matrix products, dot_sum(): term = lax.dot_general(left, right, dims, preferred_element_type=f32)  92.4 us
    dot_general x26, matrix products, dot_low(): lax.dot_general(left, right, dims, preferred_element_type=f32).astype(bf16)  89.4 us
    pallas_call x4, Pallas kernels, attn_fwd(): pl.pallas_call(partial(fwd_kernel, causal, bq), grid=(pairs,), in_specs=[...  66.2 us
    ppermute x18, waiting for transfers between devices, swap_tensor(): return lax.ppermute(block, 'tensor', [(0, 1), (1, 0)])  34.1 us
    dot_general x5, matrix products, hidden_grads(): lax.dot_general(low, part, NT, preferred_element_type=f32)  32.2 us
    ppermute x45, starting transfers between devices, swap_bit(): lax.ppermute(block, 'dp', [(place, place ^ 1 << bit) for place in range(d...  32.1 us
  transfers between devices with their start and end apart: 69, of which 23 were waited for; matrix products, arithmetic and copies ran while one was open for 38% of the time, Pallas kernels for 23%

profile of v5, /device:TPU:0, one launch (start us, length us, event | category | flops | bytes accessed | tf_op | source)
XLA Modules:
  0.0 919.6 jit_solution(7020216977907815347)
XLA Ops:
  27.6 17.4 %collective-permute-done = bf16[512,1024]{1,0:T(8,128)(2,1)S(1)} collective-permute-done((bf16[512,1024]{1,0:T(8,128)(2,1)S(1)}, bf16[512,1024]{1,0:T(8,128)(2,1)S(1)}, u32[]{:S(2)}, u32[]{:S(2)}) %collective-permute-start) | collective-permute-done | bytes 1048608 | tf_op jit(solution)/shard_map/ppermute | solution.py:448
  52.6 10.6 %collective-permute-done.2 = bf16[768,512]{1,0:T(8,128)(2,1)} collective-permute-done((bf16[768,512]{1,0:T(8,128)(2,1)S(1)}, bf16[768,512]{1,0:T(8,128)(2,1)}, u32[]{:S(2)}, u32[]{:S(2)}) %collective-permute-start.2) | collective-permute-done | bytes 786464 | tf_op jit(solution)/shard_map/ppermute | solution.py:448
  67.5 14.0 %attn_fwd_causal.2 = (bf16[1024,512]{1,0:T(8,128)(2,1)S(1)}, f32[4,2,1024]{2,1,0:T(2,128)S(1)}) custom-call(s32[2]{0:T(128)S(1)} %pad_add_fusion.lims_ref, bf16[1024,1536]{1,0:T(8,128)(2,1)S(1)} %convolution_convert_fusion.7.q_ref.k_ref.v_ref, bf16[1024,1536]{1,0:T(8,128)(2,1)S(1)} %convolution_convert_fusion.7.q_ref.k_ref.v_ref, ...), custom_call_target="tpu_custom_call" | custom-call | flops 4194304 | bytes 4194304 | tf_op jit(solution)/shard_map/attn_fwd_causal/pallas_call | solution.py:381
  98.5 14.4 %attn_fwd_causal.3 = (bf16[1024,512]{1,0:T(8,128)(2,1)S(1)}, f32[4,2,1024]{2,1,0:T(2,128)S(1)}) custom-call(s32[2]{0:T(128)S(1)} %pad_add_fusion.lims_ref, bf16[1024,1536]{1,0:T(8,128)(2,1)S(1)} %convolution_convert_fusion.6.q_ref.k_ref.v_ref, bf16[1024,1536]{1,0:T(8,128)(2,1)S(1)} %convolution_convert_fusion.6.q_ref.k_ref.v_ref, ...), custom_call_target="tpu_custom_call" | custom-call | flops 4194304 | bytes 4194304 | tf_op jit(solution)/shard_map/attn_fwd_causal/pallas_call | solution.py:381
  123.4 9.6 %add_convert_fusion.2 = (bf16[1024,2048]{1,0:T(8,128)(2,1)}, bf16[1024,2048]{1,0:T(8,128)(2,1)}) fusion(bf16[1024,1024]{1,0:T(8,128)(2,1)S(1)} %add_convert_fusion.11, bf16[2,1024,2048]{2,1,0:T(8,128)(2,1)S(1)} %bitcast.425), kind=kOutput, calls=%fused_computation.11 | convolution fusion | flops 4326424576 | bytes 14680064 | tf_op jit(solution)/shard_map/dot_general | solution.py:1056
  152.8 8.5 collective-permute-done.7
  181.1 19.0 %attn_fwd_full.2 = (bf16[1024,512]{1,0:T(8,128)(2,1)S(1)}, f32[4,2,1024]{2,1,0:T(2,128)S(1)}) custom-call(s32[2]{0:T(128)S(1)} %pad_add_fusion.lims_ref, bf16[1024,1536]{1,0:T(8,128)(2,1)S(1)} %convolution_convert_fusion.5.q_ref.k_ref.v_ref, bf16[1024,1536]{1,0:T(8,128)(2,1)S(1)} %convolution_convert_fusion.5.q_ref.k_ref.v_ref, ...), custom_call_target="tpu_custom_call" | custom-call | flops 4194304 | bytes 4194304 | tf_op jit(solution)/shard_map/attn_fwd_full/pallas_call | solution.py:381
  217.6 18.7 %attn_fwd_full.3 = (bf16[1024,512]{1,0:T(8,128)(2,1)S(1)}, f32[4,2,1024]{2,1,0:T(2,128)S(1)}) custom-call(s32[2]{0:T(128)S(1)} %pad_add_fusion.lims_ref, bf16[1024,1536]{1,0:T(8,128)(2,1)S(1)} %convolution_convert_fusion.4.q_ref.k_ref.v_ref, bf16[1024,1536]{1,0:T(8,128)(2,1)S(1)} %convolution_convert_fusion.4.q_ref.k_ref.v_ref, ...), custom_call_target="tpu_custom_call" | custom-call | flops 4194304 | bytes 4194304 | tf_op jit(solution)/shard_map/attn_fwd_full/pallas_call | solution.py:381
  243.0 13.3 %add_convert_fusion.1 = (bf16[1024,2048]{1,0:T(8,128)(2,1)}, bf16[1024,2048]{1,0:T(8,128)(2,1)}) fusion(bf16[1024,1024]{1,0:T(8,128)(2,1)S(1)} %add_convert_fusion.7, bf16[2,1024,2048]{2,1,0:T(8,128)(2,1)} %refs_2_.1), kind=kOutput, calls=%fused_computation.7 | convolution fusion | flops 4326424576 | bytes 14680064 | tf_op jit(solution)/shard_map/dot_general | solution.py:1096
  256.3 8.9 add_convert_fusion
  329.5 10.5 %fusion.127 = f32[1024,1024]{1,0:T(8,128)} fusion(bf16[1024,2048]{1,0:T(8,128)(2,1)} %multiply_convert_fusion.1, bf16[1024,2048]{1,0:T(8,128)(2,1)} %copy-done.19), kind=kOutput, calls=%fused_computation.360 | convolution fusion | flops 4294967296 | bytes 12582912 | tf_op jit(solution)/shard_map/dot_general | solution.py:497
  340.1 11.0 %multiply_reduce_fusion = (f32[1024]{0:T(1024)S(1)}, f32[1024]{0:T(1024)S(1)}, f32[1024]{0:T(1024)S(1)}, f32[1024]{0:T(1024)S(1)}, f32[1024,1024]{1,0:T(8,128)}) fusion(f32[1024,1024]{1,0:T(8,128)S(1)} %copy-done.31, f32[1024]{0:T(1024)S(1)} %broadcast_multiply_fusion.12, f32[1024]{0:T(1024)S(1)} %add_rsqrt_fusion, f32[1024]{0:T(1024)S(1)} %get-tuple-element.432, ...), kind=kOutput, calls=%fused_computation.47 | convolution fusion | flops 4305448960 | bytes 21000192 | tf_op jit(solution)/shard_map/dot_general | solution.py:497
  357.3 28.9 %attn_bwd_full.2 = bf16[1024,1536]{1,0:T(8,128)(2,1)S(1)} custom-call(s32[2]{0:T(128)S(1)} %pad_add_fusion.lims_ref, bf16[1024,1536]{1,0:T(8,128)(2,1)} %copy-done.3, bf16[1024,1536]{1,0:T(8,128)(2,1)} %copy-done.3, bf16[1024,1536]{1,0:T(8,128)(2,1)} %copy-done.3, f32[4,2,1024]{2,1,0:T(2,128)S(1)} %get-tuple-element.271.l_ref, ...), custom_call_target="tpu_custom_call" | custom-call | flops 4194304 | bytes 4194304 | tf_op jit(solution)/shard_map/attn_bwd_full/pallas_call | solution.py:431
  392.5 29.1 %attn_bwd_full.3 = bf16[1024,1536]{1,0:T(8,128)(2,1)S(1)} custom-call(s32[2]{0:T(128)S(1)} %pad_add_fusion.lims_ref, bf16[1024,1536]{1,0:T(8,128)(2,1)} %copy-done.2, bf16[1024,1536]{1,0:T(8,128)(2,1)} %copy-done.2, bf16[1024,1536]{1,0:T(8,128)(2,1)} %copy-done.2, f32[4,2,1024]{2,1,0:T(2,128)S(1)} %get-tuple-element.244.l_ref, ...), custom_call_target="tpu_custom_call" | custom-call | flops 4194304 | bytes 4194304 | tf_op jit(solution)/shard_map/attn_bwd_full/pallas_call | solution.py:431
  471.2 9.1 multiply_convert_fusion
  493.1 14.1 %collective-permute-done.15 = bf16[256,1536]{1,0:T(8,128)(2,1)S(1)} collective-permute-done((bf16[256,1536]{1,0:T(8,128)(2,1)}, bf16[256,1536]{1,0:T(8,128)(2,1)S(1)}, u32[]{:S(2)}, u32[]{:S(2)}) %collective-permute-start.15) | collective-permute-done | bytes 786464 | tf_op jit(solution)/shard_map/ppermute | solution.py:452
  600.6 22.6 %attn_bwd_causal.2 = bf16[1024,1536]{1,0:T(8,128)(2,1)S(1)} custom-call(s32[2]{0:T(128)S(1)} %pad_add_fusion.lims_ref, bf16[1024,1536]{1,0:T(8,128)(2,1)} %copy-done.1, bf16[1024,1536]{1,0:T(8,128)(2,1)} %copy-done.1, bf16[1024,1536]{1,0:T(8,128)(2,1)} %copy-done.1, f32[4,2,1024]{2,1,0:T(2,128)S(1)} %get-tuple-element.224.l_ref, ...), custom_call_target="tpu_custom_call" | custom-call | flops 4194304 | bytes 4194304 | tf_op jit(solution)/shard_map/attn_bwd_causal/pallas_call | solution.py:431
  651.6 22.2 %attn_bwd_causal.3 = bf16[1024,1536]{1,0:T(8,128)(2,1)S(1)} custom-call(s32[2]{0:T(128)S(1)} %pad_add_fusion.lims_ref, bf16[1024,1536]{1,0:T(8,128)(2,1)} %copy-done, bf16[1024,1536]{1,0:T(8,128)(2,1)} %copy-done, bf16[1024,1536]{1,0:T(8,128)(2,1)} %copy-done, f32[4,2,1024]{2,1,0:T(2,128)S(1)} %get-tuple-element.217.l_ref, ...), custom_call_target="tpu_custom_call" | custom-call | flops 4194304 | bytes 4194304 | tf_op jit(solution)/shard_map/attn_bwd_causal/pallas_call | solution.py:431
  746.6 9.0 collective-permute-done.47
  782.7 18.3 %collective-permute-done.53 = bf16[64,1024]{1,0:T(8,128)(2,1)S(1)} collective-permute-done((bf16[64,1024]{1,0:T(8,128)(2,1)S(1)}, bf16[64,1024]{1,0:T(8,128)(2,1)S(1)}, u32[]{:S(2)}, u32[]{:S(2)}) %collective-permute-start.53) | collective-permute-done | bytes 131104 | tf_op jit(solution)/shard_map/ppermute | solution.py:452
  804.4 24.1 %collective-permute-done.56 = bf16[32,1024]{1,0:T(8,128)(2,1)S(1)} collective-permute-done((bf16[32,1024]{1,0:T(8,128)(2,1)S(1)}, bf16[32,1024]{1,0:T(8,128)(2,1)S(1)}, u32[]{:S(2)}, u32[]{:S(2)}) %collective-permute-start.56) | collective-permute-done | bytes 65568 | tf_op jit(solution)/shard_map/ppermute | solution.py:452
  842.7 15.8 %collective-permute-done.59 = f32[32,1024]{1,0:T(8,128)S(1)} collective-permute-done((f32[32,1024]{1,0:T(8,128)S(1)}, f32[32,1024]{1,0:T(8,128)S(1)}, u32[]{:S(2)}, u32[]{:S(2)}) %collective-permute-start.59) | collective-permute-done | bytes 131104 | tf_op jit(solution)/shard_map/ppermute | solution.py:452
  858.7 12.0 %collective-permute-done.60 = bf16[2,256,512]{2,1,0:T(8,128)(2,1)S(1)} collective-permute-done((bf16[2,256,512]{2,1,0:T(8,128)(2,1)S(1)}, bf16[2,256,512]{2,1,0:T(8,128)(2,1)S(1)}, u32[]{:S(2)}, u32[]{:S(2)}) %collective-permute-start.60) | collective-permute-done | bytes 524320 | tf_op jit(solution)/shard_map/ppermute | solution.py:452
  870.9 22.2 %collective-permute-done.61 = bf16[4,256,512]{2,1,0:T(8,128)(2,1)S(1)} collective-permute-done((bf16[4,256,512]{2,1,0:T(8,128)(2,1)S(1)}, bf16[4,256,512]{2,1,0:T(8,128)(2,1)S(1)}, u32[]{:S(2)}, u32[]{:S(2)}) %collective-permute-start.61) | collective-permute-done | bytes 1048608 | tf_op jit(solution)/shard_map/ppermute | solution.py:452
  (680 shorter events, 519.1 us)
Async XLA Ops:
  7.2 82.0 %all-gather.11.cloned.1.call-start = ((), (), s32[]{:S(2)}) async-start(), calls=%async_computation.2 | async-start | bytes 4456448 | tf_op jit(solution)/shard_map/all_gather | solution.py:1011
  20.4 181.4 %all-gather.13.cloned.1.call-start = ((), (), s32[]{:S(2)}) async-start(), calls=%async_computation.3 | async-start | bytes 13369344 | tf_op jit(solution)/shard_map/all_gather | solution.py:1011
  63.2 485.1 %reduce-scatter.2.cloned.1.call-start = ((), (), s32[]{:S(2)}) async-start(), calls=%async_computation.1 | async-start | bytes 17301504 | tf_op jit(solution)/shard_map/reduce_scatter | solution.py:890
  115.2 46.0 %collective-permute-start.7 = (bf16[512,1024]{1,0:T(8,128)(2,1)S(1)}, bf16[512,1024]{1,0:T(8,128)(2,1)S(1)}, u32[]{:S(2)}, u32[]{:S(2)}) collective-permute-start(bf16[512,1024]{1,0:T(8,128)(2,1)S(1)} %collective-permute-done.5), channel_id=1, source_target_pairs={{0,4},{2,6},{4,0},{6,2},{8,12},{10,14},{12,8},{14,10},{16,20},{18,... | collective-permute-start | bytes 3145736 | tf_op jit(solution)/shard_map/ppermute | solution.py:452
  168.5 109.1 %collective-permute-start.9 = (bf16[512,1024]{1,0:T(8,128)(2,1)}, bf16[512,1024]{1,0:T(8,128)(2,1)}, u32[]{:S(2)}, u32[]{:S(2)}) collective-permute-start(bf16[512,1024]{1,0:T(8,128)(2,1)} %dynamic-slice_bitcast_fusion), channel_id=1, source_target_pairs={{0,1},{1,0},{2,3},{3,2},{4,5},{5,4},{6,7},{7,6},{8,9},{9,8},{10,11... | collective-permute-start | bytes 3145736 | tf_op jit(solution)/shard_map/ppermute | solution.py:448
  326.3 405.7 %all-gather.15.cloned.1.call-start = ((), (), s32[]{:S(2)}) async-start(), calls=%async_computation.4 | async-start | bytes 8912896 | tf_op jit(solution)/shard_map/all_gather | solution.py:895
  329.2 161.9 %collective-permute-start.14 = (bf16[512,1024]{1,0:T(8,128)(2,1)}, bf16[512,1024]{1,0:T(8,128)(2,1)}, u32[]{:S(2)}, u32[]{:S(2)}) collective-permute-start(bf16[512,1024]{1,0:T(8,128)(2,1)} %dynamic-slice_convert_fusion.1), channel_id=1, source_target_pairs={{0,1},{1,0},{2,3},{3,2},{4,5},{5,4},{6,7},{7,6},{8,9},{9,8},{10,11... | collective-permute-start | bytes 3145736 | tf_op jit(solution)/shard_map/ppermute | solution.py:448
  391.1 38.3 %collective-permute-start.10 = (bf16[256,1024]{1,0:T(8,128)(2,1)}, bf16[256,1024]{1,0:T(8,128)(2,1)S(1)}, u32[]{:S(2)}, u32[]{:S(2)}) collective-permute-start(bf16[256,1024]{1,0:T(8,128)(2,1)} %bitcast.35), channel_id=1, source_target_pairs={{0,2},{2,0},{4,6},{6,4},{8,10},{10,8},{12,14},{14,12},{16,18},{18,... | collective-permute-start | bytes 1572872 | tf_op jit(solution)/shard_map/ppermute | solution.py:452
  430.4 60.7 %collective-permute-start.16 = (bf16[128,1024]{1,0:T(8,128)(2,1)}, bf16[128,1024]{1,0:T(8,128)(2,1)}, u32[]{:S(2)}, u32[]{:S(2)}) collective-permute-start(bf16[128,1024]{1,0:T(8,128)(2,1)} %bitcast.47), channel_id=1, source_target_pairs={{0,1},{1,0},{2,3},{3,2},{4,5},{5,4},{6,7},{7,6},{8,9},{9,8},{10,11... | collective-permute-start | bytes 786440 | tf_op jit(solution)/shard_map/ppermute | solution.py:448
  491.1 47.4 %collective-permute-start.21 = (bf16[128,1024]{1,0:T(8,128)(2,1)S(1)}, bf16[128,1024]{1,0:T(8,128)(2,1)S(1)}, u32[]{:S(2)}, u32[]{:S(2)}) collective-permute-start(bf16[128,1024]{1,0:T(8,128)(2,1)S(1)} %bitcast.476), channel_id=1, source_target_pairs={{0,1},{1,0},{2,3},{3,2},{4,5},{5,4},{6,7},{7,6},{8,9},{9,8},{10,11... | collective-permute-start | bytes 786440 | tf_op jit(solution)/shard_map/ppermute | solution.py:448
  491.1 49.2 %collective-permute-start.20 = (bf16[256,1536]{1,0:T(8,128)(2,1)S(1)}, bf16[256,1536]{1,0:T(8,128)(2,1)}, u32[]{:S(2)}, u32[]{:S(2)}) collective-permute-start(bf16[256,1536]{1,0:T(8,128)(2,1)S(1)} %bitcast.466), channel_id=1, source_target_pairs={{0,4},{2,6},{4,0},{6,2},{8,12},{10,14},{12,8},{14,10},{16,20},{18,... | collective-permute-start | bytes 2359304 | tf_op jit(solution)/shard_map/ppermute | solution.py:452
  508.5 39.8 %collective-permute-start.22 = (bf16[128,1024]{1,0:T(8,128)(2,1)S(1)}, bf16[128,1024]{1,0:T(8,128)(2,1)S(1)}, u32[]{:S(2)}, u32[]{:S(2)}) collective-permute-start(bf16[128,1024]{1,0:T(8,128)(2,1)S(1)} %fusion.89), channel_id=1, source_target_pairs={{0,4},{2,6},{4,0},{6,2},{8,12},{10,14},{12,8},{14,10},{16,20},{18,... | collective-permute-start | bytes 786440 | tf_op jit(solution)/shard_map/ppermute | solution.py:452
  508.9 39.3 %collective-permute-start.19 = (bf16[256,1536]{1,0:T(8,128)(2,1)S(1)}, bf16[256,1536]{1,0:T(8,128)(2,1)}, u32[]{:S(2)}, u32[]{:S(2)}) collective-permute-start(bf16[256,1536]{1,0:T(8,128)(2,1)S(1)} %fusion.64), channel_id=1, source_target_pairs={{0,1},{1,0},{2,3},{3,2},{4,5},{5,4},{6,7},{7,6},{8,9},{9,8},{10,11... | collective-permute-start | bytes 2359304 | tf_op jit(solution)/shard_map/ppermute | solution.py:448
  548.3 256.2 %all-gather.17.cloned.1.call-start = ((), (), s32[]{:S(2)}) async-start(), calls=%async_computation.5 | async-start | bytes 4456448 | tf_op jit(solution)/shard_map/all_gather | solution.py:911
  555.0 73.5 %collective-permute-start.27 = (bf16[512,1024]{1,0:T(8,128)(2,1)}, bf16[512,1024]{1,0:T(8,128)(2,1)}, u32[]{:S(2)}, u32[]{:S(2)}) collective-permute-start(bf16[512,1024]{1,0:T(8,128)(2,1)} %bitcast.66), channel_id=1, source_target_pairs={{0,1},{1,0},{2,3},{3,2},{4,5},{5,4},{6,7},{7,6},{8,9},{9,8},{10,11... | collective-permute-start | bytes 3145736 | tf_op jit(solution)/shard_map/ppermute | solution.py:448
  591.8 46.4 %collective-permute-start.29 = (bf16[64,1536]{1,0:T(8,128)(2,1)}, bf16[64,1536]{1,0:T(8,128)(2,1)}, u32[]{:S(2)}, u32[]{:S(2)}) collective-permute-start(bf16[64,1536]{1,0:T(8,128)(2,1)} %dynamic-slice_bitcast_fusion.7), channel_id=1, source_target_pairs={{0,16},{2,18},{4,20},{6,22},{8,24},{10,26},{12,28},{14,30},{16,0},... | collective-permute-start | bytes 589832 | tf_op jit(solution)/shard_map/ppermute | solution.py:452
  595.2 43.0 %collective-permute-start.31 = (bf16[256,1024]{1,0:T(8,128)(2,1)}, bf16[256,1024]{1,0:T(8,128)(2,1)}, u32[]{:S(2)}, u32[]{:S(2)}) collective-permute-start(bf16[256,1024]{1,0:T(8,128)(2,1)} %bitcast.76), channel_id=1, source_target_pairs={{0,2},{2,0},{4,6},{6,4},{8,10},{10,8},{12,14},{14,12},{16,18},{18,... | collective-permute-start | bytes 1572872 | tf_op jit(solution)/shard_map/ppermute | solution.py:452
  596.2 42.0 %collective-permute-start.32 = (bf16[256,1024]{1,0:T(8,128)(2,1)}, bf16[256,1024]{1,0:T(8,128)(2,1)}, u32[]{:S(2)}, u32[]{:S(2)}) collective-permute-start(bf16[256,1024]{1,0:T(8,128)(2,1)} %bitcast.78), channel_id=1, source_target_pairs={{0,2},{2,0},{4,6},{6,4},{8,10},{10,8},{12,14},{14,12},{16,18},{18,... | collective-permute-start | bytes 1572872 | tf_op jit(solution)/shard_map/ppermute | solution.py:452
  598.9 43.4 %collective-permute-start.28 = (bf16[512,1024]{1,0:T(8,128)(2,1)}, bf16[512,1024]{1,0:T(8,128)(2,1)}, u32[]{:S(2)}, u32[]{:S(2)}) collective-permute-start(bf16[512,1024]{1,0:T(8,128)(2,1)} %bitcast.68), channel_id=1, source_target_pairs={{0,4},{2,6},{4,0},{6,2},{8,12},{10,14},{12,8},{14,10},{16,20},{18,... | collective-permute-start | bytes 3145736 | tf_op jit(solution)/shard_map/ppermute | solution.py:452
  636.7 49.7 %collective-permute-start.33 = (bf16[512,1024]{1,0:T(8,128)(2,1)}, bf16[512,1024]{1,0:T(8,128)(2,1)}, u32[]{:S(2)}, u32[]{:S(2)}) collective-permute-start(bf16[512,1024]{1,0:T(8,128)(2,1)} %bitcast.79), channel_id=1, source_target_pairs={{0,1},{1,0},{2,3},{3,2},{4,5},{5,4},{6,7},{7,6},{8,9},{9,8},{10,11... | collective-permute-start | bytes 3145736 | tf_op jit(solution)/shard_map/ppermute | solution.py:448
  638.2 48.5 %collective-permute-start.36 = (bf16[512,1024]{1,0:T(8,128)(2,1)}, bf16[512,1024]{1,0:T(8,128)(2,1)}, u32[]{:S(2)}, u32[]{:S(2)}) collective-permute-start(bf16[512,1024]{1,0:T(8,128)(2,1)} %bitcast.84), channel_id=1, source_target_pairs={{0,4},{2,6},{4,0},{6,2},{8,12},{10,14},{12,8},{14,10},{16,20},{18,... | collective-permute-start | bytes 3145736 | tf_op jit(solution)/shard_map/ppermute | solution.py:452
  644.9 42.0 %collective-permute-start.34 = (bf16[512,1024]{1,0:T(8,128)(2,1)}, bf16[512,1024]{1,0:T(8,128)(2,1)}, u32[]{:S(2)}, u32[]{:S(2)}) collective-permute-start(bf16[512,1024]{1,0:T(8,128)(2,1)} %fusion.55), channel_id=1, source_target_pairs={{0,4},{2,6},{4,0},{6,2},{8,12},{10,14},{12,8},{14,10},{16,20},{18,... | collective-permute-start | bytes 3145736 | tf_op jit(solution)/shard_map/ppermute | solution.py:452
  647.9 39.0 %collective-permute-start.35 = (bf16[512,1024]{1,0:T(8,128)(2,1)}, bf16[512,1024]{1,0:T(8,128)(2,1)}, u32[]{:S(2)}, u32[]{:S(2)}) collective-permute-start(bf16[512,1024]{1,0:T(8,128)(2,1)} %fusion.54), channel_id=1, source_target_pairs={{0,1},{1,0},{2,3},{3,2},{4,5},{5,4},{6,7},{7,6},{8,9},{9,8},{10,11... | collective-permute-start | bytes 3145736 | tf_op jit(solution)/shard_map/ppermute | solution.py:448
  677.3 215.8 %all-gather.19.cloned.1.call-start = ((), (), s32[]{:S(2)}) async-start(), calls=%async_computation.6 | async-start | bytes 8912896 | tf_op jit(solution)/shard_map/all_gather | solution.py:911
  (206 other events, 2831.2 us)
Sparse Core Ops, SparseCore 0:
  20.5 52.0 all-gather.10
  74.9 120.1 all-gather.12
  326.4 216.0 reduce-scatter.1
  548.4 106.1 all-gather.14
  677.4 62.4 all-gather.16
  766.7 97.5 all-gather.18

commit v6 on v5

--- a/solution.py
+++ b/solution.py
@@ -1013,14 +1013,14 @@
     def unpacked(whole, kinds):
         return dict(zip(kinds, unpack_halves(whole, [flat_shape[kind] for kind in kinds])))
 
-    attn_kinds, all_kinds = ("qkv", "out"), ("qkv", "out", "up", "down")
+    attn_kinds, hidden_kinds = ("qkv", "out"), ("up", "down")
     rows_away, first_send = pin(away_rows(frames_in), packed(0, attn_kinds))
     other_rows = swap_tensor(rows_away)
     first_pack = swap_tensor(first_send)
     own_qkv = [flat_qkv(stacked, layer) for layer in range(2)]
     first_pack, own_qkv = pin(first_pack, own_qkv)
     first_whole = gathered(first_pack)
-    second_send = packed(1, all_kinds)
+    attn_send, hidden_send = packed(1, attn_kinds), packed(1, hidden_kinds)
     piece_rows, piece_columns = model_width // 2, w_up.shape[2] // 2
     up_send = lax.dynamic_slice(
         w_up, (0, near_row * piece_rows, core * piece_columns), (1, piece_rows, piece_columns)
@@ -1029,32 +1029,37 @@
     down_send = lax.dynamic_slice(
         w_down, (0, (2 * core + near_row) * piece_rows, 0), (1, piece_rows, model_width)
     )[0]
-    other_rows, second_send, up_send, down_send, own_qkv = pin(
-        other_rows, second_send, up_send, down_send, own_qkv
-    )
-    second_pack = swap_tensor(second_send)
+    other_rows, attn_send, hidden_send, up_send, down_send, own_qkv = pin(
+        other_rows, attn_send, hidden_send, up_send, down_send, own_qkv
+    )
+    up_piece = swap_tensor(up_send)
     rows = whole_rows(frames_in, other_rows).astype(f32)
     normed, norm_kept = norm_forward(rows, gains[0][0], shifts[0][0])
     mine = dot_low(normed, own_qkv[0], NN)
-    mine, second_pack, up_send, down_send = pin(mine, second_pack, up_send, down_send)
-    second_whole = gathered(second_pack)
-    up_piece = swap_tensor(up_send)
     mix_mine = attn_fwd(mine, limits, True, 512)
-    mix_mine, up_piece, down_send = pin(mix_mine, up_piece, down_send)
+    mix_mine, up_piece, attn_send, down_send = pin(mix_mine, up_piece, attn_send, down_send)
+    attn_pack = swap_tensor(attn_send)
+    up_there = swap_bit(up_piece, 1, dp_size)
     down_piece = swap_tensor(down_send)
-    up_there = swap_bit(up_piece, 1, dp_size)
     first = unpacked(first_whole, attn_kinds)
     theirs = dot_low(normed, first["qkv"], NN)
     mix_theirs = attn_fwd(theirs, limits, True, 512)
-    mix_theirs, up_there, down_piece = pin(mix_theirs, up_there, down_piece)
+    mix_theirs, up_there, down_piece, hidden_send, attn_pack = pin(
+        mix_theirs, up_there, down_piece, hidden_send, attn_pack
+    )
+    attn_whole = gathered(attn_pack)
     up_near = in_order(near_row, up_piece, up_there)
     up_far = swap_bit(up_near, 0, dp_size)
     down_there = swap_bit(down_piece, 1, dp_size)
+    hidden_pack = swap_tensor(hidden_send)
     kept = [(normed, norm_kept, [mine, theirs], [mix_mine, mix_theirs])]
     rows = rows + dot_sum([(mix_mine[0], w_out[0]), (mix_theirs[0], first["out"])], NN)
     normed, norm_kept = norm_forward(rows, gains[0][1], shifts[0][1])
     pair_own = gelu_pair(jnp.dot(normed, w_up[0], preferred_element_type=f32))
-    pair_own, up_far, normed, norm_kept, rows = pin(pair_own, up_far, normed, norm_kept, rows)
+    pair_own, up_far, normed, norm_kept, rows, hidden_pack = pin(
+        pair_own, up_far, normed, norm_kept, rows, hidden_pack
+    )
+    hidden_whole = gathered(hidden_pack)
     pair_near = gelu_pair(jnp.dot(normed, up_near, preferred_element_type=f32))
     pair_far = gelu_pair(jnp.dot(normed, up_far, preferred_element_type=f32))
     rows = rows + dot_sum([(pair_own[0], w_down[0])], NN)
@@ -1071,8 +1076,24 @@
     normed, norm_kept = norm_forward(rows, gains[1][0], shifts[1][0])
     mine = dot_low(normed, own_qkv[1], NN)
     mix_mine = attn_fwd(mine, limits, False, 512)
-    mix_mine, second_whole = pin(mix_mine, second_whole)
-    second = unpacked(second_whole, all_kinds)
+    mix_mine, attn_whole = pin(mix_mine, attn_whole)
+    second = unpacked(attn_whole, attn_kinds)
+    theirs = dot_low(normed, second["qkv"], NN)
+    mix_theirs = attn_fwd(theirs, limits, False, 512)
+    mixed = [mix_mine, mix_theirs]
+    kept.append((normed, norm_kept, [mine, theirs], mixed))
+    rows = rows + dot_sum([(mix_mine[0], w_out[1]), (mix_theirs[0], second["out"])], NN)
+    normed, norm_kept = norm_forward(rows, gains[1][1], shifts[1][1])
+    pair_own = gelu_pair(jnp.dot(normed, w_up[1], preferred_element_type=f32))
+    pair_own, rows, normed, norm_kept = pin(pair_own, rows, normed, norm_kept)
+    rows = rows + dot_sum([(pair_own[0], w_down[1])], NN)
+    rows, hidden_whole = pin(rows, hidden_whole)
+    second.update(unpacked(hidden_whole, hidden_kinds))
+    pair_other = gelu_pair(jnp.dot(normed, second["up"], preferred_element_type=f32))
+    pair_other, rows = pin(pair_other, rows)
+    rows = rows + dot_sum([(pair_other[0], second["down"])], NN)
+    pairs = [pair_own, pair_other]
+    kept.append((normed, norm_kept, pairs))
     weights = [
         {
             "qkv": [own_qkv[0], first["qkv"]],
@@ -1087,16 +1108,6 @@
             "down": [w_down[1], second["down"]],
         },
     ]
-    theirs = dot_low(normed, second["qkv"], NN)
-    mix_theirs = attn_fwd(theirs, limits, False, 512)
-    mixed = [mix_mine, mix_theirs]
-    kept.append((normed, norm_kept, [mine, theirs], mixed))
-    rows = rows + dot_sum([(mix[0], part) for mix, part in zip(mixed, weights[1]["out"])], NN)
-    normed, norm_kept = norm_forward(rows, gains[1][1], shifts[1][1])
-    pairs = [gelu_pair(jnp.dot(normed, part, preferred_element_type=f32)) for part in weights[1]["up"]]
-    pairs, rows, normed, norm_kept = pin(pairs, rows, normed, norm_kept)
-    rows = rows + dot_sum([(pair[0], part) for pair, part in zip(pairs, weights[1]["down"])], NN)
-    kept.append((normed, norm_kept, pairs))
     rows, grad_other = pin(rows, grad_other)
 
     def halves_of(block):
@@ -1187,7 +1198,7 @@
     parts, low, grad_rows = move((parts, low, grad_rows), out1, qkv1)
     start_quarters(down0, "down", parts)
     hidden = hidden_grads(0, low)
-    hidden, grad_rows, out_there = move((hidden, grad_rows, out_there), qkv1, out1, hold=[down0])
+    hidden, grad_rows, out_there = move((hidden, grad_rows, out_there), hold=[down0])
     parts = up_grads(0, hidden)
     grad_normed = dot_sum(list(zip(hidden, weights[0]["up"])), NT)
     parts, grad_normed, grad_rows = move((parts, grad_normed, grad_rows), qkv1, out1, down0, pair1)
@@ -1203,13 +1214,13 @@
     part_theirs, mine, theirs, grad_rows = move(
         (part_theirs, mine, theirs, grad_rows), down0, up0, qkv1, out1, hold=[out0]
     )
-    joint1 = Gather(qkv1, out1, PACK_WIDTH, True)
     qkv0.start_other(part_theirs)
     mine = attention_grad(0, 0, mine)
     part_mine = dot_low(kept[0][0], mine, TN)
     part_mine, mine, theirs, grad_rows = move(
-        (part_mine, mine, theirs, grad_rows), down0, up0, out0, qkv0
-    )
+        (part_mine, mine, theirs, grad_rows), down0, up0, out0, qkv0, qkv1, out1
+    )
+    joint1 = Gather(qkv1, out1, PACK_WIDTH, True)
     qkv0.add_own(part_mine)
     grad_normed = dot_sum([(mine, weights[0]["qkv"][0]), (theirs, weights[0]["qkv"][1])], NT)
     grad_rows = norm_step(0, 0, grad_rows, grad_normed)
@@ -1234,10 +1245,10 @@
     joint_bases = place_joint(joint1.whole, 1, *shapes, None)
     frames_grad = place_frames(side, grad_mine, grad_there)
     joint_bases, frames_grad = move((joint_bases, frames_grad), joint0, late)
-    joint_bases, frames_grad = move((joint_bases, frames_grad), joint0, late)
-    (joint_bases,) = move((joint_bases,), joint0, pair0)
+    joint_bases, frames_grad = move((joint_bases, frames_grad), joint0, pair0)
     grad_up = place_quarters("up", pair0.whole, 1, 0, bases["up"])
     grad_down = place_quarters("down", pair0.whole, 0, 0, bases["down"])
+    joint_bases, grad_up, grad_down = move((joint_bases, grad_up, grad_down), joint0, late)
     while joint0.flight:
         joint0.advance(joint0.flight)
     while late.flight:

time: 925 us -> 899 us (0.972)
  waiting for transfers between devices: 206 us -> 177 us
    ppermute x18 -> x19, waiting for transfers between devices: 34.1 us -> 18.9 us  [swap_tensor(): return lax.ppermute(block, 'tensor', [(0, 1), (1, 0)])]
    ppermute x45, waiting for transfers between devices: 171 us -> 157 us  [swap_bit(): lax.ppermute(block, 'dp', [(place, place ^ 1 << bit) for place in range(d...]
    unnamed x332 -> x344, local copies, waits for them, and re-layouts: 31.1 us -> 38.8 us
    ppermute x18 -> x19, starting transfers between devices: 21.9 us -> 21.8 us  [swap_tensor(): return lax.ppermute(block, 'tensor', [(0, 1), (1, 0)])]
  transfers between devices with their start and end apart: 69 -> 71, of which waited for: 23 -> 20; matrix products, arithmetic and copies ran while one was open for 38% -> 38% of each run, Pallas kernels for 23% -> 23%
where the time goes in v6:
time: 899 us; the launch traced here: 895 us
  matrix products  252 us (28%)
  Pallas kernels  220 us (24%)
  waiting for transfers between devices  177 us (20%)
  other arithmetic  86.4 us (10%)
  local copies, waits for them, and re-layouts  81.4 us (9%)
  starting transfers between devices  60.7 us (7%)
  between operations  17.3 us (2%)
    ppermute x45, waiting for transfers between devices, swap_bit(): lax.ppermute(block, 'dp', [(place, place ^ 1 << bit) for place in range(d...  157 us
    pallas_call x4, Pallas kernels, attn_bwd(): pl.pallas_call(partial(bwd_kernel, causal, bq), grid=(pairs,), in_specs=[...  103 us
    dot_general x26, matrix products, dot_low(): lax.dot_general(left, right, dims, preferred_element_type=f32).astype(bf16)  90.6 us
    dot_general x18, matrix products, dot_sum(): term = lax.dot_general(left, right, dims, preferred_element_type=f32)  85.6 us
    pallas_call x4, Pallas kernels, attn_fwd(): pl.pallas_call(partial(fwd_kernel, causal, bq), grid=(pairs,), in_specs=[...  65.6 us
    unnamed x344, local copies, waits for them, and re-layouts  38.8 us
    ppermute x45, starting transfers between devices, swap_bit(): lax.ppermute(block, 'dp', [(place, place ^ 1 << bit) for place in range(d...  38.1 us
    convert_element_type x30, other arithmetic, add_rounded(): return (left.astype(f32) + right.astype(f32)).astype(bf16)  33 us
  transfers between devices with their start and end apart: 71, of which 20 were waited for; matrix products, arithmetic and copies ran while one was open for 38% of the time, Pallas kernels for 23%

profile of v6, /device:TPU:0, one launch (start us, length us, event | category | flops | bytes accessed | tf_op | source)
XLA Modules:
  0.0 894.6 jit_solution(4474329615878710731)
XLA Ops:
  31.9 13.1 %collective-permute-done = bf16[512,1024]{1,0:T(8,128)(2,1)S(1)} collective-permute-done((bf16[512,1024]{1,0:T(8,128)(2,1)S(1)}, bf16[512,1024]{1,0:T(8,128)(2,1)S(1)}, u32[]{:S(2)}, u32[]{:S(2)}) %collective-permute-start) | collective-permute-done | bytes 1048608 | tf_op jit(solution)/shard_map/ppermute | solution.py:448
  53.2 14.0 %attn_fwd_causal.2 = (bf16[1024,512]{1,0:T(8,128)(2,1)S(1)}, f32[4,2,1024]{2,1,0:T(2,128)S(1)}) custom-call(s32[2]{0:T(128)S(1)} %pad_add_fusion.lims_ref, bf16[1024,1536]{1,0:T(8,128)(2,1)S(1)} %convolution_convert_fusion.7.q_ref.k_ref.v_ref, bf16[1024,1536]{1,0:T(8,128)(2,1)S(1)} %convolution_convert_fusion.7.q_ref.k_ref.v_ref, ...), custom_call_target="tpu_custom_call" | custom-call | flops 4194304 | bytes 4194304 | tf_op jit(solution)/shard_map/attn_fwd_causal/pallas_call | solution.py:381
  82.0 14.0 %attn_fwd_causal.3 = (bf16[1024,512]{1,0:T(8,128)(2,1)S(1)}, f32[4,2,1024]{2,1,0:T(2,128)S(1)}) custom-call(s32[2]{0:T(128)S(1)} %pad_add_fusion.lims_ref, bf16[1024,1536]{1,0:T(8,128)(2,1)S(1)} %convolution_convert_fusion.6.q_ref.k_ref.v_ref, bf16[1024,1536]{1,0:T(8,128)(2,1)S(1)} %convolution_convert_fusion.6.q_ref.k_ref.v_ref, ...), custom_call_target="tpu_custom_call" | custom-call | flops 4194304 | bytes 4194304 | tf_op jit(solution)/shard_map/attn_fwd_causal/pallas_call | solution.py:381
  108.3 9.6 %add_convert_fusion.2 = (bf16[1024,2048]{1,0:T(8,128)(2,1)}, bf16[1024,2048]{1,0:T(8,128)(2,1)}) fusion(bf16[1024,1024]{1,0:T(8,128)(2,1)S(1)} %add_convert_fusion.11, bf16[2,1024,2048]{2,1,0:T(8,128)(2,1)S(1)} %bitcast.427), kind=kOutput, calls=%fused_computation.11 | convolution fusion | flops 4326424576 | bytes 14680064 | tf_op jit(solution)/shard_map/dot_general | solution.py:1058
  140.8 14.0 %collective-permute-done.8 = bf16[512,1024]{1,0:T(8,128)(2,1)S(1)} collective-permute-done((bf16[512,1024]{1,0:T(8,128)(2,1)}, bf16[512,1024]{1,0:T(8,128)(2,1)S(1)}, u32[]{:S(2)}, u32[]{:S(2)}) %collective-permute-start.8) | collective-permute-done | bytes 1048608 | tf_op jit(solution)/shard_map/ppermute | solution.py:452
  174.3 18.7 %attn_fwd_full.2 = (bf16[1024,512]{1,0:T(8,128)(2,1)S(1)}, f32[4,2,1024]{2,1,0:T(2,128)S(1)}) custom-call(s32[2]{0:T(128)S(1)} %pad_add_fusion.lims_ref, bf16[1024,1536]{1,0:T(8,128)(2,1)S(1)} %convolution_convert_fusion.5.q_ref.k_ref.v_ref, bf16[1024,1536]{1,0:T(8,128)(2,1)S(1)} %convolution_convert_fusion.5.q_ref.k_ref.v_ref, ...), custom_call_target="tpu_custom_call" | custom-call | flops 4194304 | bytes 4194304 | tf_op jit(solution)/shard_map/attn_fwd_full/pallas_call | solution.py:381
  204.0 18.7 %attn_fwd_full.3 = (bf16[1024,512]{1,0:T(8,128)(2,1)S(1)}, f32[4,2,1024]{2,1,0:T(2,128)S(1)}) custom-call(s32[2]{0:T(128)S(1)} %pad_add_fusion.lims_ref, bf16[1024,1536]{1,0:T(8,128)(2,1)S(1)} %convolution_convert_fusion.4.q_ref.k_ref.v_ref, bf16[1024,1536]{1,0:T(8,128)(2,1)S(1)} %convolution_convert_fusion.4.q_ref.k_ref.v_ref, ...), custom_call_target="tpu_custom_call" | custom-call | flops 4194304 | bytes 4194304 | tf_op jit(solution)/shard_map/attn_fwd_full/pallas_call | solution.py:381
  228.3 12.7 %add_convert_fusion.1 = (bf16[1024,2048]{1,0:T(8,128)(2,1)}, bf16[1024,2048]{1,0:T(8,128)(2,1)S(1)}) fusion(bf16[1024,1024]{1,0:T(8,128)(2,1)S(1)} %add_convert_fusion.7, bf16[2,1024,2048]{2,1,0:T(8,128)(2,1)} %refs_0_.1), kind=kOutput, calls=%fused_computation.7 | convolution fusion | flops 4326424576 | bytes 14680064 | tf_op jit(solution)/shard_map/dot_general | solution.py:1087
  253.0 9.2 %add_convert_fusion = (bf16[1024,2048]{1,0:T(8,128)(2,1)}, bf16[1024,2048]{1,0:T(8,128)(2,1)S(1)}) fusion(bf16[1024,1024]{1,0:T(8,128)(2,1)S(1)} %add_convert_fusion.7, bf16[1024,2048]{1,0:T(8,128)(2,1)S(1)} %get-tuple-element.261), kind=kOutput, calls=%fused_computation.3 | convolution fusion | flops 4326424576 | bytes 14680064 | tf_op jit(solution)/shard_map/dot_general | solution.py:1092
  317.6 10.6 %fusion.130 = f32[1024,1024]{1,0:T(8,128)} fusion(bf16[1024,2048]{1,0:T(8,128)(2,1)} %multiply_convert_fusion.1, bf16[1024,2048]{1,0:T(8,128)(2,1)} %copy-done.22), kind=kOutput, calls=%fused_computation.361 | convolution fusion | flops 4294967296 | bytes 12582912 | tf_op jit(solution)/shard_map/dot_general | solution.py:497
  328.2 11.0 %multiply_reduce_fusion = (f32[1024]{0:T(1024)S(1)}, f32[1024]{0:T(1024)S(1)}, f32[1024]{0:T(1024)S(1)}, f32[1024]{0:T(1024)S(1)}, f32[1024,1024]{1,0:T(8,128)}) fusion(f32[1024,1024]{1,0:T(8,128)S(1)} %copy-done.36, f32[1024]{0:T(1024)S(1)} %broadcast_multiply_fusion.12, f32[1024]{0:T(1024)S(1)} %add_rsqrt_fusion, f32[1024]{0:T(1024)S(1)} %get-tuple-element.444, ...), kind=kOutput, calls=%fused_computation.47 | convolution fusion | flops 4305448960 | bytes 21000192 | tf_op jit(solution)/shard_map/dot_general | solution.py:497
  345.2 28.9 %attn_bwd_full.2 = bf16[1024,1536]{1,0:T(8,128)(2,1)S(1)} custom-call(s32[2]{0:T(128)S(1)} %pad_add_fusion.lims_ref, bf16[1024,1536]{1,0:T(8,128)(2,1)} %copy-done.3, bf16[1024,1536]{1,0:T(8,128)(2,1)} %copy-done.3, bf16[1024,1536]{1,0:T(8,128)(2,1)} %copy-done.3, f32[4,2,1024]{2,1,0:T(2,128)S(1)} %get-tuple-element.281.l_ref, ...), custom_call_target="tpu_custom_call" | custom-call | flops 4194304 | bytes 4194304 | tf_op jit(solution)/shard_map/attn_bwd_full/pallas_call | solution.py:431
  379.6 29.5 %attn_bwd_full.3 = bf16[1024,1536]{1,0:T(8,128)(2,1)S(1)} custom-call(s32[2]{0:T(128)S(1)} %pad_add_fusion.lims_ref, bf16[1024,1536]{1,0:T(8,128)(2,1)} %copy-done.2, bf16[1024,1536]{1,0:T(8,128)(2,1)} %copy-done.2, bf16[1024,1536]{1,0:T(8,128)(2,1)} %copy-done.2, f32[4,2,1024]{2,1,0:T(2,128)S(1)} %get-tuple-element.250.l_ref, ...), custom_call_target="tpu_custom_call" | custom-call | flops 4194304 | bytes 4194304 | tf_op jit(solution)/shard_map/attn_bwd_full/pallas_call | solution.py:431
  467.2 9.0 %multiply_convert_fusion = bf16[1024,2048]{1,0:T(8,128)(2,1)} fusion(bf16[1024,2048]{1,0:T(8,128)(2,1)} %get-tuple-element.293, bf16[1024,1024]{1,0:T(8,128)(2,1)} %copy-done.90, bf16[2,2048,1024]{2,1,0:T(8,128)(2,1)S(1)} %bitcast.425), kind=kOutput, calls=%fused_computation | convolution fusion | flops 4301258752 | bytes 14680064 | tf_op jit(solution)/shard_map/dot_general | solution.py:1140
  569.7 22.3 %attn_bwd_causal.2 = bf16[1024,1536]{1,0:T(8,128)(2,1)S(1)} custom-call(s32[2]{0:T(128)S(1)} %copy-done.21, bf16[1024,1536]{1,0:T(8,128)(2,1)} %copy-done.1, bf16[1024,1536]{1,0:T(8,128)(2,1)} %copy-done.1, bf16[1024,1536]{1,0:T(8,128)(2,1)} %copy-done.1, f32[4,2,1024]{2,1,0:T(2,128)S(1)} %get-tuple-element.229.l_ref, ...), custom_call_target="tpu_custom_call" | custom-call | flops 4194304 | bytes 4194304 | tf_op jit(solution)/shard_map/attn_bwd_causal/pallas_call | solution.py:431
  600.0 8.5 collective-permute-done.29
  621.7 22.6 %attn_bwd_causal.3 = bf16[1024,1536]{1,0:T(8,128)(2,1)S(1)} custom-call(s32[2]{0:T(128)S(1)} %copy-done.21, bf16[1024,1536]{1,0:T(8,128)(2,1)} %copy-done, bf16[1024,1536]{1,0:T(8,128)(2,1)} %copy-done, bf16[1024,1536]{1,0:T(8,128)(2,1)} %copy-done, f32[4,2,1024]{2,1,0:T(2,128)S(1)} %get-tuple-element.220.l_ref, ...), custom_call_target="tpu_custom_call" | custom-call | flops 4194304 | bytes 4194304 | tf_op jit(solution)/shard_map/attn_bwd_causal/pallas_call | solution.py:431
  654.1 10.5 %collective-permute-done.38 = bf16[32,1024]{1,0:T(8,128)(2,1)S(1)} collective-permute-done((bf16[32,1024]{1,0:T(8,128)(2,1)S(1)}, bf16[32,1024]{1,0:T(8,128)(2,1)S(1)}, u32[]{:S(2)}, u32[]{:S(2)}) %collective-permute-start.38) | collective-permute-done | bytes 65568 | tf_op jit(solution)/shard_map/ppermute | solution.py:452
  720.7 21.3 %collective-permute-done.48 = bf16[128,1024]{1,0:T(8,128)(2,1)S(1)} collective-permute-done((bf16[128,1024]{1,0:T(8,128)(2,1)S(1)}, bf16[128,1024]{1,0:T(8,128)(2,1)S(1)}, u32[]{:S(2)}, u32[]{:S(2)}) %collective-permute-start.48) | collective-permute-done | bytes 262176 | tf_op jit(solution)/shard_map/ppermute | solution.py:452
  767.0 17.7 %collective-permute-done.54 = bf16[64,1024]{1,0:T(8,128)(2,1)S(1)} collective-permute-done((bf16[64,1024]{1,0:T(8,128)(2,1)S(1)}, bf16[64,1024]{1,0:T(8,128)(2,1)S(1)}, u32[]{:S(2)}, u32[]{:S(2)}) %collective-permute-start.54) | collective-permute-done | bytes 131104 | tf_op jit(solution)/shard_map/ppermute | solution.py:452
  788.1 22.6 %collective-permute-done.57 = bf16[32,1024]{1,0:T(8,128)(2,1)S(1)} collective-permute-done((bf16[32,1024]{1,0:T(8,128)(2,1)S(1)}, bf16[32,1024]{1,0:T(8,128)(2,1)S(1)}, u32[]{:S(2)}, u32[]{:S(2)}) %collective-permute-start.57) | collective-permute-done | bytes 65568 | tf_op jit(solution)/shard_map/ppermute | solution.py:452
  825.0 17.1 %collective-permute-done.60 = f32[32,1024]{1,0:T(8,128)S(1)} collective-permute-done((f32[32,1024]{1,0:T(8,128)S(1)}, f32[32,1024]{1,0:T(8,128)S(1)}, u32[]{:S(2)}, u32[]{:S(2)}) %collective-permute-start.60) | collective-permute-done | bytes 131104 | tf_op jit(solution)/shard_map/ppermute | solution.py:452
  842.3 12.0 %collective-permute-done.61 = bf16[2,256,512]{2,1,0:T(8,128)(2,1)S(1)} collective-permute-done((bf16[2,256,512]{2,1,0:T(8,128)(2,1)S(1)}, bf16[2,256,512]{2,1,0:T(8,128)(2,1)S(1)}, u32[]{:S(2)}, u32[]{:S(2)}) %collective-permute-start.61) | collective-permute-done | bytes 524320 | tf_op jit(solution)/shard_map/ppermute | solution.py:452
  866.2 10.7 %collective-permute-done.62 = bf16[4,256,512]{2,1,0:T(8,128)(2,1)S(1)} collective-permute-done((bf16[4,256,512]{2,1,0:T(8,128)(2,1)S(1)}, bf16[4,256,512]{2,1,0:T(8,128)(2,1)S(1)}, u32[]{:S(2)}, u32[]{:S(2)}) %collective-permute-start.62) | collective-permute-done | bytes 1048608 | tf_op jit(solution)/shard_map/ppermute | solution.py:452
  (698 shorter events, 498.8 us)
Async XLA Ops:
  7.2 65.7 %all-gather.13.cloned.1.call-start = ((), (), s32[]{:S(2)}) async-start(), calls=%async_computation.2 | async-start | bytes 4456448 | tf_op jit(solution)/shard_map/all_gather | solution.py:1011
  20.4 174.4 %all-gather.15.cloned.1.call-start = ((), (), s32[]{:S(2)}) async-start(), calls=%async_computation.3 | async-start | bytes 4456448 | tf_op jit(solution)/shard_map/all_gather | solution.py:1011
  97.5 151.4 %all-gather.17.cloned.1.call-start = ((), (), s32[]{:S(2)}) async-start(), calls=%async_computation.4 | async-start | bytes 8912896 | tf_op jit(solution)/shard_map/all_gather | solution.py:1011
  118.0 397.1 %reduce-scatter.2.cloned.1.call-start = ((), (), s32[]{:S(2)}) async-start(), calls=%async_computation.1 | async-start | bytes 17301504 | tf_op jit(solution)/shard_map/reduce_scatter | solution.py:890
  161.9 106.3 %collective-permute-start.10 = (bf16[512,1024]{1,0:T(8,128)(2,1)}, bf16[512,1024]{1,0:T(8,128)(2,1)}, u32[]{:S(2)}, u32[]{:S(2)}) collective-permute-start(bf16[512,1024]{1,0:T(8,128)(2,1)} %dynamic-slice_bitcast_fusion), channel_id=1, source_target_pairs={{0,1},{1,0},{2,3},{3,2},{4,5},{5,4},{6,7},{7,6},{8,9},{9,8},{10,11... | collective-permute-start | bytes 3145736 | tf_op jit(solution)/shard_map/ppermute | solution.py:448
  314.0 391.9 %all-gather.19.cloned.1.call-start = ((), (), s32[]{:S(2)}) async-start(), calls=%async_computation.5 | async-start | bytes 8912896 | tf_op jit(solution)/shard_map/all_gather | solution.py:895
  317.1 159.0 %collective-permute-start.15 = (bf16[512,1024]{1,0:T(8,128)(2,1)}, bf16[512,1024]{1,0:T(8,128)(2,1)}, u32[]{:S(2)}, u32[]{:S(2)}) collective-permute-start(bf16[512,1024]{1,0:T(8,128)(2,1)} %dynamic-slice_convert_fusion.1), channel_id=1, source_target_pairs={{0,1},{1,0},{2,3},{3,2},{4,5},{5,4},{6,7},{7,6},{8,9},{9,8},{10,11... | collective-permute-start | bytes 3145736 | tf_op jit(solution)/shard_map/ppermute | solution.py:448
  378.2 41.1 %collective-permute-start.11 = (bf16[256,1024]{1,0:T(8,128)(2,1)S(1)}, bf16[256,1024]{1,0:T(8,128)(2,1)S(1)}, u32[]{:S(2)}, u32[]{:S(2)}) collective-permute-start(bf16[256,1024]{1,0:T(8,128)(2,1)S(1)} %bitcast.475), channel_id=1, source_target_pairs={{0,2},{2,0},{4,6},{6,4},{8,10},{10,8},{12,14},{14,12},{16,18},{18,... | collective-permute-start | bytes 1572872 | tf_op jit(solution)/shard_map/ppermute | solution.py:452
  379.1 40.1 %collective-permute-start.12 = (bf16[256,1024]{1,0:T(8,128)(2,1)}, bf16[256,1024]{1,0:T(8,128)(2,1)S(1)}, u32[]{:S(2)}, u32[]{:S(2)}) collective-permute-start(bf16[256,1024]{1,0:T(8,128)(2,1)} %bitcast.38), channel_id=1, source_target_pairs={{0,2},{2,0},{4,6},{6,4},{8,10},{10,8},{12,14},{14,12},{16,18},{18,... | collective-permute-start | bytes 1572872 | tf_op jit(solution)/shard_map/ppermute | solution.py:452
  420.4 85.9 %collective-permute-start.19 = (bf16[128,1024]{1,0:T(8,128)(2,1)}, bf16[128,1024]{1,0:T(8,128)(2,1)}, u32[]{:S(2)}, u32[]{:S(2)}) collective-permute-start(bf16[128,1024]{1,0:T(8,128)(2,1)} %bitcast.48), channel_id=1, source_target_pairs={{0,1},{1,0},{2,3},{3,2},{4,5},{5,4},{6,7},{7,6},{8,9},{9,8},{10,11... | collective-permute-start | bytes 786440 | tf_op jit(solution)/shard_map/ppermute | solution.py:448
  422.3 127.3 %collective-permute-start.24 = (bf16[128,1024]{1,0:T(8,128)(2,1)}, bf16[128,1024]{1,0:T(8,128)(2,1)}, u32[]{:S(2)}, u32[]{:S(2)}) collective-permute-start(bf16[128,1024]{1,0:T(8,128)(2,1)} %bitcast.56), channel_id=1, source_target_pairs={{0,1},{1,0},{2,3},{3,2},{4,5},{5,4},{6,7},{7,6},{8,9},{9,8},{10,11... | collective-permute-start | bytes 786440 | tf_op jit(solution)/shard_map/ppermute | solution.py:448
  476.2 38.5 %collective-permute-start.18 = (bf16[256,1536]{1,0:T(8,128)(2,1)S(1)}, bf16[256,1536]{1,0:T(8,128)(2,1)}, u32[]{:S(2)}, u32[]{:S(2)}) collective-permute-start(bf16[256,1536]{1,0:T(8,128)(2,1)S(1)} %bitcast.470), channel_id=1, source_target_pairs={{0,4},{2,6},{4,0},{6,2},{8,12},{10,14},{12,8},{14,10},{16,20},{18,... | collective-permute-start | bytes 2359304 | tf_op jit(solution)/shard_map/ppermute | solution.py:452
  515.2 273.0 %all-gather.21.cloned.1.call-start = ((), (), s32[]{:S(2)}) async-start(), calls=%async_computation.6 | async-start | bytes 4456448 | tf_op jit(solution)/shard_map/all_gather | solution.py:911
  551.8 46.6 %collective-permute-start.26 = (bf16[512,1024]{1,0:T(8,128)(2,1)}, bf16[512,1024]{1,0:T(8,128)(2,1)}, u32[]{:S(2)}, u32[]{:S(2)}) collective-permute-start(bf16[512,1024]{1,0:T(8,128)(2,1)} %bitcast.61), channel_id=1, source_target_pairs={{0,1},{1,0},{2,3},{3,2},{4,5},{5,4},{6,7},{7,6},{8,9},{9,8},{10,11... | collective-permute-start | bytes 3145736 | tf_op jit(solution)/shard_map/ppermute | solution.py:448
  561.4 48.3 %collective-permute-start.28 = (bf16[128,1536]{1,0:T(8,128)(2,1)}, bf16[128,1536]{1,0:T(8,128)(2,1)}, u32[]{:S(2)}, u32[]{:S(2)}) collective-permute-start(bf16[128,1536]{1,0:T(8,128)(2,1)} %bitcast.66), channel_id=1, source_target_pairs={{0,8},{2,10},{4,12},{6,14},{8,0},{10,2},{12,4},{14,6},{16,24},{18,... | collective-permute-start | bytes 1179656 | tf_op jit(solution)/shard_map/ppermute | solution.py:452
  564.6 46.3 %collective-permute-start.30 = (bf16[256,1024]{1,0:T(8,128)(2,1)}, bf16[256,1024]{1,0:T(8,128)(2,1)}, u32[]{:S(2)}, u32[]{:S(2)}) collective-permute-start(bf16[256,1024]{1,0:T(8,128)(2,1)} %bitcast.71), channel_id=1, source_target_pairs={{0,2},{2,0},{4,6},{6,4},{8,10},{10,8},{12,14},{14,12},{16,18},{18,... | collective-permute-start | bytes 1572872 | tf_op jit(solution)/shard_map/ppermute | solution.py:452
  565.5 45.4 %collective-permute-start.31 = (bf16[256,1024]{1,0:T(8,128)(2,1)}, bf16[256,1024]{1,0:T(8,128)(2,1)}, u32[]{:S(2)}, u32[]{:S(2)}) collective-permute-start(bf16[256,1024]{1,0:T(8,128)(2,1)} %bitcast.73), channel_id=1, source_target_pairs={{0,2},{2,0},{4,6},{6,4},{8,10},{10,8},{12,14},{14,12},{16,18},{18,... | collective-permute-start | bytes 1572872 | tf_op jit(solution)/shard_map/ppermute | solution.py:452
  568.2 42.8 %collective-permute-start.27 = (bf16[512,1024]{1,0:T(8,128)(2,1)}, bf16[512,1024]{1,0:T(8,128)(2,1)S(1)}, u32[]{:S(2)}, u32[]{:S(2)}) collective-permute-start(bf16[512,1024]{1,0:T(8,128)(2,1)} %bitcast.63), channel_id=1, source_target_pairs={{0,4},{2,6},{4,0},{6,2},{8,12},{10,14},{12,8},{14,10},{16,20},{18,... | collective-permute-start | bytes 3145736 | tf_op jit(solution)/shard_map/ppermute | solution.py:452
  608.5 41.9 %collective-permute-start.32 = (bf16[512,1024]{1,0:T(8,128)(2,1)}, bf16[512,1024]{1,0:T(8,128)(2,1)}, u32[]{:S(2)}, u32[]{:S(2)}) collective-permute-start(bf16[512,1024]{1,0:T(8,128)(2,1)} %bitcast.74), channel_id=1, source_target_pairs={{0,1},{1,0},{2,3},{3,2},{4,5},{5,4},{6,7},{7,6},{8,9},{9,8},{10,11... | collective-permute-start | bytes 3145736 | tf_op jit(solution)/shard_map/ppermute | solution.py:448
  609.8 43.0 %collective-permute-start.35 = (bf16[512,1024]{1,0:T(8,128)(2,1)}, bf16[512,1024]{1,0:T(8,128)(2,1)}, u32[]{:S(2)}, u32[]{:S(2)}) collective-permute-start(bf16[512,1024]{1,0:T(8,128)(2,1)} %bitcast.79), channel_id=1, source_target_pairs={{0,4},{2,6},{4,0},{6,2},{8,12},{10,14},{12,8},{14,10},{16,20},{18,... | collective-permute-start | bytes 3145736 | tf_op jit(solution)/shard_map/ppermute | solution.py:452
  613.6 52.3 %collective-permute-start.33 = (bf16[512,1024]{1,0:T(8,128)(2,1)}, bf16[512,1024]{1,0:T(8,128)(2,1)}, u32[]{:S(2)}, u32[]{:S(2)}) collective-permute-start(bf16[512,1024]{1,0:T(8,128)(2,1)} %fusion.55), channel_id=1, source_target_pairs={{0,4},{2,6},{4,0},{6,2},{8,12},{10,14},{12,8},{14,10},{16,20},{18,... | collective-permute-start | bytes 3145736 | tf_op jit(solution)/shard_map/ppermute | solution.py:452
  615.9 50.0 %collective-permute-start.34 = (bf16[512,1024]{1,0:T(8,128)(2,1)}, bf16[512,1024]{1,0:T(8,128)(2,1)}, u32[]{:S(2)}, u32[]{:S(2)}) collective-permute-start(bf16[512,1024]{1,0:T(8,128)(2,1)} %fusion.54), channel_id=1, source_target_pairs={{0,1},{1,0},{2,3},{3,2},{4,5},{5,4},{6,7},{7,6},{8,9},{9,8},{10,11... | collective-permute-start | bytes 3145736 | tf_op jit(solution)/shard_map/ppermute | solution.py:448
  618.0 47.8 %collective-permute-start.36 = (bf16[512,1536]{1,0:T(8,128)(2,1)S(1)}, bf16[512,1536]{1,0:T(8,128)(2,1)S(1)}, u32[]{:S(2)}, u32[]{:S(2)}) collective-permute-start(bf16[512,1536]{1,0:T(8,128)(2,1)S(1)} %bitcast.466), channel_id=1, source_target_pairs={{0,2},{2,0},{4,6},{6,4},{8,10},{10,8},{12,14},{14,12},{16,18},{18,... | collective-permute-start | bytes 4718600 | tf_op jit(solution)/shard_map/ppermute | solution.py:452
  672.9 181.4 %all-gather.23.cloned.1.call-start = ((), (), s32[]{:S(2)}) async-start(), calls=%async_computation.7 | async-start | bytes 8912896 | tf_op jit(solution)/shard_map/all_gather | solution.py:911
  (214 other events, 2995.3 us)
Sparse Core Ops, SparseCore 0:
  20.5 52.3 all-gather.12
  97.6 63.4 all-gather.14
  163.3 74.4 all-gather.16
  314.1 200.9 reduce-scatter.1
  517.1 93.3 all-gather.18
  673.0 72.0 all-gather.20
  749.4 98.4 all-gather.22

commit v7 on v6

--- a/solution.py
+++ b/solution.py
@@ -506,6 +506,7 @@
 NN = (((1,), (0,)), ((), ()))
 SPLIT_AXIS = {"up": 1, "down": 0}
 PACK_WIDTH = 512
+LIGHT = pl.CostEstimate(flops=0, bytes_accessed=2**16, transcendentals=0)
 
 
 def quarter_of(kind, half, place):
@@ -534,7 +535,7 @@
         in_specs=[pl.BlockSpec((1, 3, rows, width), lambda step: (layer, 0, step, 0))],
         out_specs=pl.BlockSpec((rows, 3 * width), lambda step: (step, 0)),
         out_shape=jax.ShapeDtypeStruct((height, 3 * width), bf16),
-        cost_estimate=pl.CostEstimate(flops=0, bytes_accessed=12 * height * width, transcendentals=0),
+        cost_estimate=LIGHT,
         name="flat_qkv",
     )(stacked)
 
@@ -573,7 +574,7 @@
             out_specs=pl.BlockSpec((total, PACK_WIDTH), lambda step, at: (0, 0)),
         ),
         out_shape=jax.ShapeDtypeStruct((total, PACK_WIDTH), bf16),
-        cost_estimate=pl.CostEstimate(flops=0, bytes_accessed=4 * total * PACK_WIDTH, transcendentals=0),
+        cost_estimate=LIGHT,
         name="pack_pieces",
     )(place.reshape(1).astype(jnp.int32), *arrays)
 
@@ -602,9 +603,7 @@
         ],
         out_shape=[jax.ShapeDtypeStruct(shape, bf16) for shape in shapes],
         compiler_params=pltpu.CompilerParams(vmem_limit_bytes=32 * 2**20),
-        cost_estimate=pl.CostEstimate(
-            flops=0, bytes_accessed=4 * dp_size * total * PACK_WIDTH, transcendentals=0
-        ),
+        cost_estimate=LIGHT,
         name="unpack_halves",
     )(gathered)
 
@@ -642,7 +641,7 @@
         ),
         out_shape=jax.ShapeDtypeStruct((2 * dp_size, 2 * rows, width), bf16),
         compiler_params=pltpu.CompilerParams(vmem_limit_bytes=32 * 2**20),
-        cost_estimate=pl.CostEstimate(flops=0, bytes_accessed=16 * height * width, transcendentals=0),
+        cost_estimate=LIGHT,
         name="stack_pair",
     )(side.reshape(1).astype(jnp.int32), down_parts[0], up_parts[0], down_parts[1], up_parts[1])
 
@@ -684,7 +683,7 @@
         ],
         input_output_aliases=aliases,
         compiler_params=pltpu.CompilerParams(vmem_limit_bytes=32 * 2**20),
-        cost_estimate=pl.CostEstimate(flops=0, bytes_accessed=6 * dp_size * total * PACK_WIDTH, transcendentals=0),
+        cost_estimate=LIGHT,
         name="place_joint",
     )(*operands)
 
@@ -713,7 +712,7 @@
             jax.ShapeDtypeStruct((2, dp_size * rows, columns), f32),
         ],
         compiler_params=pltpu.CompilerParams(vmem_limit_bytes=40 * 2**20),
-        cost_estimate=pl.CostEstimate(flops=0, bytes_accessed=12 * dp_size * rows * columns, transcendentals=0),
+        cost_estimate=LIGHT,
         name="place_pair",
     )(whole.reshape(dp_size, 2, rows, columns))
 
@@ -743,7 +742,7 @@
         out_shape=jax.ShapeDtypeStruct(base.shape, f32),
         input_output_aliases={1: 0},
         compiler_params=pltpu.CompilerParams(vmem_limit_bytes=32 * 2**20),
-        cost_estimate=pl.CostEstimate(flops=0, bytes_accessed=6 * dp_size * rows * columns, transcendentals=0),
+        cost_estimate=LIGHT,
         name="place_" + kind,
     )(whole.reshape(half, 2, 2, rows, columns), base)
 
@@ -766,6 +765,7 @@
             out_specs=pl.BlockSpec((1, 1, rows, width), lambda slot, step, side_ref: (slot, 0, step, 0)),
         ),
         out_shape=jax.ShapeDtypeStruct((2, 1, height, width), f32),
+        cost_estimate=LIGHT,
         name="place_frames",
     )(side.reshape(1).astype(jnp.int32), mine, other)
 
@@ -1018,7 +1018,7 @@
     other_rows = swap_tensor(rows_away)
     first_pack = swap_tensor(first_send)
     own_qkv = [flat_qkv(stacked, layer) for layer in range(2)]
-    first_pack, own_qkv = pin(first_pack, own_qkv)
+    (first_pack,) = pin(first_pack)
     first_whole = gathered(first_pack)
     attn_send, hidden_send = packed(1, attn_kinds), packed(1, hidden_kinds)
     piece_rows, piece_columns = model_width // 2, w_up.shape[2] // 2
@@ -1166,7 +1166,7 @@
         norm_sums[layer][part] = (grad_gain, grad_shift)
         return grad_rows + added
 
-    out1, qkv1 = chain("out", "x", None), chain("qkv", "y", None)
+    out1, qkv1 = chain("out", "y", None), chain("qkv", "x", None)
     down0, up0 = chain("down", "x", None, "core"), chain("up", "y", None, "core")
     out0, qkv0 = chain("out", "x", None), chain("qkv", "y", None)
 
@@ -1194,11 +1194,12 @@
     grad_normed = dot_sum(list(zip((mine, theirs), weights[1]["qkv"])), NT)
     grad_rows = norm_step(1, 0, grad_rows, grad_normed)
     low = grad_rows.astype(bf16)
+    low, grad_rows = move((low, grad_rows), out1, qkv1)
     parts = down_grads(0, low)
-    parts, low, grad_rows = move((parts, low, grad_rows), out1, qkv1)
+    parts, low, grad_rows = pin(parts, low, grad_rows)
     start_quarters(down0, "down", parts)
     hidden = hidden_grads(0, low)
-    hidden, grad_rows, out_there = move((hidden, grad_rows, out_there), hold=[down0])
+    hidden, grad_rows, out_there = move((hidden, grad_rows, out_there), qkv1, out1, hold=[down0])
     parts = up_grads(0, hidden)
     grad_normed = dot_sum(list(zip(hidden, weights[0]["up"])), NT)
     parts, grad_normed, grad_rows = move((parts, grad_normed, grad_rows), qkv1, out1, down0, pair1)
@@ -1214,13 +1215,13 @@
     part_theirs, mine, theirs, grad_rows = move(
         (part_theirs, mine, theirs, grad_rows), down0, up0, qkv1, out1, hold=[out0]
     )
+    joint1 = Gather(qkv1, out1, PACK_WIDTH, True)
     qkv0.start_other(part_theirs)
     mine = attention_grad(0, 0, mine)
     part_mine = dot_low(kept[0][0], mine, TN)
     part_mine, mine, theirs, grad_rows = move(
-        (part_mine, mine, theirs, grad_rows), down0, up0, out0, qkv0, qkv1, out1
-    )
-    joint1 = Gather(qkv1, out1, PACK_WIDTH, True)
+        (part_mine, mine, theirs, grad_rows), down0, up0, out0, qkv0
+    )
     qkv0.add_own(part_mine)
     grad_normed = dot_sum([(mine, weights[0]["qkv"][0]), (theirs, weights[0]["qkv"][1])], NT)
     grad_rows = norm_step(0, 0, grad_rows, grad_normed)

time: 899 us -> 897 us (level)
  waiting for transfers between devices: 177 us -> 154 us
  starting transfers between devices: 60.7 us -> 72.2 us
    ppermute x45, waiting for transfers between devices: 157 us -> 136 us  [swap_bit(): lax.ppermute(block, 'dp', [(place, place ^ 1 << bit) for place in range(d...]
    dot_general x18, matrix products: 85.6 us -> 96.4 us  [dot_sum(): term = lax.dot_general(left, right, dims, preferred_element_type=f32)]
    ppermute x45, starting transfers between devices: 38.1 us -> 48.3 us  [swap_bit(): lax.ppermute(block, 'dp', [(place, place ^ 1 << bit) for place in range(d...]
    unnamed x344 -> x346, local copies, waits for them, and re-layouts: 38.8 us -> 39.6 us
  transfers between devices with their start and end apart: 71 -> 71, of which waited for: 20 -> 22; matrix products, arithmetic and copies ran while one was open for 38% -> 39% of each run, Pallas kernels for 23% -> 23%
where the time goes in v7:
time: 897 us; the launch traced here: 888 us
  matrix products  256 us (29%)
  Pallas kernels  219 us (24%)
  waiting for transfers between devices  154 us (17%)
  other arithmetic  85.2 us (9%)
  local copies, waits for them, and re-layouts  83.7 us (9%)
  starting transfers between devices  72.2 us (8%)
  between operations  17.4 us (2%)
    ppermute x45, waiting for transfers between devices, swap_bit(): lax.ppermute(block, 'dp', [(place, place ^ 1 << bit) for place in range(d...  136 us
    pallas_call x4, Pallas kernels, attn_bwd(): pl.pallas_call(partial(bwd_kernel, causal, bq), grid=(pairs,), in_specs=[...  102 us
    dot_general x18, matrix products, dot_sum(): term = lax.dot_general(left, right, dims, preferred_element_type=f32)  96.4 us
    dot_general x26, matrix products, dot_low(): lax.dot_general(left, right, dims, preferred_element_type=f32).astype(bf16)  88.1 us
    pallas_call x4, Pallas kernels, attn_fwd(): pl.pallas_call(partial(fwd_kernel, causal, bq), grid=(pairs,), in_specs=[...  65.8 us
    ppermute x45, starting transfers between devices, swap_bit(): lax.ppermute(block, 'dp', [(place, place ^ 1 << bit) for place in range(d...  48.3 us
    unnamed x346, local copies, waits for them, and re-layouts  39.6 us
    convert_element_type x30, other arithmetic, add_rounded(): return (left.astype(f32) + right.astype(f32)).astype(bf16)  30 us
  transfers between devices with their start and end apart: 71, of which 22 were waited for; matrix products, arithmetic and copies ran while one was open for 39% of the time, Pallas kernels for 23%

profile of v7, /device:TPU:0, one launch (start us, length us, event | category | flops | bytes accessed | tf_op | source)
XLA Modules:
  0.0 888.0 jit_solution(6246974270685207774)
XLA Ops:
  52.5 14.0 %attn_fwd_causal.2 = (bf16[1024,512]{1,0:T(8,128)(2,1)S(1)}, f32[4,2,1024]{2,1,0:T(2,128)S(1)}) custom-call(s32[2]{0:T(128)S(1)} %pad_add_fusion.lims_ref, bf16[1024,1536]{1,0:T(8,128)(2,1)S(1)} %convolution_convert_fusion.7.q_ref.k_ref.v_ref, bf16[1024,1536]{1,0:T(8,128)(2,1)S(1)} %convolution_convert_fusion.7.q_ref.k_ref.v_ref, ...), custom_call_target="tpu_custom_call" | custom-call | flops 4194304 | bytes 4194304 | tf_op jit(solution)/shard_map/attn_fwd_causal/pallas_call | solution.py:381
  81.7 14.3 %attn_fwd_causal.3 = (bf16[1024,512]{1,0:T(8,128)(2,1)S(1)}, f32[4,2,1024]{2,1,0:T(2,128)S(1)}) custom-call(s32[2]{0:T(128)S(1)} %pad_add_fusion.lims_ref, bf16[1024,1536]{1,0:T(8,128)(2,1)S(1)} %convolution_convert_fusion.6.q_ref.k_ref.v_ref, bf16[1024,1536]{1,0:T(8,128)(2,1)S(1)} %convolution_convert_fusion.6.q_ref.k_ref.v_ref, ...), custom_call_target="tpu_custom_call" | custom-call | flops 4194304 | bytes 4194304 | tf_op jit(solution)/shard_map/attn_fwd_causal/pallas_call | solution.py:381
  108.1 9.6 %add_convert_fusion.2 = (bf16[1024,2048]{1,0:T(8,128)(2,1)}, bf16[1024,2048]{1,0:T(8,128)(2,1)}) fusion(bf16[1024,1024]{1,0:T(8,128)(2,1)S(1)} %add_convert_fusion.11, bf16[2,1024,2048]{2,1,0:T(8,128)(2,1)S(1)} %bitcast.427), kind=kOutput, calls=%fused_computation.11 | convolution fusion | flops 4326424576 | bytes 14680064 | tf_op jit(solution)/shard_map/dot_general | solution.py:1058
  119.4 19.1 %fusion.29 = f32[1024,1024]{1,0:T(8,128)S(1)} fusion(bf16[1024,2048]{1,0:T(8,128)(2,1)} %get-tuple-element.232, bf16[2,2048,1024]{2,1,0:T(8,128)(2,1)} %refs_1_.5), kind=kOutput, calls=%fused_computation.42 | convolution fusion | flops 4294967296 | bytes 12582912 | tf_op jit(solution)/shard_map/dot_general | solution.py:497
  173.8 18.7 %attn_fwd_full.2 = (bf16[1024,512]{1,0:T(8,128)(2,1)S(1)}, f32[4,2,1024]{2,1,0:T(2,128)S(1)}) custom-call(s32[2]{0:T(128)S(1)} %pad_add_fusion.lims_ref, bf16[1024,1536]{1,0:T(8,128)(2,1)S(1)} %convolution_convert_fusion.5.q_ref.k_ref.v_ref, bf16[1024,1536]{1,0:T(8,128)(2,1)S(1)} %convolution_convert_fusion.5.q_ref.k_ref.v_ref, ...), custom_call_target="tpu_custom_call" | custom-call | flops 4194304 | bytes 4194304 | tf_op jit(solution)/shard_map/attn_fwd_full/pallas_call | solution.py:381
  203.5 18.7 %attn_fwd_full.3 = (bf16[1024,512]{1,0:T(8,128)(2,1)S(1)}, f32[4,2,1024]{2,1,0:T(2,128)S(1)}) custom-call(s32[2]{0:T(128)S(1)} %pad_add_fusion.lims_ref, bf16[1024,1536]{1,0:T(8,128)(2,1)S(1)} %convolution_convert_fusion.4.q_ref.k_ref.v_ref, bf16[1024,1536]{1,0:T(8,128)(2,1)S(1)} %convolution_convert_fusion.4.q_ref.k_ref.v_ref, ...), custom_call_target="tpu_custom_call" | custom-call | flops 4194304 | bytes 4194304 | tf_op jit(solution)/shard_map/attn_fwd_full/pallas_call | solution.py:381
  227.8 12.6 %add_convert_fusion.1 = (bf16[1024,2048]{1,0:T(8,128)(2,1)}, bf16[1024,2048]{1,0:T(8,128)(2,1)S(1)}) fusion(bf16[1024,1024]{1,0:T(8,128)(2,1)S(1)} %add_convert_fusion.7, bf16[2,1024,2048]{2,1,0:T(8,128)(2,1)} %refs_0_.1), kind=kOutput, calls=%fused_computation.7 | convolution fusion | flops 4326424576 | bytes 14680064 | tf_op jit(solution)/shard_map/dot_general | solution.py:1087
  252.5 8.9 %add_convert_fusion = (bf16[1024,2048]{1,0:T(8,128)(2,1)}, bf16[1024,2048]{1,0:T(8,128)(2,1)S(1)}) fusion(bf16[1024,1024]{1,0:T(8,128)(2,1)S(1)} %add_convert_fusion.7, bf16[1024,2048]{1,0:T(8,128)(2,1)S(1)} %get-tuple-element.257), kind=kOutput, calls=%fused_computation.3 | convolution fusion | flops 4326424576 | bytes 14680064 | tf_op jit(solution)/shard_map/dot_general | solution.py:1092
  281.2 8.1 multiply_convert_fusion.1
  289.3 7.8 multiply_convert_fusion.2
  317.7 10.8 %fusion.132 = f32[1024,1024]{1,0:T(8,128)} fusion(bf16[1024,2048]{1,0:T(8,128)(2,1)} %multiply_convert_fusion.1, bf16[1024,2048]{1,0:T(8,128)(2,1)} %copy-done.22), kind=kOutput, calls=%fused_computation.363 | convolution fusion | flops 4294967296 | bytes 12582912 | tf_op jit(solution)/shard_map/dot_general | solution.py:497
  328.5 11.3 %multiply_reduce_fusion = (f32[1024]{0:T(1024)S(1)}, f32[1024]{0:T(1024)S(1)}, f32[1024]{0:T(1024)S(1)}, f32[1024]{0:T(1024)S(1)}, f32[1024,1024]{1,0:T(8,128)}) fusion(f32[1024,1024]{1,0:T(8,128)S(1)} %copy-done.36, f32[1024]{0:T(1024)S(1)} %broadcast_multiply_fusion.12, f32[1024]{0:T(1024)S(1)} %add_rsqrt_fusion, f32[1024]{0:T(1024)S(1)} %get-tuple-element.442, ...), kind=kOutput, calls=%fused_computation.48 | convolution fusion | flops 4305448960 | bytes 21000192 | tf_op jit(solution)/shard_map/dot_general | solution.py:497
  346.1 28.8 %attn_bwd_full.2 = bf16[1024,1536]{1,0:T(8,128)(2,1)S(1)} custom-call(s32[2]{0:T(128)S(1)} %pad_add_fusion.lims_ref, bf16[1024,1536]{1,0:T(8,128)(2,1)} %copy-done.3, bf16[1024,1536]{1,0:T(8,128)(2,1)} %copy-done.3, bf16[1024,1536]{1,0:T(8,128)(2,1)} %copy-done.3, f32[4,2,1024]{2,1,0:T(2,128)S(1)} %get-tuple-element.277.l_ref, ...), custom_call_target="tpu_custom_call" | custom-call | flops 4194304 | bytes 4194304 | tf_op jit(solution)/shard_map/attn_bwd_full/pallas_call | solution.py:431
  379.7 28.9 %attn_bwd_full.3 = bf16[1024,1536]{1,0:T(8,128)(2,1)S(1)} custom-call(s32[2]{0:T(128)S(1)} %pad_add_fusion.lims_ref, bf16[1024,1536]{1,0:T(8,128)(2,1)} %copy-done.2, bf16[1024,1536]{1,0:T(8,128)(2,1)} %copy-done.2, bf16[1024,1536]{1,0:T(8,128)(2,1)} %copy-done.2, f32[4,2,1024]{2,1,0:T(2,128)S(1)} %get-tuple-element.246.l_ref, ...), custom_call_target="tpu_custom_call" | custom-call | flops 4194304 | bytes 4194304 | tf_op jit(solution)/shard_map/attn_bwd_full/pallas_call | solution.py:431
  479.8 12.1 %collective-permute-start.21 = (bf16[256,1536]{1,0:T(8,128)(2,1)S(1)}, bf16[256,1536]{1,0:T(8,128)(2,1)}, u32[]{:S(2)}, u32[]{:S(2)}) collective-permute-start(bf16[256,1536]{1,0:T(8,128)(2,1)S(1)} %fusion.68), channel_id=1, source_target_pairs={{0,4},{2,6},{4,0},{6,2},{8,12},{10,14},{12,8},{14,10},{16,20},{18,... | collective-permute-start | bytes 2359304 | tf_op jit(solution)/shard_map/ppermute | solution.py:452
  518.3 7.7 collective-permute-done.21
  578.9 22.3 %attn_bwd_causal.2 = bf16[1024,1536]{1,0:T(8,128)(2,1)S(1)} custom-call(s32[2]{0:T(128)S(1)} %copy-done.21, bf16[1024,1536]{1,0:T(8,128)(2,1)} %copy-done.1, bf16[1024,1536]{1,0:T(8,128)(2,1)} %copy-done.1, bf16[1024,1536]{1,0:T(8,128)(2,1)} %copy-done.1, f32[4,2,1024]{2,1,0:T(2,128)S(1)} %get-tuple-element.225.l_ref, ...), custom_call_target="tpu_custom_call" | custom-call | flops 4194304 | bytes 4194304 | tf_op jit(solution)/shard_map/attn_bwd_causal/pallas_call | solution.py:431
  629.6 22.1 %attn_bwd_causal.3 = bf16[1024,1536]{1,0:T(8,128)(2,1)S(1)} custom-call(s32[2]{0:T(128)S(1)} %copy-done.21, bf16[1024,1536]{1,0:T(8,128)(2,1)} %copy-done, bf16[1024,1536]{1,0:T(8,128)(2,1)} %copy-done, bf16[1024,1536]{1,0:T(8,128)(2,1)} %copy-done, f32[4,2,1024]{2,1,0:T(2,128)S(1)} %get-tuple-element.216.l_ref, ...), custom_call_target="tpu_custom_call" | custom-call | flops 4194304 | bytes 4194304 | tf_op jit(solution)/shard_map/attn_bwd_causal/pallas_call | solution.py:431
  724.7 9.0 %collective-permute-done.48 = bf16[128,1024]{1,0:T(8,128)(2,1)S(1)} collective-permute-done((bf16[128,1024]{1,0:T(8,128)(2,1)S(1)}, bf16[128,1024]{1,0:T(8,128)(2,1)S(1)}, u32[]{:S(2)}, u32[]{:S(2)}) %collective-permute-start.48) | collective-permute-done | bytes 262176 | tf_op jit(solution)/shard_map/ppermute | solution.py:452
  760.6 16.9 %collective-permute-done.54 = bf16[64,1024]{1,0:T(8,128)(2,1)S(1)} collective-permute-done((bf16[64,1024]{1,0:T(8,128)(2,1)S(1)}, bf16[64,1024]{1,0:T(8,128)(2,1)S(1)}, u32[]{:S(2)}, u32[]{:S(2)}) %collective-permute-start.54) | collective-permute-done | bytes 131104 | tf_op jit(solution)/shard_map/ppermute | solution.py:452
  780.9 24.2 %collective-permute-done.57 = bf16[32,1024]{1,0:T(8,128)(2,1)S(1)} collective-permute-done((bf16[32,1024]{1,0:T(8,128)(2,1)S(1)}, bf16[32,1024]{1,0:T(8,128)(2,1)S(1)}, u32[]{:S(2)}, u32[]{:S(2)}) %collective-permute-start.57) | collective-permute-done | bytes 65568 | tf_op jit(solution)/shard_map/ppermute | solution.py:452
  819.2 15.9 %collective-permute-done.60 = f32[32,1024]{1,0:T(8,128)S(1)} collective-permute-done((f32[32,1024]{1,0:T(8,128)S(1)}, f32[32,1024]{1,0:T(8,128)S(1)}, u32[]{:S(2)}, u32[]{:S(2)}) %collective-permute-start.60) | collective-permute-done | bytes 131104 | tf_op jit(solution)/shard_map/ppermute | solution.py:452
  835.4 12.3 %collective-permute-done.61 = bf16[2,256,512]{2,1,0:T(8,128)(2,1)S(1)} collective-permute-done((bf16[2,256,512]{2,1,0:T(8,128)(2,1)S(1)}, bf16[2,256,512]{2,1,0:T(8,128)(2,1)S(1)}, u32[]{:S(2)}, u32[]{:S(2)}) %collective-permute-start.61) | collective-permute-done | bytes 524320 | tf_op jit(solution)/shard_map/ppermute | solution.py:452
  859.1 11.0 %collective-permute-done.62 = bf16[4,256,512]{2,1,0:T(8,128)(2,1)S(1)} collective-permute-done((bf16[4,256,512]{2,1,0:T(8,128)(2,1)S(1)}, bf16[4,256,512]{2,1,0:T(8,128)(2,1)S(1)}, u32[]{:S(2)}, u32[]{:S(2)}) %collective-permute-start.62) | collective-permute-done | bytes 1048608 | tf_op jit(solution)/shard_map/ppermute | solution.py:452
  (701 shorter events, 505.4 us)
Async XLA Ops:
  7.2 65.4 %all-gather.13.cloned.1.call-start = ((), (), s32[]{:S(2)}) async-start(), calls=%async_computation.2 | async-start | bytes 4456448 | tf_op jit(solution)/shard_map/all_gather | solution.py:1011
  20.4 173.8 %all-gather.15.cloned.1.call-start = ((), (), s32[]{:S(2)}) async-start(), calls=%async_computation.3 | async-start | bytes 4456448 | tf_op jit(solution)/shard_map/all_gather | solution.py:1011
  97.0 151.3 %all-gather.17.cloned.1.call-start = ((), (), s32[]{:S(2)}) async-start(), calls=%async_computation.4 | async-start | bytes 8912896 | tf_op jit(solution)/shard_map/all_gather | solution.py:1011
  117.8 408.2 %reduce-scatter.2.cloned.1.call-start = ((), (), s32[]{:S(2)}) async-start(), calls=%async_computation.1 | async-start | bytes 17301504 | tf_op jit(solution)/shard_map/reduce_scatter | solution.py:890
  161.8 105.7 %collective-permute-start.10 = (bf16[512,1024]{1,0:T(8,128)(2,1)}, bf16[512,1024]{1,0:T(8,128)(2,1)}, u32[]{:S(2)}, u32[]{:S(2)}) collective-permute-start(bf16[512,1024]{1,0:T(8,128)(2,1)} %dynamic-slice_bitcast_fusion), channel_id=1, source_target_pairs={{0,1},{1,0},{2,3},{3,2},{4,5},{5,4},{6,7},{7,6},{8,9},{9,8},{10,11... | collective-permute-start | bytes 3145736 | tf_op jit(solution)/shard_map/ppermute | solution.py:448
  313.6 396.4 %all-gather.19.cloned.1.call-start = ((), (), s32[]{:S(2)}) async-start(), calls=%async_computation.5 | async-start | bytes 8912896 | tf_op jit(solution)/shard_map/all_gather | solution.py:895
  316.8 158.4 %collective-permute-start.15 = (bf16[512,1024]{1,0:T(8,128)(2,1)}, bf16[512,1024]{1,0:T(8,128)(2,1)}, u32[]{:S(2)}, u32[]{:S(2)}) collective-permute-start(bf16[512,1024]{1,0:T(8,128)(2,1)} %dynamic-slice_convert_fusion.1), channel_id=1, source_target_pairs={{0,1},{1,0},{2,3},{3,2},{4,5},{5,4},{6,7},{7,6},{8,9},{9,8},{10,11... | collective-permute-start | bytes 3145736 | tf_op jit(solution)/shard_map/ppermute | solution.py:448
  378.9 37.3 %collective-permute-start.11 = (bf16[256,1024]{1,0:T(8,128)(2,1)S(1)}, bf16[256,1024]{1,0:T(8,128)(2,1)S(1)}, u32[]{:S(2)}, u32[]{:S(2)}) collective-permute-start(bf16[256,1024]{1,0:T(8,128)(2,1)S(1)} %bitcast.474), channel_id=1, source_target_pairs={{0,2},{2,0},{4,6},{6,4},{8,10},{10,8},{12,14},{14,12},{16,18},{18,... | collective-permute-start | bytes 1572872 | tf_op jit(solution)/shard_map/ppermute | solution.py:452
  417.2 56.2 %collective-permute-start.17 = (bf16[128,1024]{1,0:T(8,128)(2,1)}, bf16[128,1024]{1,0:T(8,128)(2,1)}, u32[]{:S(2)}, u32[]{:S(2)}) collective-permute-start(bf16[128,1024]{1,0:T(8,128)(2,1)} %bitcast.48), channel_id=1, source_target_pairs={{0,4},{2,6},{4,0},{6,2},{8,12},{10,14},{12,8},{14,10},{16,20},{18,... | collective-permute-start | bytes 786440 | tf_op jit(solution)/shard_map/ppermute | solution.py:452
  473.4 44.2 %collective-permute-start.23 = (bf16[128,1024]{1,0:T(8,128)(2,1)S(1)}, bf16[128,1024]{1,0:T(8,128)(2,1)S(1)}, u32[]{:S(2)}, u32[]{:S(2)}) collective-permute-start(bf16[128,1024]{1,0:T(8,128)(2,1)S(1)} %bitcast.480), channel_id=1, source_target_pairs={{0,4},{2,6},{4,0},{6,2},{8,12},{10,14},{12,8},{14,10},{16,20},{18,... | collective-permute-start | bytes 786440 | tf_op jit(solution)/shard_map/ppermute | solution.py:452
  475.2 42.5 %collective-permute-start.20 = (bf16[256,1536]{1,0:T(8,128)(2,1)S(1)}, bf16[256,1536]{1,0:T(8,128)(2,1)}, u32[]{:S(2)}, u32[]{:S(2)}) collective-permute-start(bf16[256,1536]{1,0:T(8,128)(2,1)S(1)} %bitcast.468), channel_id=1, source_target_pairs={{0,1},{1,0},{2,3},{3,2},{4,5},{5,4},{6,7},{7,6},{8,9},{9,8},{10,11... | collective-permute-start | bytes 2359304 | tf_op jit(solution)/shard_map/ppermute | solution.py:448
  477.0 40.6 %collective-permute-start.22 = (bf16[128,1024]{1,0:T(8,128)(2,1)S(1)}, bf16[128,1024]{1,0:T(8,128)(2,1)S(1)}, u32[]{:S(2)}, u32[]{:S(2)}) collective-permute-start(bf16[128,1024]{1,0:T(8,128)(2,1)S(1)} %fusion.93), channel_id=1, source_target_pairs={{0,1},{1,0},{2,3},{3,2},{4,5},{5,4},{6,7},{7,6},{8,9},{9,8},{10,11... | collective-permute-start | bytes 786440 | tf_op jit(solution)/shard_map/ppermute | solution.py:448
  479.8 46.2 %collective-permute-start.21 = (bf16[256,1536]{1,0:T(8,128)(2,1)S(1)}, bf16[256,1536]{1,0:T(8,128)(2,1)}, u32[]{:S(2)}, u32[]{:S(2)}) collective-permute-start(bf16[256,1536]{1,0:T(8,128)(2,1)S(1)} %fusion.68), channel_id=1, source_target_pairs={{0,4},{2,6},{4,0},{6,2},{8,12},{10,14},{12,8},{14,10},{16,20},{18,... | collective-permute-start | bytes 2359304 | tf_op jit(solution)/shard_map/ppermute | solution.py:452
  526.1 254.9 %all-gather.21.cloned.1.call-start = ((), (), s32[]{:S(2)}) async-start(), calls=%async_computation.6 | async-start | bytes 4456448 | tf_op jit(solution)/shard_map/all_gather | solution.py:911
  534.3 72.1 %collective-permute-start.28 = (bf16[512,1024]{1,0:T(8,128)(2,1)}, bf16[512,1024]{1,0:T(8,128)(2,1)}, u32[]{:S(2)}, u32[]{:S(2)}) collective-permute-start(bf16[512,1024]{1,0:T(8,128)(2,1)} %bitcast.67), channel_id=1, source_target_pairs={{0,1},{1,0},{2,3},{3,2},{4,5},{5,4},{6,7},{7,6},{8,9},{9,8},{10,11... | collective-permute-start | bytes 3145736 | tf_op jit(solution)/shard_map/ppermute | solution.py:448
  569.8 46.3 %collective-permute-start.30 = (bf16[64,1536]{1,0:T(8,128)(2,1)S(1)}, bf16[64,1536]{1,0:T(8,128)(2,1)}, u32[]{:S(2)}, u32[]{:S(2)}) collective-permute-start(bf16[64,1536]{1,0:T(8,128)(2,1)S(1)} %dynamic-slice_bitcast_fusion.7), channel_id=1, source_target_pairs={{0,16},{2,18},{4,20},{6,22},{8,24},{10,26},{12,28},{14,30},{16,0},... | collective-permute-start | bytes 589832 | tf_op jit(solution)/shard_map/ppermute | solution.py:452
  573.1 43.0 %collective-permute-start.32 = (bf16[256,1024]{1,0:T(8,128)(2,1)}, bf16[256,1024]{1,0:T(8,128)(2,1)}, u32[]{:S(2)}, u32[]{:S(2)}) collective-permute-start(bf16[256,1024]{1,0:T(8,128)(2,1)} %bitcast.77), channel_id=1, source_target_pairs={{0,2},{2,0},{4,6},{6,4},{8,10},{10,8},{12,14},{14,12},{16,18},{18,... | collective-permute-start | bytes 1572872 | tf_op jit(solution)/shard_map/ppermute | solution.py:452
  574.2 41.9 %collective-permute-start.33 = (bf16[256,1024]{1,0:T(8,128)(2,1)}, bf16[256,1024]{1,0:T(8,128)(2,1)}, u32[]{:S(2)}, u32[]{:S(2)}) collective-permute-start(bf16[256,1024]{1,0:T(8,128)(2,1)} %bitcast.79), channel_id=1, source_target_pairs={{0,2},{2,0},{4,6},{6,4},{8,10},{10,8},{12,14},{14,12},{16,18},{18,... | collective-permute-start | bytes 1572872 | tf_op jit(solution)/shard_map/ppermute | solution.py:452
  576.9 43.5 %collective-permute-start.29 = (bf16[512,1024]{1,0:T(8,128)(2,1)}, bf16[512,1024]{1,0:T(8,128)(2,1)}, u32[]{:S(2)}, u32[]{:S(2)}) collective-permute-start(bf16[512,1024]{1,0:T(8,128)(2,1)} %bitcast.69), channel_id=1, source_target_pairs={{0,4},{2,6},{4,0},{6,2},{8,12},{10,14},{12,8},{14,10},{16,20},{18,... | collective-permute-start | bytes 3145736 | tf_op jit(solution)/shard_map/ppermute | solution.py:452
  614.6 49.9 %collective-permute-start.34 = (bf16[512,1024]{1,0:T(8,128)(2,1)}, bf16[512,1024]{1,0:T(8,128)(2,1)}, u32[]{:S(2)}, u32[]{:S(2)}) collective-permute-start(bf16[512,1024]{1,0:T(8,128)(2,1)} %bitcast.80), channel_id=1, source_target_pairs={{0,1},{1,0},{2,3},{3,2},{4,5},{5,4},{6,7},{7,6},{8,9},{9,8},{10,11... | collective-permute-start | bytes 3145736 | tf_op jit(solution)/shard_map/ppermute | solution.py:448
  616.1 48.7 %collective-permute-start.37 = (bf16[512,1024]{1,0:T(8,128)(2,1)}, bf16[512,1024]{1,0:T(8,128)(2,1)}, u32[]{:S(2)}, u32[]{:S(2)}) collective-permute-start(bf16[512,1024]{1,0:T(8,128)(2,1)} %bitcast.85), channel_id=1, source_target_pairs={{0,4},{2,6},{4,0},{6,2},{8,12},{10,14},{12,8},{14,10},{16,20},{18,... | collective-permute-start | bytes 3145736 | tf_op jit(solution)/shard_map/ppermute | solution.py:452
  623.0 42.1 %collective-permute-start.35 = (bf16[512,1024]{1,0:T(8,128)(2,1)}, bf16[512,1024]{1,0:T(8,128)(2,1)}, u32[]{:S(2)}, u32[]{:S(2)}) collective-permute-start(bf16[512,1024]{1,0:T(8,128)(2,1)} %fusion.56), channel_id=1, source_target_pairs={{0,4},{2,6},{4,0},{6,2},{8,12},{10,14},{12,8},{14,10},{16,20},{18,... | collective-permute-start | bytes 3145736 | tf_op jit(solution)/shard_map/ppermute | solution.py:452
  626.0 39.1 %collective-permute-start.36 = (bf16[512,1024]{1,0:T(8,128)(2,1)}, bf16[512,1024]{1,0:T(8,128)(2,1)}, u32[]{:S(2)}, u32[]{:S(2)}) collective-permute-start(bf16[512,1024]{1,0:T(8,128)(2,1)} %fusion.55), channel_id=1, source_target_pairs={{0,1},{1,0},{2,3},{3,2},{4,5},{5,4},{6,7},{7,6},{8,9},{9,8},{10,11... | collective-permute-start | bytes 3145736 | tf_op jit(solution)/shard_map/ppermute | solution.py:448
  655.3 192.4 %all-gather.23.cloned.1.call-start = ((), (), s32[]{:S(2)}) async-start(), calls=%async_computation.7 | async-start | bytes 8912896 | tf_op jit(solution)/shard_map/all_gather | solution.py:911
  (215 other events, 2965.6 us)
Sparse Core Ops, SparseCore 0:
  20.5 52.0 all-gather.12
  97.2 63.8 all-gather.14
  163.2 74.6 all-gather.16
  313.7 210.9 reduce-scatter.1
  526.7 106.7 all-gather.18
  655.4 63.6 all-gather.20
  744.5 96.6 all-gather.22
